TPU v7x, 32 devices: a whole 2x2x4 slice. The times are simulated.
32 devices in a mesh: wide: 8 (over y, x, core), narrow: 4 (over z).
Axes of the slice: x: 2, y: 2, z: 4, core: 2. Of those that a mesh axis runs over, the one named last changes fastest.
Arguments:
- cache: bfloat16 [8, 8192, 128], P('wide', 'narrow'), may hold values from -6 to 6
- lookup_slots: int32 [8, 4096, 16], P('wide'), may hold values from 0 to 8191
- bag_lengths: int32 [8, 4096], P('wide'), may hold values from 1 to 16
- miss_rows: bfloat16 [8, 4096, 128], P('wide', 'narrow'), may hold values from -6 to 6
- miss_slots: int32 [8, 4096], P('wide', 'narrow'), may hold values from 0 to 8191, as said below
- holder_counts: int32 [8, 16], P('wide', 'narrow'), may hold values from 0 to 512, as said below
- w_first: bfloat16 [1024, 4096], P(None, 'narrow'), may hold values from -0.1875 to 0.1875
- b_first: float32 [4096], P('narrow'), may hold values from -4 to 4
- w_second: bfloat16 [4096, 4096], P('narrow'), may hold values from -0.09375 to 0.09375
- b_second: float32 [4096], P('narrow'), may hold values from -4 to 4
- w_out: bfloat16 [4096], P('narrow'), may hold values from -0.09375 to 0.09375
Outputs:
- top_hidden: bfloat16 [4096, 4096], P('wide', 'narrow')
- logits: float32 [4096], P('wide')
- cache_next: bfloat16 [8, 8192, 128], P('wide', 'narrow')
Inputs may be any that keep to these rules, and one draw needn't show every extreme that they name: `holder_counts`: entry h * 4 + o is the number of row blocks that holder h sections for owner o, the device holding slots o * 2048 to (o + 1) * 2048 - 1; a holder's counts sum to at most 1024, and this is reached by some holder of every table; the largest count, 512, is reached in every table. `miss_slots`: A holder's live entries are packed by owner, owner 0 first, as its counts say; each live entry names a slot of its owner, no slot twice in a table; entries past a holder's live ones are 0 and unused.
All inputs are finite; a program needn't handle non-finite values.
Results may differ from a plain program's by a relative error of at most 0.0076.
Values may be sent and summed in bfloat16 or wider, within the bound.
No kernel may reach another device: no remote copies, remote signals or barrier semaphores. Data moves between devices by JAX's collectives and lax.ppermute only.
A program may use at most 128 MiB of HBM per device.

v0:
```python
import jax
import jax.numpy as jnp
from jax import lax
from jax.experimental import pallas as pl
from jax.experimental.pallas import tpu as pltpu
from jax.sharding import PartitionSpec as P


SEND_CAP = 512
LOW_BITS = 8
LOW = 1 << LOW_BITS
GROUP = 16


def from_ahead(value, distance, count):
    pairs = [(source, (source - distance) % count) for source in range(count)]
    return lax.ppermute(value, "narrow", pairs)


def from_flipped(value, bit, count):
    return lax.ppermute(value, "wide", [(index, index ^ bit) for index in range(count)])


def pool_quarter(lookups, lengths, cache_table, distance):
    owners, quarters, blocks, width = lookups.shape
    slot_count, emb = cache_table.shape
    highs = slot_count // LOW
    rows_per = blocks * GROUP
    total = owners * rows_per

    def kernel(lookups_ref, lengths_ref, table_ref, out_ref, counts_ref):
        here = lax.axis_index("narrow")
        which = lax.rem(here + quarters - distance, quarters)
        base = here * slot_count
        bag_size = width // GROUP
        key_rows = lax.broadcasted_iota(jnp.int32, (highs * GROUP, width), 0).astype(jnp.bfloat16)
        low_rows = lax.broadcasted_iota(jnp.int32, (LOW, width), 0).astype(jnp.bfloat16)
        lane = lax.broadcasted_iota(jnp.int32, (blocks, width), 1)
        bag_lane = lane // bag_size
        place_lane = lane - bag_lane * bag_size
        bag_rows = lax.broadcasted_iota(jnp.int32, (rows_per, width), 0) & (GROUP - 1)
        bag_lanes = lax.broadcasted_iota(jnp.int32, (rows_per, width), 1) // bag_size
        widen = jnp.where(bag_rows == bag_lanes, 1.0, 0.0).astype(jnp.bfloat16)
        row_block = lax.broadcasted_iota(jnp.int32, (blocks, rows_per), 1) // GROUP
        own_block = row_block == lax.broadcasted_iota(jnp.int32, (blocks, rows_per), 0)
        one = jnp.ones((), jnp.bfloat16)
        zero = jnp.zeros((), jnp.bfloat16)

        def owner_step(owner, carry):
            slots = lookups_ref[owner, which] - base
            bag_lengths = lengths_ref[pl.ds(owner * quarters + which, 1), :].astype(jnp.float32)
            bag_lengths = jnp.where(own_block, bag_lengths, 0.0).astype(jnp.bfloat16)
            used = jnp.dot(bag_lengths, widen, preferred_element_type=jnp.float32)
            used = used.astype(jnp.int32)
            usable = (place_lane < used) & (slots >= 0) & (slots < slot_count)
            keys = jnp.where(usable, (slots >> LOW_BITS) * GROUP + bag_lane, -1)
            lows = slots & (LOW - 1)
            keys = keys.astype(jnp.float32).astype(jnp.bfloat16)
            lows = lows.astype(jnp.float32).astype(jnp.bfloat16)
            for block in range(blocks):
                hot_key = jnp.where(key_rows == keys[block : block + 1, :], one, zero)
                hot_low = jnp.where(low_rows == lows[block : block + 1, :], one, zero)
                counts = lax.dot_general(
                    hot_key.astype(jnp.float8_e4m3fn),
                    hot_low.astype(jnp.float8_e4m3fn),
                    (((1,), (1,)), ((), ())),
                    preferred_element_type=jnp.float32,
                )
                start = pl.multiple_of(owner * rows_per + block * GROUP, GROUP)
                counts_ref[:, pl.ds(start, GROUP), :] = counts.astype(jnp.bfloat16).reshape(
                    highs, GROUP, LOW
                )
            return carry

        lax.fori_loop(0, owners, owner_step, 0, unroll=2)
        tile = min(total, 512)

        def tile_step(index, carry):
            start = pl.multiple_of(index * tile, tile)
            acc = jnp.zeros((tile, emb), jnp.float32)
            for high in range(highs):
                acc = acc + jnp.dot(
                    counts_ref[high, pl.ds(start, tile), :],
                    table_ref[high * LOW : (high + 1) * LOW, :],
                    preferred_element_type=jnp.float32,
                )
            out_ref[pl.ds(start, tile), :] = acc.astype(jnp.bfloat16)
            return carry

        lax.fori_loop(0, total // tile, tile_step, 0)

    return pl.pallas_call(
        kernel,
        out_shape=jax.ShapeDtypeStruct((total, emb), jnp.bfloat16),
        scratch_shapes=[pltpu.VMEM((highs, total, LOW), jnp.bfloat16)],
        cost_estimate=pl.CostEstimate(
            flops=4 * total * slot_count * emb, bytes_accessed=2 * total * emb, transcendentals=0
        ),
        name="pool_quarter",
    )(lookups, lengths, cache_table)


def section_rows(counts, rows, slots, slot_count):
    count = counts.shape[0]
    held, emb = rows.shape
    spans = SEND_CAP // emb

    def kernel(counts_ref, rows_ref, slots_ref, *out_refs):
        here = lax.axis_index("narrow")
        row_ids = lax.broadcasted_iota(jnp.int32, (SEND_CAP, held), 0)
        places = lax.broadcasted_iota(jnp.int32, (SEND_CAP, held), 1)
        live_lanes = lax.broadcasted_iota(jnp.int32, (1, SEND_CAP), 1)
        for distance, out_ref in enumerate(out_refs):
            owner = lax.rem(here + count - distance, count)
            start = jnp.int32(0)
            for other in range(count):
                start = start + jnp.where(other < owner, counts_ref[other], 0)
            live = counts_ref[owner]
            source = jnp.where(row_ids < live, row_ids + start, -1)
            hot = jnp.where(source == places, 1.0, 0.0).astype(jnp.bfloat16)
            picked = jnp.dot(hot, rows_ref[...], preferred_element_type=jnp.float32)
            out_ref[:SEND_CAP, :] = picked.astype(jnp.bfloat16)
            local = slots_ref[...] - owner * slot_count
            digits = jnp.concatenate([local >> LOW_BITS, local & (LOW - 1)] * 4, axis=0)
            digits = digits.astype(jnp.float32).astype(jnp.bfloat16)
            moved = lax.dot_general(
                digits, hot, (((1,), (1,)), ((), ())), preferred_element_type=jnp.float32
            )
            high = jnp.where(live_lanes < live, moved[0:1, :], -1.0)
            low = moved[1:2, :]
            tail = [high[:, span * emb : (span + 1) * emb] for span in range(spans)]
            tail += [low[:, span * emb : (span + 1) * emb] for span in range(spans)]
            tail.append(jnp.zeros((GROUP - 2 * spans, emb), jnp.float32))
            out_ref[SEND_CAP:, :] = jnp.concatenate(tail, axis=0).astype(jnp.bfloat16)

    smem = pl.BlockSpec(memory_space=pltpu.SMEM)
    vmem = pl.BlockSpec(memory_space=pltpu.VMEM)
    return pl.pallas_call(
        kernel,
        out_shape=tuple(
            jax.ShapeDtypeStruct((SEND_CAP + GROUP, emb), jnp.bfloat16) for _ in range(count)
        ),
        in_specs=[smem, vmem, vmem],
        out_specs=tuple(vmem for _ in range(count)),
        cost_estimate=pl.CostEstimate(
            flops=2 * count * SEND_CAP * held * emb,
            bytes_accessed=4 * held * emb,
            transcendentals=0,
        ),
        name="section_rows",
    )(counts, rows, slots.reshape(1, held))


def place_rows(pieces, cache_table):
    slot_count, emb = cache_table.shape
    spans = SEND_CAP // emb
    arrived = SEND_CAP * len(pieces)

    def kernel(*refs):
        piece_refs = refs[: len(pieces)]
        cache_ref, out_ref, rows_ref = refs[len(pieces) :]
        high, low = [], []
        for index, piece in enumerate(piece_refs):
            rows_ref[index * SEND_CAP : (index + 1) * SEND_CAP, :emb] = piece[:SEND_CAP, :]
            digits = piece[SEND_CAP:, :].astype(jnp.float32)
            high += [digits[span : span + 1, :] for span in range(spans)]
            low += [digits[spans + span : spans + span + 1, :] for span in range(spans)]
        rows_ref[:, emb:] = jnp.ones((arrived, emb), jnp.bfloat16)
        high = jnp.concatenate(high, axis=1)
        low = jnp.concatenate(low, axis=1)
        low_rows = lax.broadcasted_iota(jnp.int32, (LOW, arrived), 0).astype(jnp.bfloat16)
        one = jnp.ones((), jnp.bfloat16)
        zero = jnp.zeros((), jnp.bfloat16)

        def step(index, carry):
            start = pl.multiple_of(index * LOW, LOW)
            targets = jnp.where(high == index.astype(jnp.float32), low, -1.0).astype(jnp.bfloat16)
            hot = jnp.where(low_rows == targets, one, zero)
            placed = jnp.dot(hot, rows_ref[...], preferred_element_type=jnp.float32)
            old = cache_ref[pl.ds(start, LOW), :]
            fresh = jnp.where(placed[:, emb:] > 0.5, placed[:, :emb], old.astype(jnp.float32))
            out_ref[pl.ds(start, LOW), :] = fresh.astype(jnp.bfloat16)
            return carry

        lax.fori_loop(0, slot_count // LOW, step, 0, unroll=2)

    return pl.pallas_call(
        kernel,
        out_shape=jax.ShapeDtypeStruct((slot_count, emb), jnp.bfloat16),
        scratch_shapes=[pltpu.VMEM((arrived, 2 * emb), jnp.bfloat16)],
        cost_estimate=pl.CostEstimate(
            flops=4 * arrived * slot_count * emb,
            bytes_accessed=4 * slot_count * emb,
            transcendentals=0,
        ),
        name="place_rows",
    )(*pieces, cache_table)


def top_network(features, first_own, second_own, parts, biases, b_second, w_out):
    count = len(features)
    quarter_rows, depth = features[0].shape
    rows = count * quarter_rows
    hidden = first_own.shape[1]
    columns = second_own.shape[1] // count
    flat_parts, layout = [], []
    for distance, pieces in parts.items():
        for mask, array, spans in pieces:
            layout.append((distance, mask, spans))
            flat_parts.append(array)
    tile = min(hidden, 512)

    def kernel(*refs):
        feature_refs = refs[:count]
        first_ref, second_ref = refs[count : count + 2]
        part_refs = refs[count + 2 : count + 2 + len(flat_parts)]
        rest = refs[count + 2 + len(flat_parts) :]
        bias_ref, b_second_ref, w_out_ref, top_ref, logit_ref = rest[:5]
        feats, firsts, seconds, hiddens, feat_sem, sems = rest[5:]
        wide_index = lax.axis_index("wide")
        narrow_index = lax.axis_index("narrow")
        for distance, ref in enumerate(feature_refs):
            spot = lax.rem(narrow_index + distance, count) * quarter_rows
            spot = pl.multiple_of(spot, quarter_rows)
            pltpu.make_async_copy(ref, feats.at[pl.ds(spot, quarter_rows), :], feat_sem).start()
        column = pl.multiple_of(narrow_index * columns, columns)

        def fetch(which, wanted):
            if wanted == 0:
                if which == 0:
                    source, target = first_ref, firsts.at[0]
                else:
                    source = second_ref.at[:, pl.ds(column, columns)]
                    target = seconds.at[:hidden, :]
                pltpu.make_async_copy(source, target, sems.at[which, 0]).start()
            for (distance, mask, spans), ref in zip(layout, part_refs):
                for layer, row, height in spans:
                    if layer != which or distance != wanted:
                        continue
                    spot = pl.multiple_of((wide_index ^ mask) * height, height)
                    target = firsts.at[distance] if which == 0 else seconds
                    spot = spot + which * distance * hidden
                    pltpu.make_async_copy(
                        ref.at[row : row + height, :],
                        target.at[pl.ds(spot, height), :],
                        sems.at[which, distance],
                    ).start()

        for distance in range(count):
            fetch(0, distance)
        pltpu.make_async_copy(feats, feats, feat_sem).wait()
        for distance in range(count):
            pltpu.make_async_copy(firsts.at[distance], firsts.at[distance], sems.at[0, distance]).wait()
            fetch(1, distance)
            for start in range(0, hidden, tile):
                terms = jnp.dot(
                    feats[...],
                    firsts[distance, :, start : start + tile],
                    preferred_element_type=jnp.float32,
                )
                bias = bias_ref[distance : distance + 1, start : start + tile]
                spot = distance * hidden + start
                hiddens[:, spot : spot + tile] = jnp.maximum(terms + bias, 0.0).astype(jnp.bfloat16)
        for distance in range(count):
            block = seconds.at[distance * hidden : (distance + 1) * hidden, :]
            pltpu.make_async_copy(block, block, sems.at[1, distance]).wait()
        for start in range(0, columns, tile):
            terms = jnp.dot(
                hiddens[...], seconds[:, start : start + tile], preferred_element_type=jnp.float32
            )
            terms = jnp.maximum(terms + b_second_ref[:, start : start + tile], 0.0)
            top_ref[:, start : start + tile] = terms.astype(jnp.bfloat16)
        logit_ref[...] = lax.dot_general(
            w_out_ref[...], top_ref[...], (((1,), (1,)), ((), ())), preferred_element_type=jnp.float32
        )[:1]

    anywhere = pl.BlockSpec(memory_space=pl.ANY)
    local = pl.BlockSpec(memory_space=pltpu.VMEM)
    return pl.pallas_call(
        kernel,
        out_shape=(
            jax.ShapeDtypeStruct((rows, columns), jnp.bfloat16),
            jax.ShapeDtypeStruct((1, rows), jnp.float32),
        ),
        in_specs=[anywhere] * (count + 2 + len(flat_parts)) + [local] * 3,
        out_specs=(local, local),
        scratch_shapes=[
            pltpu.VMEM((rows, depth), jnp.bfloat16),
            pltpu.VMEM((count, depth, hidden), jnp.bfloat16),
            pltpu.VMEM((count * hidden, columns), jnp.bfloat16),
            pltpu.VMEM((rows, count * hidden), jnp.bfloat16),
            pltpu.SemaphoreType.DMA,
            pltpu.SemaphoreType.DMA((2, count)),
        ],
        cost_estimate=pl.CostEstimate(
            flops=2 * rows * count * hidden * (depth + columns),
            bytes_accessed=2 * count * hidden * (depth + columns),
            transcendentals=0,
        ),
        name="top_network",
    )(
        *features,
        first_own,
        second_own,
        *flat_parts,
        jnp.stack(biases),
        b_second.reshape(1, columns),
        jnp.broadcast_to(w_out.reshape(1, columns), (8, columns)),
    )


def after(value, *earlier):
    return lax.optimization_barrier((value,) + earlier)[0]


def spread(piece, spans, bits, wide_count, gate=None):
    if gate is not None:
        piece = after(piece, gate)
    pieces = [(0, piece)]
    for bit in bits:
        pieces = pieces + [
            (mask ^ bit, from_flipped(array, bit, wide_count)) for mask, array in pieces
        ]
    pieces = pieces + [
        (mask ^ 1, from_flipped(array, 1, wide_count)) for mask, array in pieces
    ]
    return [(mask, array, spans) for mask, array in pieces]


def step(
    cache,
    lookup_slots,
    bag_lengths,
    miss_rows,
    miss_slots,
    holder_counts,
    w_first,
    b_first,
    w_second,
    b_second,
    w_out,
):
    wide_count = lax.axis_size("wide")
    count = lax.axis_size("narrow")
    wide_index = lax.axis_index("wide")
    narrow_index = lax.axis_index("narrow")
    cache_table = cache[0]
    slot_count, emb = cache_table.shape
    lookups = lookup_slots[0]
    lengths = bag_lengths[0]
    batch_rows, bag_size = lookups.shape
    owner_rows = batch_rows // wide_count
    quarter_rows = owner_rows // count
    columns = w_second.shape[1] // count

    bits = [1 << place for place in range(1, (wide_count - 1).bit_length())]
    first_height = w_first.shape[0] // wide_count
    second_height = w_second.shape[0] // wide_count
    first_slice = lax.dynamic_slice_in_dim(w_first, wide_index * first_height, first_height, 0)

    def slices_for(distance):
        taker = lax.rem(narrow_index + count - distance, count)
        second_slice = lax.dynamic_slice(
            w_second,
            (wide_index * second_height, taker * columns),
            (second_height, columns),
        )
        return first_slice, second_slice

    both_spans = ((0, 0, first_height), (1, first_height, second_height))

    def merged(distance, gate=None):
        message = jnp.concatenate(slices_for(distance), axis=0)
        if gate is not None:
            message = after(message, gate)
        return from_ahead(message, distance, count)

    last = count - 1
    arrived_slices = {distance: merged(distance) for distance in range(1, last)}

    lookups = lookups.reshape(wide_count, count, quarter_rows // GROUP, GROUP * bag_size)
    lengths = lengths.reshape(wide_count * count, quarter_rows)
    sent, pooled = [], []
    for distance in range(count - 1, -1, -1):
        own_part = pool_quarter(lookups, lengths, cache_table, distance)
        pooled.append(own_part)
        if distance:
            sent.append(from_ahead(own_part, distance, count))
    biases = [b_first]
    for distance in range(1, count):
        biases.append(from_ahead(after(b_first, own_part), distance, count))
    summed = own_part.astype(jnp.float32)
    for part in sent:
        summed = summed + part.astype(jnp.float32)
    summed = summed.astype(jnp.bfloat16).reshape(wide_count, quarter_rows, emb)
    arrived_slices[last] = [
        from_ahead(after(piece, summed), last, count) for piece in slices_for(last)
    ]
    arrived = lax.all_to_all(summed, "wide", split_axis=0, concat_axis=0, tiled=True)
    own_features = jnp.transpose(arrived, (1, 0, 2)).reshape(quarter_rows, wide_count * emb)
    features = [own_features] + [
        from_ahead(own_features, distance, count) for distance in range(1, count)
    ]

    sections = section_rows(
        holder_counts[0], after(miss_rows[0], own_features), miss_slots[0], slot_count
    )
    arrived_rows = [sections[0]] + [
        from_ahead(sections[distance], distance, count) for distance in range(1, count)
    ]

    parts = {}
    for distance in range(1, last):
        ordered = bits if distance % 2 else bits[::-1]
        parts[distance] = spread(
            arrived_slices[distance],
            both_spans,
            ordered,
            wide_count,
            pooled[min(2 * distance - 1, last)],
        )
    first_piece, second_piece = arrived_slices[last]
    parts[last] = spread(
        first_piece, ((0, 0, first_height),), bits, wide_count, own_features
    ) + spread(second_piece, ((1, 0, second_height),), bits[::-1], wide_count, own_features)
    top_hidden, logit_terms = top_network(
        features, w_first, w_second, parts, biases, b_second, w_out
    )
    shares = [logit_terms] + [
        from_ahead(logit_terms, distance, count) for distance in range(1, count)
    ]
    while len(shares) > 1:
        half = len(shares) // 2
        shares = [shares[place] + shares[place + half] for place in range(half)]
    logits = shares[0].reshape(owner_rows)

    cache_next = place_rows(arrived_rows, cache_table)[None]
    return (top_hidden, logits, cache_next)


def solution(mesh):
    return jax.shard_map(
        step,
        mesh=mesh,
        in_specs=(
            P("wide", "narrow", None),
            P("wide", None, None),
            P("wide", None),
            P("wide", "narrow", None),
            P("wide", "narrow"),
            P("wide", "narrow"),
            P(None, "narrow"),
            P("narrow"),
            P("narrow", None),
            P("narrow"),
            P("narrow"),
        ),
        out_specs=(P("wide", "narrow"), P("wide"), P("wide", "narrow", None)),
        check_vma=False,
    )
```

profile of v0, /device:TPU:0, one launch (start us, length us, event | category | flops | bytes accessed | tf_op | source)
XLA Modules:
  0.0 200.5 jit_solution(13924352045727426554)
XLA Ops:
  0.6 1.5 copy.18
  2.2 1.5 reshape_squeeze.6.lookups_ref
  3.7 5.8 %pool_quarter.5 = bf16[1024,128]{1,0:T(8,128)(2,1)} custom-call(s32[8,4,8,256]{3,2,1,0:T(8,128)} %reshape_squeeze.6.lookups_ref, s32[32,128]{1,0:T(8,128)} %bitcast.29, bf16[2048,128]{1,0:T(8,128)(2,1)} %bitcast.23), custom_call_target="tpu_custom_call" | custom-call | flops 1073741824 | bytes 262144 | tf_op jit(solution)/shard_map/pool_quarter/pallas_call | solution.py:92
  9.5 3.1 %collective-permute-start = (bf16[1024,128]{1,0:T(8,128)(2,1)}, bf16[1024,128]{1,0:T(8,128)(2,1)S(1)}, u32[]{:S(2)}, u32[]{:S(2)}) collective-permute-start(bf16[1024,128]{1,0:T(8,128)(2,1)} %pool_quarter.5), channel_id=1, source_target_pairs={{0,1},{1,2},{2,3},{3,0},{4,5},{5,6},{6,7},{7,4},{8,9},{9,10},{10,1... | collective-permute-start | bytes 786440 | tf_op jit(solution)/shard_map/ppermute | solution.py:17
  12.6 5.8 %pool_quarter.7 = bf16[1024,128]{1,0:T(8,128)(2,1)} custom-call(s32[8,4,8,256]{3,2,1,0:T(8,128)} %reshape_squeeze.6.lookups_ref, s32[32,128]{1,0:T(8,128)} %bitcast.30, bf16[2048,128]{1,0:T(8,128)(2,1)} %bitcast.24), custom_call_target="tpu_custom_call" | custom-call | flops 1073741824 | bytes 262144 | tf_op jit(solution)/shard_map/pool_quarter/pallas_call | solution.py:92
  18.3 2.0 %collective-permute-start.2 = (bf16[1024,128]{1,0:T(8,128)(2,1)}, bf16[1024,128]{1,0:T(8,128)(2,1)S(1)}, u32[]{:S(2)}, u32[]{:S(2)}) collective-permute-start(bf16[1024,128]{1,0:T(8,128)(2,1)} %pool_quarter.7), channel_id=1, source_target_pairs={{0,3},{1,0},{2,1},{3,2},{4,7},{5,4},{6,5},{7,6},{8,11},{9,8},{10,9... | collective-permute-start | bytes 786440 | tf_op jit(solution)/shard_map/ppermute | solution.py:17
  20.4 5.8 %pool_quarter.6 = bf16[1024,128]{1,0:T(8,128)(2,1)} custom-call(s32[8,4,8,256]{3,2,1,0:T(8,128)} %reshape_squeeze.6.lookups_ref, s32[32,128]{1,0:T(8,128)} %bitcast.31, bf16[2048,128]{1,0:T(8,128)(2,1)} %bitcast.25), custom_call_target="tpu_custom_call" | custom-call | flops 1073741824 | bytes 262144 | tf_op jit(solution)/shard_map/pool_quarter/pallas_call | solution.py:92
  26.1 1.0 collective-permute-start.1
  27.2 1.3 fusion
  28.5 2.0 collective-permute-start.14
  30.5 2.0 %collective-permute-start.6 = (bf16[256,1024]{1,0:T(8,128)(2,1)S(1)}, bf16[256,1024]{1,0:T(8,128)(2,1)S(1)}, u32[]{:S(2)}, u32[]{:S(2)}) collective-permute-start(bf16[256,1024]{1,0:T(8,128)(2,1)S(1)} %get-tuple-element.35), channel_id=1, source_target_pairs={{0,3},{1,0},{2,1},{3,2},{4,7},{5,4},{6,5},{7,6},{8,11},{9,8},{10,9... | collective-permute-start | bytes 1572872 | tf_op jit(solution)/shard_map/ppermute | solution.py:17
  32.5 5.8 %pool_quarter.4 = bf16[1024,128]{1,0:T(8,128)(2,1)} custom-call(s32[8,4,8,256]{3,2,1,0:T(8,128)} %reshape_squeeze.6.lookups_ref, s32[32,128]{1,0:T(8,128)} %bitcast.32, bf16[2048,128]{1,0:T(8,128)(2,1)} %bitcast.26), custom_call_target="tpu_custom_call" | custom-call | flops 1073741824 | bytes 262144 | tf_op jit(solution)/shard_map/pool_quarter/pallas_call | solution.py:92
  38.3 12.8 %collective-permute-done.1 = bf16[1024,128]{1,0:T(8,128)(2,1)S(1)} collective-permute-done((bf16[1024,128]{1,0:T(8,128)(2,1)}, bf16[1024,128]{1,0:T(8,128)(2,1)S(1)}, u32[]{:S(2)}, u32[]{:S(2)}) %collective-permute-start.1) | collective-permute-done | bytes 262176 | tf_op jit(solution)/shard_map/ppermute | solution.py:17
  51.1 1.8 add_convert_fusion
  52.9 11.0 %collective-permute-start.22 = (bf16[128,1024]{1,0:T(8,128)(2,1)S(1)}, bf16[128,1024]{1,0:T(8,128)(2,1)S(1)}, u32[]{:S(2)}, u32[]{:S(2)}) collective-permute-start(bf16[128,1024]{1,0:T(8,128)(2,1)S(1)} %get-tuple-element.19), channel_id=1, source_target_pairs={{0,1},{1,2},{2,3},{3,0},{4,5},{5,6},{6,7},{7,4},{8,9},{9,10},{10,1... | collective-permute-start | bytes 786440 | tf_op jit(solution)/shard_map/ppermute | solution.py:17
  63.9 3.7 %all-to-all-start = ((bf16[8,128,128]{2,1,0:T(8,128)(2,1)}), bf16[8,128,128]{2,1,0:T(8,128)(2,1)S(1)}, u32[]{:S(2)}, u32[]{:S(2)}) async-start(bf16[8,128,128]{2,1,0:T(8,128)(2,1)} %bitcast.2), calls=%async_computation | async-start | bytes 524288 | tf_op jit(solution)/shard_map/all_to_all | solution.py:399
  67.7 3.8 %collective-permute-start.40 = (f32[1024]{0:T(1024)S(1)}, f32[1024]{0:T(1024)S(1)}, u32[]{:S(2)}, u32[]{:S(2)}) collective-permute-start(f32[1024]{0:T(1024)S(1)} %copy-done.1), channel_id=1, source_target_pairs={{0,1},{1,2},{2,3},{3,0},{4,5},{5,6},{6,7},{7,4},{8,9},{9,10},{10,1... | collective-permute-start | bytes 12296 | tf_op jit(solution)/shard_map/ppermute | solution.py:17
  71.5 7.4 %collective-permute-done.40 = f32[1024]{0:T(1024)S(1)} collective-permute-done((f32[1024]{0:T(1024)S(1)}, f32[1024]{0:T(1024)S(1)}, u32[]{:S(2)}, u32[]{:S(2)}) %collective-permute-start.40) | collective-permute-done | bytes 4128 | tf_op jit(solution)/shard_map/ppermute | solution.py:17
  78.9 7.6 %collective-permute-start.39 = (f32[1024]{0:T(1024)S(1)}, f32[1024]{0:T(1024)S(1)}, u32[]{:S(2)}, u32[]{:S(2)}) collective-permute-start(f32[1024]{0:T(1024)S(1)} %copy-done.1), channel_id=1, source_target_pairs={{0,2},{1,3},{2,0},{3,1},{4,6},{5,7},{6,4},{7,5},{8,10},{9,11},{10,... | collective-permute-start | bytes 12296 | tf_op jit(solution)/shard_map/ppermute | solution.py:17
  86.5 0.9 collective-permute-start.38
  88.1 1.4 collective-permute-start.5
  90.1 2.3 %collective-permute-start.4 = (bf16[128,1024]{1,0:T(8,128)(2,1)S(1)}, bf16[128,1024]{1,0:T(8,128)(2,1)S(1)}, u32[]{:S(2)}, u32[]{:S(2)}) collective-permute-start(bf16[128,1024]{1,0:T(8,128)(2,1)S(1)} %copy_bitcast_fusion.refs_0_), channel_id=1, source_target_pairs={{0,2},{1,3},{2,0},{3,1},{4,6},{5,7},{6,4},{7,5},{8,10},{9,11},{10,... | collective-permute-start | bytes 786440 | tf_op jit(solution)/shard_map/ppermute | solution.py:17
  92.4 1.5 collective-permute-start.3
  94.0 1.6 collective-permute-start.24
  95.6 3.6 %collective-permute-done.5.refs_3_ = bf16[128,1024]{1,0:T(8,128)(2,1)S(1)} collective-permute-done((bf16[128,1024]{1,0:T(8,128)(2,1)S(1)}, bf16[128,1024]{1,0:T(8,128)(2,1)S(1)}, u32[]{:S(2)}, u32[]{:S(2)}) %collective-permute-start.5) | collective-permute-done | bytes 262176 | tf_op jit(solution)/shard_map/ppermute | solution.py:17
  99.2 1.5 collective-permute-start.23
  100.7 8.0 %collective-permute-done.4.refs_2_ = bf16[128,1024]{1,0:T(8,128)(2,1)S(1)} collective-permute-done((bf16[128,1024]{1,0:T(8,128)(2,1)S(1)}, bf16[128,1024]{1,0:T(8,128)(2,1)S(1)}, u32[]{:S(2)}, u32[]{:S(2)}) %collective-permute-start.4) | collective-permute-done | bytes 262176 | tf_op jit(solution)/shard_map/ppermute | solution.py:17
  108.7 1.6 collective-permute-start.32
  110.3 1.5 collective-permute-start.31
  112.4 5.2 %collective-permute-done.32.refs_32_ = bf16[128,1024]{1,0:T(8,128)(2,1)S(1)} collective-permute-done((bf16[128,1024]{1,0:T(8,128)(2,1)}, bf16[128,1024]{1,0:T(8,128)(2,1)S(1)}, u32[]{:S(2)}, u32[]{:S(2)}) %collective-permute-start.32) | collective-permute-done | bytes 262176 | tf_op jit(solution)/shard_map/ppermute | solution.py:21
  117.6 1.5 collective-permute-start.25
  119.7 1.5 collective-permute-start.33
  121.2 4.2 %collective-permute-done.25.refs_25_ = bf16[128,1024]{1,0:T(8,128)(2,1)S(1)} collective-permute-done((bf16[128,1024]{1,0:T(8,128)(2,1)S(1)}, bf16[128,1024]{1,0:T(8,128)(2,1)S(1)}, u32[]{:S(2)}, u32[]{:S(2)}) %collective-permute-start.25) | collective-permute-done | bytes 262176 | tf_op jit(solution)/shard_map/ppermute | solution.py:21
  125.4 1.5 collective-permute-start.8
  127.0 1.6 collective-permute-start.7
  129.8 10.5 %collective-permute-done.8.refs_8_ = bf16[256,1024]{1,0:T(8,128)(2,1)S(1)} collective-permute-done((bf16[256,1024]{1,0:T(8,128)(2,1)S(1)}, bf16[256,1024]{1,0:T(8,128)(2,1)S(1)}, u32[]{:S(2)}, u32[]{:S(2)}) %collective-permute-start.8) | collective-permute-done | bytes 524320 | tf_op jit(solution)/shard_map/ppermute | solution.py:21
  140.2 1.6 collective-permute-done.7.refs_7_
  142.3 9.2 %collective-permute-done.15.refs_15_ = bf16[256,1024]{1,0:T(8,128)(2,1)} collective-permute-done((bf16[256,1024]{1,0:T(8,128)(2,1)S(1)}, bf16[256,1024]{1,0:T(8,128)(2,1)}, u32[]{:S(2)}, u32[]{:S(2)}) %collective-permute-start.15) | collective-permute-done | bytes 524320 | tf_op jit(solution)/shard_map/ppermute | solution.py:21
  151.6 1.5 collective-permute-start.17
  153.6 1.0 collective-permute-done.29.refs_29_
  155.5 5.1 %collective-permute-done.9.refs_9_ = bf16[256,1024]{1,0:T(8,128)(2,1)} collective-permute-done((bf16[256,1024]{1,0:T(8,128)(2,1)S(1)}, bf16[256,1024]{1,0:T(8,128)(2,1)}, u32[]{:S(2)}, u32[]{:S(2)}) %collective-permute-start.9) | collective-permute-done | bytes 524320 | tf_op jit(solution)/shard_map/ppermute | solution.py:21
  160.6 1.3 collective-permute-done.17.refs_17_
  162.5 4.0 %section_rows.1 = (bf16[528,128]{1,0:T(8,128)(2,1)}, bf16[528,128]{1,0:T(8,128)(2,1)}, bf16[528,128]{1,0:T(8,128)(2,1)}, bf16[528,128]{1,0:T(8,128)(2,1)}) custom-call(s32[4]{0:T(128)} %bitcast.34, bf16[1024,128]{1,0:T(8,128)(2,1)} %bitcast.28, s32[1,1024]{1,0:T(1,128)} %slots_ref.1), custom_call_target="tpu_custom_call" | custom-call | flops 536870912 | bytes 524288 | tf_op jit(solution)/shard_map/section_rows/pallas_call | solution.py:138
  166.6 7.2 %collective-permute-start.44 = (bf16[528,128]{1,0:T(8,128)(2,1)}, bf16[528,128]{1,0:T(8,128)(2,1)}, u32[]{:S(2)}, u32[]{:S(2)}) collective-permute-start(bf16[528,128]{1,0:T(8,128)(2,1)} %get-tuple-element.28), channel_id=1, source_target_pairs={{0,3},{1,0},{2,1},{3,2},{4,7},{5,4},{6,5},{7,6},{8,11},{9,8},{10,9... | collective-permute-start | bytes 405512 | tf_op jit(solution)/shard_map/ppermute | solution.py:17
  175.2 15.3 %top_network.1 = (bf16[512,1024]{1,0:T(8,128)(2,1)}, f32[1,512]{1,0:T(1,128)}) custom-call(bf16[128,1024]{1,0:T(8,128)(2,1)} %copy-done, bf16[128,1024]{1,0:T(8,128)(2,1)} %copy-done.14, bf16[128,1024]{1,0:T(8,128)(2,1)} %copy-done.13, bf16[128,1024]{1,0:T(8,128)(2,1)} %copy-done.12, bf16[1024,1024]{1,0:T(8,128)(2,1)} %refs_4_.1, ...), custom_call_target="tpu_custom_call" | custom-call | flops 8589934592 | bytes 16777216 | tf_op jit(solution)/shard_map/top_network/pallas_call | solution.py:279
  190.5 2.8 %collective-permute-start.43 = (f32[1,512]{1,0:T(1,128)}, f32[1,512]{1,0:T(1,128)S(1)}, u32[]{:S(2)}, u32[]{:S(2)}) collective-permute-start(f32[1,512]{1,0:T(1,128)} %get-tuple-element.25), channel_id=1, source_target_pairs={{0,1},{1,2},{2,3},{3,0},{4,5},{5,6},{6,7},{7,4},{8,9},{9,10},{10,1... | collective-permute-start | bytes 6152 | tf_op jit(solution)/shard_map/ppermute | solution.py:17
  193.2 1.1 collective-permute-start.42
  194.8 5.1 %place_rows.1 = bf16[2048,128]{1,0:T(8,128)(2,1)} custom-call(bf16[528,128]{1,0:T(8,128)(2,1)} %get-tuple-element.27.refs_0_, bf16[528,128]{1,0:T(8,128)(2,1)} %collective-permute-done.44.refs_1_, bf16[528,128]{1,0:T(8,128)(2,1)} %collective-permute-done.45.refs_2_, bf16[528,128]{1,0:T(8,128)(2,1)} %collective-permute-done.46.refs_3_, bf16[2048,128]{1,0:T(8,128)(2,1)} %bitcast.27), custom_call_target="tpu_custom_call" | custom-call | flops 2147483648 | bytes 1048576 | tf_op jit(solution)/shard_map/place_rows/pallas_call | solution.py:187
  (120 shorter events, 8.7 us)
Async XLA Ops:
  9.5 28.8 %collective-permute-start = (bf16[1024,128]{1,0:T(8,128)(2,1)}, bf16[1024,128]{1,0:T(8,128)(2,1)S(1)}, u32[]{:S(2)}, u32[]{:S(2)}) collective-permute-start(bf16[1024,128]{1,0:T(8,128)(2,1)} %pool_quarter.5), channel_id=1, source_target_pairs={{0,1},{1,2},{2,3},{3,0},{4,5},{5,6},{6,7},{7,4},{8,9},{9,10},{10,1... | collective-permute-start | bytes 786440 | tf_op jit(solution)/shard_map/ppermute | solution.py:17
  18.3 20.0 %collective-permute-start.2 = (bf16[1024,128]{1,0:T(8,128)(2,1)}, bf16[1024,128]{1,0:T(8,128)(2,1)S(1)}, u32[]{:S(2)}, u32[]{:S(2)}) collective-permute-start(bf16[1024,128]{1,0:T(8,128)(2,1)} %pool_quarter.7), channel_id=1, source_target_pairs={{0,3},{1,0},{2,1},{3,2},{4,7},{5,4},{6,5},{7,6},{8,11},{9,8},{10,9... | collective-permute-start | bytes 786440 | tf_op jit(solution)/shard_map/ppermute | solution.py:17
  26.1 25.0 %collective-permute-start.1 = (bf16[1024,128]{1,0:T(8,128)(2,1)}, bf16[1024,128]{1,0:T(8,128)(2,1)S(1)}, u32[]{:S(2)}, u32[]{:S(2)}) collective-permute-start(bf16[1024,128]{1,0:T(8,128)(2,1)} %pool_quarter.6), channel_id=1, source_target_pairs={{0,2},{1,3},{2,0},{3,1},{4,6},{5,7},{6,4},{7,5},{8,10},{9,11},{10,... | collective-permute-start | bytes 786440 | tf_op jit(solution)/shard_map/ppermute | solution.py:17
  28.5 63.9 %collective-permute-start.14 = (bf16[256,1024]{1,0:T(8,128)(2,1)S(1)}, bf16[256,1024]{1,0:T(8,128)(2,1)S(1)}, u32[]{:S(2)}, u32[]{:S(2)}) collective-permute-start(bf16[256,1024]{1,0:T(8,128)(2,1)S(1)} %get-tuple-element.34), channel_id=1, source_target_pairs={{0,2},{1,3},{2,0},{3,1},{4,6},{5,7},{6,4},{7,5},{8,10},{9,11},{10,... | collective-permute-start | bytes 1572872 | tf_op jit(solution)/shard_map/ppermute | solution.py:17
  30.5 63.5 %collective-permute-start.6 = (bf16[256,1024]{1,0:T(8,128)(2,1)S(1)}, bf16[256,1024]{1,0:T(8,128)(2,1)S(1)}, u32[]{:S(2)}, u32[]{:S(2)}) collective-permute-start(bf16[256,1024]{1,0:T(8,128)(2,1)S(1)} %get-tuple-element.35), channel_id=1, source_target_pairs={{0,3},{1,0},{2,1},{3,2},{4,7},{5,4},{6,5},{7,6},{8,11},{9,8},{10,9... | collective-permute-start | bytes 1572872 | tf_op jit(solution)/shard_map/ppermute | solution.py:17
  52.9 33.6 %collective-permute-start.22 = (bf16[128,1024]{1,0:T(8,128)(2,1)S(1)}, bf16[128,1024]{1,0:T(8,128)(2,1)S(1)}, u32[]{:S(2)}, u32[]{:S(2)}) collective-permute-start(bf16[128,1024]{1,0:T(8,128)(2,1)S(1)} %get-tuple-element.19), channel_id=1, source_target_pairs={{0,1},{1,2},{2,3},{3,0},{4,5},{5,6},{6,7},{7,4},{8,9},{9,10},{10,1... | collective-permute-start | bytes 786440 | tf_op jit(solution)/shard_map/ppermute | solution.py:17
  63.9 23.5 %all-to-all-start = ((bf16[8,128,128]{2,1,0:T(8,128)(2,1)}), bf16[8,128,128]{2,1,0:T(8,128)(2,1)S(1)}, u32[]{:S(2)}, u32[]{:S(2)}) async-start(bf16[8,128,128]{2,1,0:T(8,128)(2,1)} %bitcast.2), calls=%async_computation | async-start | bytes 524288 | tf_op jit(solution)/shard_map/all_to_all | solution.py:399
  67.7 26.3 %collective-permute-start.30 = (bf16[128,1024]{1,0:T(8,128)(2,1)S(1)}, bf16[128,1024]{1,0:T(8,128)(2,1)}, u32[]{:S(2)}, u32[]{:S(2)}) collective-permute-start(bf16[128,1024]{1,0:T(8,128)(2,1)S(1)} %get-tuple-element.21), channel_id=1, source_target_pairs={{0,1},{1,2},{2,3},{3,0},{4,5},{5,6},{6,7},{7,4},{8,9},{9,10},{10,1... | collective-permute-start | bytes 786440 | tf_op jit(solution)/shard_map/ppermute | solution.py:17
  67.7 11.2 %collective-permute-start.40 = (f32[1024]{0:T(1024)S(1)}, f32[1024]{0:T(1024)S(1)}, u32[]{:S(2)}, u32[]{:S(2)}) collective-permute-start(f32[1024]{0:T(1024)S(1)} %copy-done.1), channel_id=1, source_target_pairs={{0,1},{1,2},{2,3},{3,0},{4,5},{5,6},{6,7},{7,4},{8,9},{9,10},{10,1... | collective-permute-start | bytes 12296 | tf_op jit(solution)/shard_map/ppermute | solution.py:17
  78.9 9.2 %collective-permute-start.39 = (f32[1024]{0:T(1024)S(1)}, f32[1024]{0:T(1024)S(1)}, u32[]{:S(2)}, u32[]{:S(2)}) collective-permute-start(f32[1024]{0:T(1024)S(1)} %copy-done.1), channel_id=1, source_target_pairs={{0,2},{1,3},{2,0},{3,1},{4,6},{5,7},{6,4},{7,5},{8,10},{9,11},{10,... | collective-permute-start | bytes 12296 | tf_op jit(solution)/shard_map/ppermute | solution.py:17
  86.5 3.6 %collective-permute-start.38 = (f32[1024]{0:T(1024)S(1)}, f32[1024]{0:T(1024)S(1)}, u32[]{:S(2)}, u32[]{:S(2)}) collective-permute-start(f32[1024]{0:T(1024)S(1)} %copy-done.1), channel_id=1, source_target_pairs={{0,3},{1,0},{2,1},{3,2},{4,7},{5,4},{6,5},{7,6},{8,11},{9,8},{10,9... | collective-permute-start | bytes 12296 | tf_op jit(solution)/shard_map/ppermute | solution.py:17
  88.1 11.1 %collective-permute-start.5 = (bf16[128,1024]{1,0:T(8,128)(2,1)S(1)}, bf16[128,1024]{1,0:T(8,128)(2,1)S(1)}, u32[]{:S(2)}, u32[]{:S(2)}) collective-permute-start(bf16[128,1024]{1,0:T(8,128)(2,1)S(1)} %copy_bitcast_fusion.refs_0_), channel_id=1, source_target_pairs={{0,1},{1,2},{2,3},{3,0},{4,5},{5,6},{6,7},{7,4},{8,9},{9,10},{10,1... | collective-permute-start | bytes 786440 | tf_op jit(solution)/shard_map/ppermute | solution.py:17
  90.1 18.6 %collective-permute-start.4 = (bf16[128,1024]{1,0:T(8,128)(2,1)S(1)}, bf16[128,1024]{1,0:T(8,128)(2,1)S(1)}, u32[]{:S(2)}, u32[]{:S(2)}) collective-permute-start(bf16[128,1024]{1,0:T(8,128)(2,1)S(1)} %copy_bitcast_fusion.refs_0_), channel_id=1, source_target_pairs={{0,2},{1,3},{2,0},{3,1},{4,6},{5,7},{6,4},{7,5},{8,10},{9,11},{10,... | collective-permute-start | bytes 786440 | tf_op jit(solution)/shard_map/ppermute | solution.py:17
  92.4 16.3 %collective-permute-start.3 = (bf16[128,1024]{1,0:T(8,128)(2,1)S(1)}, bf16[128,1024]{1,0:T(8,128)(2,1)S(1)}, u32[]{:S(2)}, u32[]{:S(2)}) collective-permute-start(bf16[128,1024]{1,0:T(8,128)(2,1)S(1)} %copy_bitcast_fusion.refs_0_), channel_id=1, source_target_pairs={{0,3},{1,0},{2,1},{3,2},{4,7},{5,4},{6,5},{7,6},{8,11},{9,8},{10,9... | collective-permute-start | bytes 786440 | tf_op jit(solution)/shard_map/ppermute | solution.py:17
  94.0 16.3 %collective-permute-start.26 = (bf16[128,1024]{1,0:T(8,128)(2,1)}, bf16[128,1024]{1,0:T(8,128)(2,1)S(1)}, u32[]{:S(2)}, u32[]{:S(2)}) collective-permute-start(bf16[128,1024]{1,0:T(8,128)(2,1)} %copy-done.11), channel_id=1, source_target_pairs={{0,4},{4,0},{8,12},{12,8},{16,20},{20,16},{24,28},{28,24},{1,5},{5... | collective-permute-start | bytes 786440 | tf_op jit(solution)/shard_map/ppermute | solution.py:21
  94.0 17.8 %collective-permute-start.24 = (bf16[128,1024]{1,0:T(8,128)(2,1)}, bf16[128,1024]{1,0:T(8,128)(2,1)S(1)}, u32[]{:S(2)}, u32[]{:S(2)}) collective-permute-start(bf16[128,1024]{1,0:T(8,128)(2,1)} %copy-done.11), channel_id=1, source_target_pairs={{0,16},{4,20},{8,24},{12,28},{16,0},{20,4},{24,8},{28,12},{1,17},{... | collective-permute-start | bytes 786440 | tf_op jit(solution)/shard_map/ppermute | solution.py:21
  99.2 12.6 %collective-permute-start.23 = (bf16[128,1024]{1,0:T(8,128)(2,1)}, bf16[128,1024]{1,0:T(8,128)(2,1)S(1)}, u32[]{:S(2)}, u32[]{:S(2)}) collective-permute-start(bf16[128,1024]{1,0:T(8,128)(2,1)} %copy-done.11), channel_id=1, source_target_pairs={{0,8},{4,12},{8,0},{12,4},{16,24},{20,28},{24,16},{28,20},{1,9},{5... | collective-permute-start | bytes 786440 | tf_op jit(solution)/shard_map/ppermute | solution.py:21
  108.7 3.6 %collective-permute-start.34 = (bf16[128,1024]{1,0:T(8,128)(2,1)}, bf16[128,1024]{1,0:T(8,128)(2,1)}, u32[]{:S(2)}, u32[]{:S(2)}) collective-permute-start(bf16[128,1024]{1,0:T(8,128)(2,1)} %collective-permute-done.30.refs_30_), channel_id=1, source_target_pairs={{0,4},{4,0},{8,12},{12,8},{16,20},{20,16},{24,28},{28,24},{1,5},{5... | collective-permute-start | bytes 786440 | tf_op jit(solution)/shard_map/ppermute | solution.py:21
  108.7 8.9 %collective-permute-start.32 = (bf16[128,1024]{1,0:T(8,128)(2,1)}, bf16[128,1024]{1,0:T(8,128)(2,1)S(1)}, u32[]{:S(2)}, u32[]{:S(2)}) collective-permute-start(bf16[128,1024]{1,0:T(8,128)(2,1)} %collective-permute-done.30.refs_30_), channel_id=1, source_target_pairs={{0,8},{4,12},{8,0},{12,4},{16,24},{20,28},{24,16},{28,20},{1,9},{5... | collective-permute-start | bytes 786440 | tf_op jit(solution)/shard_map/ppermute | solution.py:21
  110.3 8.9 %collective-permute-start.31 = (bf16[128,1024]{1,0:T(8,128)(2,1)}, bf16[128,1024]{1,0:T(8,128)(2,1)S(1)}, u32[]{:S(2)}, u32[]{:S(2)}) collective-permute-start(bf16[128,1024]{1,0:T(8,128)(2,1)} %collective-permute-done.30.refs_30_), channel_id=1, source_target_pairs={{0,16},{4,20},{8,24},{12,28},{16,0},{20,4},{24,8},{28,12},{1,17},{... | collective-permute-start | bytes 786440 | tf_op jit(solution)/shard_map/ppermute | solution.py:21
  111.8 7.4 %collective-permute-start.28 = (bf16[128,1024]{1,0:T(8,128)(2,1)S(1)}, bf16[128,1024]{1,0:T(8,128)(2,1)S(1)}, u32[]{:S(2)}, u32[]{:S(2)}) collective-permute-start(bf16[128,1024]{1,0:T(8,128)(2,1)S(1)} %collective-permute-done.24.refs_24_), channel_id=1, source_target_pairs={{0,4},{4,0},{8,12},{12,8},{16,20},{20,16},{24,28},{28,24},{1,5},{5... | collective-permute-start | bytes 786440 | tf_op jit(solution)/shard_map/ppermute | solution.py:21
  111.8 7.9 %collective-permute-start.27 = (bf16[128,1024]{1,0:T(8,128)(2,1)S(1)}, bf16[128,1024]{1,0:T(8,128)(2,1)S(1)}, u32[]{:S(2)}, u32[]{:S(2)}) collective-permute-start(bf16[128,1024]{1,0:T(8,128)(2,1)S(1)} %collective-permute-done.23.refs_23_), channel_id=1, source_target_pairs={{0,4},{4,0},{8,12},{12,8},{16,20},{20,16},{24,28},{28,24},{1,5},{5... | collective-permute-start | bytes 786440 | tf_op jit(solution)/shard_map/ppermute | solution.py:21
  112.3 16.8 %collective-permute-start.10 = (bf16[256,1024]{1,0:T(8,128)(2,1)S(1)}, bf16[256,1024]{1,0:T(8,128)(2,1)S(1)}, u32[]{:S(2)}, u32[]{:S(2)}) collective-permute-start(bf16[256,1024]{1,0:T(8,128)(2,1)S(1)} %collective-permute-done.6.refs_6_), channel_id=1, source_target_pairs={{0,4},{4,0},{8,12},{12,8},{16,20},{20,16},{24,28},{28,24},{1,5},{5... | collective-permute-start | bytes 1572872 | tf_op jit(solution)/shard_map/ppermute | solution.py:21
  117.6 7.8 %collective-permute-start.25 = (bf16[128,1024]{1,0:T(8,128)(2,1)S(1)}, bf16[128,1024]{1,0:T(8,128)(2,1)S(1)}, u32[]{:S(2)}, u32[]{:S(2)}) collective-permute-start(bf16[128,1024]{1,0:T(8,128)(2,1)S(1)} %collective-permute-done.23.refs_23_), channel_id=1, source_target_pairs={{0,16},{4,20},{8,24},{12,28},{16,0},{20,4},{24,8},{28,12},{1,17},{... | collective-permute-start | bytes 786440 | tf_op jit(solution)/shard_map/ppermute | solution.py:21
  119.2 7.8 %collective-permute-start.36 = (bf16[128,1024]{1,0:T(8,128)(2,1)S(1)}, bf16[128,1024]{1,0:T(8,128)(2,1)S(1)}, u32[]{:S(2)}, u32[]{:S(2)}) collective-permute-start(bf16[128,1024]{1,0:T(8,128)(2,1)S(1)} %collective-permute-done.32.refs_32_), channel_id=1, source_target_pairs={{0,4},{4,0},{8,12},{12,8},{16,20},{20,16},{24,28},{28,24},{1,5},{5... | collective-permute-start | bytes 786440 | tf_op jit(solution)/shard_map/ppermute | solution.py:21
  119.2 9.3 %collective-permute-start.35 = (bf16[128,1024]{1,0:T(8,128)(2,1)S(1)}, bf16[128,1024]{1,0:T(8,128)(2,1)S(1)}, u32[]{:S(2)}, u32[]{:S(2)}) collective-permute-start(bf16[128,1024]{1,0:T(8,128)(2,1)S(1)} %collective-permute-done.31.refs_31_), channel_id=1, source_target_pairs={{0,4},{4,0},{8,12},{12,8},{16,20},{20,16},{24,28},{28,24},{1,5},{5... | collective-permute-start | bytes 786440 | tf_op jit(solution)/shard_map/ppermute | solution.py:21
  119.7 9.4 %collective-permute-start.33 = (bf16[128,1024]{1,0:T(8,128)(2,1)S(1)}, bf16[128,1024]{1,0:T(8,128)(2,1)S(1)}, u32[]{:S(2)}, u32[]{:S(2)}) collective-permute-start(bf16[128,1024]{1,0:T(8,128)(2,1)S(1)} %collective-permute-done.31.refs_31_), channel_id=1, source_target_pairs={{0,8},{4,12},{8,0},{12,4},{16,24},{20,28},{24,16},{28,20},{1,9},{5... | collective-permute-start | bytes 786440 | tf_op jit(solution)/shard_map/ppermute | solution.py:21
  125.4 14.8 %collective-permute-start.8 = (bf16[256,1024]{1,0:T(8,128)(2,1)S(1)}, bf16[256,1024]{1,0:T(8,128)(2,1)S(1)}, u32[]{:S(2)}, u32[]{:S(2)}) collective-permute-start(bf16[256,1024]{1,0:T(8,128)(2,1)S(1)} %collective-permute-done.6.refs_6_), channel_id=1, source_target_pairs={{0,16},{4,20},{8,24},{12,28},{16,0},{20,4},{24,8},{28,12},{1,17},{... | collective-permute-start | bytes 1572872 | tf_op jit(solution)/shard_map/ppermute | solution.py:21
  127.0 14.9 %collective-permute-start.7 = (bf16[256,1024]{1,0:T(8,128)(2,1)S(1)}, bf16[256,1024]{1,0:T(8,128)(2,1)S(1)}, u32[]{:S(2)}, u32[]{:S(2)}) collective-permute-start(bf16[256,1024]{1,0:T(8,128)(2,1)S(1)} %collective-permute-done.6.refs_6_), channel_id=1, source_target_pairs={{0,8},{4,12},{8,0},{12,4},{16,24},{20,28},{24,16},{28,20},{1,9},{5... | collective-permute-start | bytes 1572872 | tf_op jit(solution)/shard_map/ppermute | solution.py:21
  128.5 23.0 %collective-permute-start.15 = (bf16[256,1024]{1,0:T(8,128)(2,1)S(1)}, bf16[256,1024]{1,0:T(8,128)(2,1)}, u32[]{:S(2)}, u32[]{:S(2)}) collective-permute-start(bf16[256,1024]{1,0:T(8,128)(2,1)S(1)} %collective-permute-done.14.refs_14_), channel_id=1, source_target_pairs={{0,16},{4,20},{8,24},{12,28},{16,0},{20,4},{24,8},{28,12},{1,17},{... | collective-permute-start | bytes 1572872 | tf_op jit(solution)/shard_map/ppermute | solution.py:21
  129.1 24.0 %collective-permute-start.18 = (bf16[256,1024]{1,0:T(8,128)(2,1)S(1)}, bf16[256,1024]{1,0:T(8,128)(2,1)S(1)}, u32[]{:S(2)}, u32[]{:S(2)}) collective-permute-start(bf16[256,1024]{1,0:T(8,128)(2,1)S(1)} %collective-permute-done.14.refs_14_), channel_id=1, source_target_pairs={{0,4},{4,0},{8,12},{12,8},{16,20},{20,16},{24,28},{28,24},{1,5},{5... | collective-permute-start | bytes 1572872 | tf_op jit(solution)/shard_map/ppermute | solution.py:21
  129.2 23.9 %collective-permute-start.16 = (bf16[256,1024]{1,0:T(8,128)(2,1)S(1)}, bf16[256,1024]{1,0:T(8,128)(2,1)}, u32[]{:S(2)}, u32[]{:S(2)}) collective-permute-start(bf16[256,1024]{1,0:T(8,128)(2,1)S(1)} %collective-permute-done.14.refs_14_), channel_id=1, source_target_pairs={{0,8},{4,12},{8,0},{12,4},{16,24},{20,28},{24,16},{28,20},{1,9},{5... | collective-permute-start | bytes 1572872 | tf_op jit(solution)/shard_map/ppermute | solution.py:21
  140.2 14.9 %collective-permute-start.12 = (bf16[256,1024]{1,0:T(8,128)(2,1)S(1)}, bf16[256,1024]{1,0:T(8,128)(2,1)S(1)}, u32[]{:S(2)}, u32[]{:S(2)}) collective-permute-start(bf16[256,1024]{1,0:T(8,128)(2,1)S(1)} %collective-permute-done.8.refs_8_), channel_id=1, source_target_pairs={{0,4},{4,0},{8,12},{12,8},{16,20},{20,16},{24,28},{28,24},{1,5},{5... | collective-permute-start | bytes 1572872 | tf_op jit(solution)/shard_map/ppermute | solution.py:21
  141.8 18.7 %collective-permute-start.9 = (bf16[256,1024]{1,0:T(8,128)(2,1)S(1)}, bf16[256,1024]{1,0:T(8,128)(2,1)}, u32[]{:S(2)}, u32[]{:S(2)}) collective-permute-start(bf16[256,1024]{1,0:T(8,128)(2,1)S(1)} %collective-permute-done.7.refs_7_), channel_id=1, source_target_pairs={{0,16},{4,20},{8,24},{12,28},{16,0},{20,4},{24,8},{28,12},{1,17},{... | collective-permute-start | bytes 1572872 | tf_op jit(solution)/shard_map/ppermute | solution.py:21
  151.6 10.3 %collective-permute-start.17 = (bf16[256,1024]{1,0:T(8,128)(2,1)}, bf16[256,1024]{1,0:T(8,128)(2,1)}, u32[]{:S(2)}, u32[]{:S(2)}) collective-permute-start(bf16[256,1024]{1,0:T(8,128)(2,1)} %collective-permute-done.15.refs_15_), channel_id=1, source_target_pairs={{0,8},{4,12},{8,0},{12,4},{16,24},{20,28},{24,16},{28,20},{1,9},{5... | collective-permute-start | bytes 1572872 | tf_op jit(solution)/shard_map/ppermute | solution.py:21
  153.1 1.5 collective-permute-start.29
  153.1 1.9 collective-permute-start.37
  154.6 11.9 %collective-permute-start.11 = (bf16[256,1024]{1,0:T(8,128)(2,1)S(1)}, bf16[256,1024]{1,0:T(8,128)(2,1)}, u32[]{:S(2)}, u32[]{:S(2)}) collective-permute-start(bf16[256,1024]{1,0:T(8,128)(2,1)S(1)} %collective-permute-done.7.refs_7_), channel_id=1, source_target_pairs={{0,4},{4,0},{8,12},{12,8},{16,20},{20,16},{24,28},{28,24},{1,5},{5... | collective-permute-start | bytes 1572872 | tf_op jit(solution)/shard_map/ppermute | solution.py:21
  155.0 18.8 %collective-permute-start.20 = (bf16[256,1024]{1,0:T(8,128)(2,1)}, bf16[256,1024]{1,0:T(8,128)(2,1)}, u32[]{:S(2)}, u32[]{:S(2)}) collective-permute-start(bf16[256,1024]{1,0:T(8,128)(2,1)} %collective-permute-done.16.refs_16_), channel_id=1, source_target_pairs={{0,4},{4,0},{8,12},{12,8},{16,20},{20,16},{24,28},{28,24},{1,5},{5... | collective-permute-start | bytes 1572872 | tf_op jit(solution)/shard_map/ppermute | solution.py:21
  155.1 18.6 %collective-permute-start.19 = (bf16[256,1024]{1,0:T(8,128)(2,1)}, bf16[256,1024]{1,0:T(8,128)(2,1)}, u32[]{:S(2)}, u32[]{:S(2)}) collective-permute-start(bf16[256,1024]{1,0:T(8,128)(2,1)} %collective-permute-done.15.refs_15_), channel_id=1, source_target_pairs={{0,4},{4,0},{8,12},{12,8},{16,20},{20,16},{24,28},{28,24},{1,5},{5... | collective-permute-start | bytes 1572872 | tf_op jit(solution)/shard_map/ppermute | solution.py:21
  160.6 14.0 %collective-permute-start.13 = (bf16[256,1024]{1,0:T(8,128)(2,1)}, bf16[256,1024]{1,0:T(8,128)(2,1)}, u32[]{:S(2)}, u32[]{:S(2)}) collective-permute-start(bf16[256,1024]{1,0:T(8,128)(2,1)} %collective-permute-done.9.refs_9_), channel_id=1, source_target_pairs={{0,4},{4,0},{8,12},{12,8},{16,20},{20,16},{24,28},{28,24},{1,5},{5... | collective-permute-start | bytes 1572872 | tf_op jit(solution)/shard_map/ppermute | solution.py:21
  161.9 12.7 %collective-permute-start.21 = (bf16[256,1024]{1,0:T(8,128)(2,1)}, bf16[256,1024]{1,0:T(8,128)(2,1)}, u32[]{:S(2)}, u32[]{:S(2)}) collective-permute-start(bf16[256,1024]{1,0:T(8,128)(2,1)} %collective-permute-done.17.refs_17_), channel_id=1, source_target_pairs={{0,4},{4,0},{8,12},{12,8},{16,20},{20,16},{24,28},{28,24},{1,5},{5... | collective-permute-start | bytes 1572872 | tf_op jit(solution)/shard_map/ppermute | solution.py:21
  166.6 27.8 %collective-permute-start.44 = (bf16[528,128]{1,0:T(8,128)(2,1)}, bf16[528,128]{1,0:T(8,128)(2,1)}, u32[]{:S(2)}, u32[]{:S(2)}) collective-permute-start(bf16[528,128]{1,0:T(8,128)(2,1)} %get-tuple-element.28), channel_id=1, source_target_pairs={{0,3},{1,0},{2,1},{3,2},{4,7},{5,4},{6,5},{7,6},{8,11},{9,8},{10,9... | collective-permute-start | bytes 405512 | tf_op jit(solution)/shard_map/ppermute | solution.py:17
  173.7 21.0 %collective-permute-start.45 = (bf16[528,128]{1,0:T(8,128)(2,1)}, bf16[528,128]{1,0:T(8,128)(2,1)}, u32[]{:S(2)}, u32[]{:S(2)}) collective-permute-start(bf16[528,128]{1,0:T(8,128)(2,1)} %get-tuple-element.29), channel_id=1, source_target_pairs={{0,2},{1,3},{2,0},{3,1},{4,6},{5,7},{6,4},{7,5},{8,10},{9,11},{10,... | collective-permute-start | bytes 405512 | tf_op jit(solution)/shard_map/ppermute | solution.py:17
  173.7 21.0 %collective-permute-start.46 = (bf16[528,128]{1,0:T(8,128)(2,1)}, bf16[528,128]{1,0:T(8,128)(2,1)}, u32[]{:S(2)}, u32[]{:S(2)}) collective-permute-start(bf16[528,128]{1,0:T(8,128)(2,1)} %get-tuple-element.30), channel_id=1, source_target_pairs={{0,1},{1,2},{2,3},{3,0},{4,5},{5,6},{6,7},{7,4},{8,9},{9,10},{10,1... | collective-permute-start | bytes 405512 | tf_op jit(solution)/shard_map/ppermute | solution.py:17
  190.5 9.4 %collective-permute-start.43 = (f32[1,512]{1,0:T(1,128)}, f32[1,512]{1,0:T(1,128)S(1)}, u32[]{:S(2)}, u32[]{:S(2)}) collective-permute-start(f32[1,512]{1,0:T(1,128)} %get-tuple-element.25), channel_id=1, source_target_pairs={{0,1},{1,2},{2,3},{3,0},{4,5},{5,6},{6,7},{7,4},{8,9},{9,10},{10,1... | collective-permute-start | bytes 6152 | tf_op jit(solution)/shard_map/ppermute | solution.py:17
  193.2 6.7 %collective-permute-start.42 = (f32[1,512]{1,0:T(1,128)}, f32[1,512]{1,0:T(1,128)S(1)}, u32[]{:S(2)}, u32[]{:S(2)}) collective-permute-start(f32[1,512]{1,0:T(1,128)} %get-tuple-element.25), channel_id=1, source_target_pairs={{0,3},{1,0},{2,1},{3,2},{4,7},{5,4},{6,5},{7,6},{8,11},{9,8},{10,9... | collective-permute-start | bytes 6152 | tf_op jit(solution)/shard_map/ppermute | solution.py:17
  194.4 5.6 %collective-permute-start.41 = (f32[1,512]{1,0:T(1,128)}, f32[1,512]{1,0:T(1,128)S(1)}, u32[]{:S(2)}, u32[]{:S(2)}) collective-permute-start(f32[1,512]{1,0:T(1,128)} %get-tuple-element.25), channel_id=1, source_target_pairs={{0,2},{1,3},{2,0},{3,1},{4,6},{5,7},{6,4},{7,5},{8,10},{9,11},{10,... | collective-permute-start | bytes 6152 | tf_op jit(solution)/shard_map/ppermute | solution.py:17
  (28 other events, 898.5 us)
where the time goes:
time: 201 us
  starting transfers between devices  72.3 us (36%)
  waiting for transfers between devices  71.5 us (36%)
  Pallas kernels  47.5 us (24%)
  local copies, waits for them, and re-layouts  5.09 us (3%)
  other arithmetic  3.12 us (2%)
    ppermute x19, starting transfers between devices, from_ahead(): return lax.ppermute(value, 'narrow', pairs)  51 us
    ppermute x28, waiting for transfers between devices, from_flipped(): lax.ppermute(value, 'wide', [(index, index ^ bit) for index in range(coun...  38.4 us
    ppermute x19, waiting for transfers between devices, from_ahead(): return lax.ppermute(value, 'narrow', pairs)  33.1 us
    pallas_call x4, Pallas kernels, pool_quarter(): pl.pallas_call(kernel, out_shape=jax.ShapeDtypeStruct((total, emb), jnp.b...  23.1 us
    ppermute x28, starting transfers between devices, from_flipped(): lax.ppermute(value, 'wide', [(index, index ^ bit) for index in range(coun...  17.7 us
    pallas_call x1, Pallas kernels, top_network(): pl.pallas_call(kernel, out_shape=(jax.ShapeDtypeStruct((rows, columns), j...  15.3 us
    pallas_call x1, Pallas kernels, place_rows(): pl.pallas_call(kernel, out_shape=jax.ShapeDtypeStruct((slot_count, emb),...  5.14 us
  transfers between devices with their start and end apart: 48, of which 15 were waited for; matrix products, arithmetic and copies ran while one was open for 2% of the time, Pallas kernels for 21%

commit v1 on v0

--- a/solution.py
+++ b/solution.py
@@ -84,14 +84,14 @@
                     table_ref[high * LOW : (high + 1) * LOW, :],
                     preferred_element_type=jnp.float32,
                 )
-            out_ref[pl.ds(start, tile), :] = acc.astype(jnp.bfloat16)
+            out_ref[pl.ds(start, tile), :] = acc.astype(out_ref.dtype)
             return carry
 
         lax.fori_loop(0, total // tile, tile_step, 0)
 
     return pl.pallas_call(
         kernel,
-        out_shape=jax.ShapeDtypeStruct((total, emb), jnp.bfloat16),
+        out_shape=jax.ShapeDtypeStruct((total, emb), jnp.bfloat16 if distance else jnp.float32),
         scratch_shapes=[pltpu.VMEM((highs, total, LOW), jnp.bfloat16)],
         cost_estimate=pl.CostEstimate(
             flops=4 * total * slot_count * emb, bytes_accessed=2 * total * emb, transcendentals=0
@@ -202,7 +202,7 @@
     quarter_rows, depth = features[0].shape
     rows = count * quarter_rows
     hidden = first_own.shape[1]
-    columns = second_own.shape[1] // count
+    columns = second_own.shape[1]
     flat_parts, layout = [], []
     for distance, pieces in parts.items():
         for mask, array, spans in pieces:
@@ -223,14 +223,13 @@
             spot = lax.rem(narrow_index + distance, count) * quarter_rows
             spot = pl.multiple_of(spot, quarter_rows)
             pltpu.make_async_copy(ref, feats.at[pl.ds(spot, quarter_rows), :], feat_sem).start()
-        column = pl.multiple_of(narrow_index * columns, columns)
 
         def fetch(which, wanted):
             if wanted == 0:
                 if which == 0:
                     source, target = first_ref, firsts.at[0]
                 else:
-                    source = second_ref.at[:, pl.ds(column, columns)]
+                    source = second_ref
                     target = seconds.at[:hidden, :]
                 pltpu.make_async_copy(source, target, sems.at[which, 0]).start()
             for (distance, mask, spans), ref in zip(layout, part_refs):
@@ -274,6 +273,8 @@
             w_out_ref[...], top_ref[...], (((1,), (1,)), ((), ())), preferred_element_type=jnp.float32
         )[:1]
 
+    held = 2 * count * hidden * (depth + columns + rows) + 2 * rows * (depth + columns)
+    room = min(held + 8 * rows * columns + (4 << 20), 60 << 20)
     anywhere = pl.BlockSpec(memory_space=pl.ANY)
     local = pl.BlockSpec(memory_space=pltpu.VMEM)
     return pl.pallas_call(
@@ -297,6 +298,7 @@
             bytes_accessed=2 * count * hidden * (depth + columns),
             transcendentals=0,
         ),
+        compiler_params=pltpu.CompilerParams(vmem_limit_bytes=room),
         name="top_network",
     )(
         *features,
@@ -318,9 +320,10 @@
         piece = after(piece, gate)
     pieces = [(0, piece)]
     for bit in bits:
-        pieces = pieces + [
-            (mask ^ bit, from_flipped(array, bit, wide_count)) for mask, array in pieces
-        ]
+        flipped = []
+        for mask, array in pieces:
+            flipped.append((mask ^ bit, from_flipped(array, bit, wide_count)))
+        pieces = pieces + flipped
     pieces = pieces + [
         (mask ^ 1, from_flipped(array, 1, wide_count)) for mask, array in pieces
     ]
@@ -375,8 +378,9 @@
             message = after(message, gate)
         return from_ahead(message, distance, count)
 
-    last = count - 1
-    arrived_slices = {distance: merged(distance) for distance in range(1, last)}
+    last = count // 2
+    early = [distance for distance in range(1, count) if distance != last]
+    arrived_slices = {distance: merged(distance) for distance in early[:1]}
 
     lookups = lookups.reshape(wide_count, count, quarter_rows // GROUP, GROUP * bag_size)
     lengths = lengths.reshape(wide_count * count, quarter_rows)
@@ -386,16 +390,20 @@
         pooled.append(own_part)
         if distance:
             sent.append(from_ahead(own_part, distance, count))
-    biases = [b_first]
-    for distance in range(1, count):
-        biases.append(from_ahead(after(b_first, own_part), distance, count))
+    for distance in early[1:]:
+        arrived_slices[distance] = merged(distance, pooled[0])
     summed = own_part.astype(jnp.float32)
     for part in sent:
         summed = summed + part.astype(jnp.float32)
     summed = summed.astype(jnp.bfloat16).reshape(wide_count, quarter_rows, emb)
-    arrived_slices[last] = [
-        from_ahead(after(piece, summed), last, count) for piece in slices_for(last)
+    biases = [b_first] + [
+        from_ahead(after(b_first, pooled[0]), distance, count) for distance in range(1, count)
     ]
+    first_piece = arrived_slices[1][:first_height]
+    for _ in range(2, last + 1):
+        first_piece = from_ahead(after(first_piece, own_part), 1, count)
+    second_piece = from_ahead(after(slices_for(last)[1], own_part), last, count)
+    arrived_slices[last] = first_piece, second_piece
     arrived = lax.all_to_all(summed, "wide", split_axis=0, concat_axis=0, tiled=True)
     own_features = jnp.transpose(arrived, (1, 0, 2)).reshape(quarter_rows, wide_count * emb)
     features = [own_features] + [
@@ -403,28 +411,33 @@
     ]
 
     sections = section_rows(
-        holder_counts[0], after(miss_rows[0], own_features), miss_slots[0], slot_count
+        holder_counts[0], after(miss_rows[0], own_part), miss_slots[0], slot_count
     )
     arrived_rows = [sections[0]] + [
         from_ahead(sections[distance], distance, count) for distance in range(1, count)
     ]
 
-    parts = {}
-    for distance in range(1, last):
-        ordered = bits if distance % 2 else bits[::-1]
-        parts[distance] = spread(
+    parts = {
+        distance: spread(
             arrived_slices[distance],
             both_spans,
-            ordered,
+            bits if place % 2 else bits[::-1],
             wide_count,
-            pooled[min(2 * distance - 1, last)],
+            own_part if place else pooled[0],
         )
+        for place, distance in enumerate(early)
+    }
     first_piece, second_piece = arrived_slices[last]
     parts[last] = spread(
         first_piece, ((0, 0, first_height),), bits, wide_count, own_features
     ) + spread(second_piece, ((1, 0, second_height),), bits[::-1], wide_count, own_features)
+    own_second = lax.dynamic_slice(
+        w_second,
+        (0, after(narrow_index, own_part) * columns),
+        (w_second.shape[0], columns),
+    )
     top_hidden, logit_terms = top_network(
-        features, w_first, w_second, parts, biases, b_second, w_out
+        features, w_first, own_second, parts, biases, b_second, w_out
     )
     shares = [logit_terms] + [
         from_ahead(logit_terms, distance, count) for distance in range(1, count)

time: 201 us -> 227 us (1.13)
  waiting for transfers between devices: 71.5 us -> 98.5 us
  local copies, waits for them, and re-layouts: 5.09 us -> 32 us
  starting transfers between devices: 72.3 us -> 47.2 us
  Pallas kernels: 47.5 us -> 44 us
    ppermute x19, waiting for transfers between devices: 33.1 us -> 62.5 us  [from_ahead(): return lax.ppermute(value, 'narrow', pairs)]
    unnamed x57 -> x95, local copies, waits for them, and re-layouts: 1.65 us -> 25.4 us
    ppermute x19, starting transfers between devices: 51 us -> 29.8 us  [from_ahead(): return lax.ppermute(value, 'narrow', pairs)]
    ppermute x28, starting transfers between devices: 17.7 us -> 13.4 us  [from_flipped(): lax.ppermute(value, 'wide', [(index, index ^ bit) for index in range(coun...]
    pallas_call x1, Pallas kernels: 15.3 us -> 11.6 us  [top_network(): pl.pallas_call(kernel, out_shape=(jax.ShapeDtypeStruct((rows, columns), j...]
    ppermute x28, waiting for transfers between devices: 38.4 us -> 36 us  [from_flipped(): lax.ppermute(value, 'wide', [(index, index ^ bit) for index in range(coun...]
  transfers between devices with their start and end apart: 48 -> 48, of which waited for: 15 -> 15; matrix products, arithmetic and copies ran while one was open for 2% -> 3% of each run, Pallas kernels for 21% -> 17%
where the time goes in v1:
time: 227 us; the launch traced here: 226 us
  waiting for transfers between devices  98.5 us (43%)
  starting transfers between devices  47.2 us (21%)
  Pallas kernels  44 us (19%)
  local copies, waits for them, and re-layouts  32 us (14%)
  other arithmetic  3.57 us (2%)
    ppermute x19, waiting for transfers between devices, from_ahead(): return lax.ppermute(value, 'narrow', pairs)  62.5 us
    ppermute x28, waiting for transfers between devices, from_flipped(): lax.ppermute(value, 'wide', [(index, index ^ bit) for index in range(coun...  36 us
    ppermute x19, starting transfers between devices, from_ahead(): return lax.ppermute(value, 'narrow', pairs)  29.8 us
    unnamed x95, local copies, waits for them, and re-layouts  25.4 us
    pallas_call x4, Pallas kernels, pool_quarter(): pl.pallas_call(kernel, out_shape=jax.ShapeDtypeStruct((total, emb), jnp.b...  23.3 us
    ppermute x28, starting transfers between devices, from_flipped(): lax.ppermute(value, 'wide', [(index, index ^ bit) for index in range(coun...  13.4 us
    pallas_call x1, Pallas kernels, top_network(): pl.pallas_call(kernel, out_shape=(jax.ShapeDtypeStruct((rows, columns), j...  11.6 us
    pallas_call x1, Pallas kernels, place_rows(): pl.pallas_call(kernel, out_shape=jax.ShapeDtypeStruct((slot_count, emb),...  5.13 us
  transfers between devices with their start and end apart: 48, of which 15 were waited for; matrix products, arithmetic and copies ran while one was open for 3% of the time, Pallas kernels for 17%

profile of v1, /device:TPU:0, one launch (start us, length us, event | category | flops | bytes accessed | tf_op | source)
XLA Modules:
  0.0 226.3 jit_solution(17673075267572958710)
XLA Ops:
  0.6 1.5 copy.18
  2.2 1.5 reshape_squeeze.6.lookups_ref
  3.7 5.8 %pool_quarter.6 = bf16[1024,128]{1,0:T(8,128)(2,1)} custom-call(s32[8,4,8,256]{3,2,1,0:T(8,128)} %reshape_squeeze.6.lookups_ref, s32[32,128]{1,0:T(8,128)} %bitcast.30, bf16[2048,128]{1,0:T(8,128)(2,1)} %bitcast.24), custom_call_target="tpu_custom_call" | custom-call | flops 1073741824 | bytes 262144 | tf_op jit(solution)/shard_map/pool_quarter/pallas_call | solution.py:92
  9.5 4.1 %collective-permute-start.1 = (bf16[1024,128]{1,0:T(8,128)(2,1)}, bf16[1024,128]{1,0:T(8,128)(2,1)S(1)}, u32[]{:S(2)}, u32[]{:S(2)}) collective-permute-start(bf16[1024,128]{1,0:T(8,128)(2,1)} %pool_quarter.6), channel_id=1, source_target_pairs={{0,2},{1,3},{2,0},{3,1},{4,6},{5,7},{6,4},{7,5},{8,10},{9,11},{10,... | collective-permute-start | bytes 786440 | tf_op jit(solution)/shard_map/ppermute | solution.py:17
  13.6 5.8 %pool_quarter.7 = bf16[1024,128]{1,0:T(8,128)(2,1)} custom-call(s32[8,4,8,256]{3,2,1,0:T(8,128)} %reshape_squeeze.6.lookups_ref, s32[32,128]{1,0:T(8,128)} %bitcast.31, bf16[2048,128]{1,0:T(8,128)(2,1)} %bitcast.25), custom_call_target="tpu_custom_call" | custom-call | flops 1073741824 | bytes 262144 | tf_op jit(solution)/shard_map/pool_quarter/pallas_call | solution.py:92
  19.3 1.3 collective-permute-start.2
  20.7 5.8 %pool_quarter.5 = bf16[1024,128]{1,0:T(8,128)(2,1)} custom-call(s32[8,4,8,256]{3,2,1,0:T(8,128)} %reshape_squeeze.6.lookups_ref, s32[32,128]{1,0:T(8,128)} %bitcast.32, bf16[2048,128]{1,0:T(8,128)(2,1)} %bitcast.26), custom_call_target="tpu_custom_call" | custom-call | flops 1073741824 | bytes 262144 | tf_op jit(solution)/shard_map/pool_quarter/pallas_call | solution.py:92
  27.1 6.0 %pool_quarter.4 = f32[1024,128]{1,0:T(8,128)} custom-call(s32[8,4,8,256]{3,2,1,0:T(8,128)} %reshape_squeeze.6.lookups_ref, s32[32,128]{1,0:T(8,128)} %bitcast.33, bf16[2048,128]{1,0:T(8,128)(2,1)} %bitcast.27), custom_call_target="tpu_custom_call" | custom-call | flops 1073741824 | bytes 262144 | tf_op jit(solution)/shard_map/pool_quarter/pallas_call | solution.py:92
  33.1 3.8 %collective-permute-done.2 = bf16[1024,128]{1,0:T(8,128)(2,1)S(1)} collective-permute-done((bf16[1024,128]{1,0:T(8,128)(2,1)}, bf16[1024,128]{1,0:T(8,128)(2,1)S(1)}, u32[]{:S(2)}, u32[]{:S(2)}) %collective-permute-start.2) | collective-permute-done | bytes 262176 | tf_op jit(solution)/shard_map/ppermute | solution.py:17
  36.9 1.9 add_convert_fusion
  38.8 4.0 %all-to-all-start = ((bf16[8,128,128]{2,1,0:T(8,128)(2,1)}), bf16[8,128,128]{2,1,0:T(8,128)(2,1)}, u32[]{:S(2)}, u32[]{:S(2)}) async-start(bf16[8,128,128]{2,1,0:T(8,128)(2,1)} %bitcast.2), calls=%async_computation | async-start | bytes 524288 | tf_op jit(solution)/shard_map/all_to_all | solution.py:407
  42.9 1.9 fusion
  44.8 1.1 pad_maximum_fusion
  45.9 3.5 %collective-permute-start.6 = (bf16[256,1024]{1,0:T(8,128)(2,1)}, bf16[256,1024]{1,0:T(8,128)(2,1)S(1)}, u32[]{:S(2)}, u32[]{:S(2)}) collective-permute-start(bf16[256,1024]{1,0:T(8,128)(2,1)} %get-tuple-element.39), channel_id=1, source_target_pairs={{0,3},{1,0},{2,1},{3,2},{4,7},{5,4},{6,5},{7,6},{8,11},{9,8},{10,9... | collective-permute-start | bytes 1572872 | tf_op jit(solution)/shard_map/ppermute | solution.py:17
  49.4 1.2 collective-permute-start.14
  50.6 1.0 copy_bitcast_fusion.refs_0_
  51.6 32.2 %collective-permute-done.30.refs_30_ = bf16[128,1024]{1,0:T(8,128)(2,1)} collective-permute-done((bf16[128,1024]{1,0:T(8,128)(2,1)}, bf16[128,1024]{1,0:T(8,128)(2,1)}, u32[]{:S(2)}, u32[]{:S(2)}) %collective-permute-start.30) | collective-permute-done | bytes 262176 | tf_op jit(solution)/shard_map/ppermute | solution.py:17
  83.8 1.6 collective-permute-start.32
  85.5 5.4 %collective-permute-done.40 = f32[1024]{0:T(1024)S(1)} collective-permute-done((f32[1024]{0:T(1024)S(1)}, f32[1024]{0:T(1024)S(1)}, u32[]{:S(2)}, u32[]{:S(2)}) %collective-permute-start.40) | collective-permute-done | bytes 4128 | tf_op jit(solution)/shard_map/ppermute | solution.py:17
  90.9 4.5 %collective-permute-done.39 = f32[1024]{0:T(1024)S(1)} collective-permute-done((f32[1024]{0:T(1024)S(1)}, f32[1024]{0:T(1024)S(1)}, u32[]{:S(2)}, u32[]{:S(2)}) %collective-permute-start.39) | collective-permute-done | bytes 4128 | tf_op jit(solution)/shard_map/ppermute | solution.py:17
  95.4 1.5 collective-permute-start.31
  96.9 2.1 collective-permute-done.38
  99.0 2.4 %collective-permute-start.4 = (bf16[128,1024]{1,0:T(8,128)(2,1)S(1)}, bf16[128,1024]{1,0:T(8,128)(2,1)S(1)}, u32[]{:S(2)}, u32[]{:S(2)}) collective-permute-start(bf16[128,1024]{1,0:T(8,128)(2,1)S(1)} %copy_bitcast_fusion.refs_0_), channel_id=1, source_target_pairs={{0,2},{1,3},{2,0},{3,1},{4,6},{5,7},{6,4},{7,5},{8,10},{9,11},{10,... | collective-permute-start | bytes 786440 | tf_op jit(solution)/shard_map/ppermute | solution.py:17
  102.1 1.4 collective-permute-start.22
  104.8 5.2 %collective-permute-done.5.refs_3_ = bf16[128,1024]{1,0:T(8,128)(2,1)S(1)} collective-permute-done((bf16[128,1024]{1,0:T(8,128)(2,1)S(1)}, bf16[128,1024]{1,0:T(8,128)(2,1)S(1)}, u32[]{:S(2)}, u32[]{:S(2)}) %collective-permute-start.5) | collective-permute-done | bytes 262176 | tf_op jit(solution)/shard_map/ppermute | solution.py:17
  110.7 6.5 %collective-permute-done.4.refs_2_ = bf16[128,1024]{1,0:T(8,128)(2,1)S(1)} collective-permute-done((bf16[128,1024]{1,0:T(8,128)(2,1)S(1)}, bf16[128,1024]{1,0:T(8,128)(2,1)S(1)}, u32[]{:S(2)}, u32[]{:S(2)}) %collective-permute-start.4) | collective-permute-done | bytes 262176 | tf_op jit(solution)/shard_map/ppermute | solution.py:17
  119.7 2.4 %collective-permute-done.3.refs_1_ = bf16[128,1024]{1,0:T(8,128)(2,1)S(1)} collective-permute-done((bf16[128,1024]{1,0:T(8,128)(2,1)S(1)}, bf16[128,1024]{1,0:T(8,128)(2,1)S(1)}, u32[]{:S(2)}, u32[]{:S(2)}) %collective-permute-start.3) | collective-permute-done | bytes 262176 | tf_op jit(solution)/shard_map/ppermute | solution.py:17
  123.5 1.2 collective-permute-start.24
  126.6 1.5 collective-permute-start.8
  129.7 3.0 %collective-permute-done.24.refs_24_ = bf16[128,1024]{1,0:T(8,128)(2,1)S(1)} collective-permute-done((bf16[128,1024]{1,0:T(8,128)(2,1)S(1)}, bf16[128,1024]{1,0:T(8,128)(2,1)S(1)}, u32[]{:S(2)}, u32[]{:S(2)}) %collective-permute-start.24) | collective-permute-done | bytes 262176 | tf_op jit(solution)/shard_map/ppermute | solution.py:21
  132.6 1.9 collective-permute-done.23.refs_23_
  136.7 9.0 %collective-permute-done.8.refs_8_ = bf16[256,1024]{1,0:T(8,128)(2,1)S(1)} collective-permute-done((bf16[256,1024]{1,0:T(8,128)(2,1)S(1)}, bf16[256,1024]{1,0:T(8,128)(2,1)S(1)}, u32[]{:S(2)}, u32[]{:S(2)}) %collective-permute-start.8) | collective-permute-done | bytes 524320 | tf_op jit(solution)/shard_map/ppermute | solution.py:21
  148.5 6.2 %collective-permute-done.16.refs_16_ = bf16[256,1024]{1,0:T(8,128)(2,1)} collective-permute-done((bf16[256,1024]{1,0:T(8,128)(2,1)S(1)}, bf16[256,1024]{1,0:T(8,128)(2,1)}, u32[]{:S(2)}, u32[]{:S(2)}) %collective-permute-start.16) | collective-permute-done | bytes 524320 | tf_op jit(solution)/shard_map/ppermute | solution.py:21
  159.9 1.2 collective-permute-start.25
  161.8 14.9 %collective-permute-done.25.refs_25_ = bf16[128,1024]{1,0:T(8,128)(2,1)S(1)} collective-permute-done((bf16[128,1024]{1,0:T(8,128)(2,1)S(1)}, bf16[128,1024]{1,0:T(8,128)(2,1)S(1)}, u32[]{:S(2)}, u32[]{:S(2)}) %collective-permute-start.25) | collective-permute-done | bytes 262176 | tf_op jit(solution)/shard_map/ppermute | solution.py:21
  178.8 4.0 %section_rows.1 = (bf16[528,128]{1,0:T(8,128)(2,1)}, bf16[528,128]{1,0:T(8,128)(2,1)}, bf16[528,128]{1,0:T(8,128)(2,1)}, bf16[528,128]{1,0:T(8,128)(2,1)}) custom-call(s32[4]{0:T(128)} %bitcast.34, bf16[1024,128]{1,0:T(8,128)(2,1)} %bitcast.29, s32[1,1024]{1,0:T(1,128)} %slots_ref.1), custom_call_target="tpu_custom_call" | custom-call | flops 536870912 | bytes 524288 | tf_op jit(solution)/shard_map/section_rows/pallas_call | solution.py:138
  183.4 2.1 constant_dynamic-slice_fusion.1.refs_5_
  185.5 9.6 %collective-permute-start.44 = (bf16[528,128]{1,0:T(8,128)(2,1)}, bf16[528,128]{1,0:T(8,128)(2,1)S(1)}, u32[]{:S(2)}, u32[]{:S(2)}) collective-permute-start(bf16[528,128]{1,0:T(8,128)(2,1)} %get-tuple-element.32), channel_id=1, source_target_pairs={{0,3},{1,0},{2,1},{3,2},{4,7},{5,4},{6,5},{7,6},{8,11},{9,8},{10,9... | collective-permute-start | bytes 405512 | tf_op jit(solution)/shard_map/ppermute | solution.py:17
  196.9 0.9 copy-done.28
  197.8 0.9 copy-done.30
  198.8 0.9 copy-done.32
  199.7 0.9 copy-done.34
  201.6 0.9 copy-done.38
  202.6 0.9 copy-done.40
  204.5 11.6 %top_network.1 = (bf16[512,1024]{1,0:T(8,128)(2,1)}, f32[1,512]{1,0:T(1,128)S(1)}) custom-call(bf16[128,1024]{1,0:T(8,128)(2,1)S(1)} %copy_bitcast_fusion.refs_0_, bf16[128,1024]{1,0:T(8,128)(2,1)S(1)} %copy-done.22, bf16[128,1024]{1,0:T(8,128)(2,1)S(1)} %copy-done.18, bf16[128,1024]{1,0:T(8,128)(2,1)S(1)} %copy-done.16, bf16[1024,1024]{1,0:T(8,128)(2,1)S(1)} %copy-done, ...), custom_call_target="tpu_custom_call" | custom-call | flops 8589934592 | bytes 16777216 | tf_op jit(solution)/shard_map/top_network/pallas_call | solution.py:280
  216.0 2.9 %collective-permute-start.43 = (f32[1,512]{1,0:T(1,128)S(1)}, f32[1,512]{1,0:T(1,128)S(1)}, u32[]{:S(2)}, u32[]{:S(2)}) collective-permute-start(f32[1,512]{1,0:T(1,128)S(1)} %get-tuple-element.29), channel_id=1, source_target_pairs={{0,1},{1,2},{2,3},{3,0},{4,5},{5,6},{6,7},{7,4},{8,9},{9,10},{10,1... | collective-permute-start | bytes 6152 | tf_op jit(solution)/shard_map/ppermute | solution.py:17
  218.9 1.0 collective-permute-start.42
  220.6 5.1 %place_rows.1 = bf16[2048,128]{1,0:T(8,128)(2,1)} custom-call(bf16[528,128]{1,0:T(8,128)(2,1)} %get-tuple-element.31.refs_0_, bf16[528,128]{1,0:T(8,128)(2,1)} %copy-done.46, bf16[528,128]{1,0:T(8,128)(2,1)} %collective-permute-done.45.refs_2_, bf16[528,128]{1,0:T(8,128)(2,1)} %collective-permute-done.46.refs_3_, bf16[2048,128]{1,0:T(8,128)(2,1)} %bitcast.28), custom_call_target="tpu_custom_call" | custom-call | flops 2147483648 | bytes 1048576 | tf_op jit(solution)/shard_map/place_rows/pallas_call | solution.py:187
  (160 shorter events, 29.0 us)
Async XLA Ops:
  9.5 23.6 %collective-permute-start.1 = (bf16[1024,128]{1,0:T(8,128)(2,1)}, bf16[1024,128]{1,0:T(8,128)(2,1)S(1)}, u32[]{:S(2)}, u32[]{:S(2)}) collective-permute-start(bf16[1024,128]{1,0:T(8,128)(2,1)} %pool_quarter.6), channel_id=1, source_target_pairs={{0,2},{1,3},{2,0},{3,1},{4,6},{5,7},{6,4},{7,5},{8,10},{9,11},{10,... | collective-permute-start | bytes 786440 | tf_op jit(solution)/shard_map/ppermute | solution.py:17
  19.3 17.6 %collective-permute-start.2 = (bf16[1024,128]{1,0:T(8,128)(2,1)}, bf16[1024,128]{1,0:T(8,128)(2,1)S(1)}, u32[]{:S(2)}, u32[]{:S(2)}) collective-permute-start(bf16[1024,128]{1,0:T(8,128)(2,1)} %pool_quarter.7), channel_id=1, source_target_pairs={{0,3},{1,0},{2,1},{3,2},{4,7},{5,4},{6,5},{7,6},{8,11},{9,8},{10,9... | collective-permute-start | bytes 786440 | tf_op jit(solution)/shard_map/ppermute | solution.py:17
  26.4 10.5 %collective-permute-start = (bf16[1024,128]{1,0:T(8,128)(2,1)}, bf16[1024,128]{1,0:T(8,128)(2,1)S(1)}, u32[]{:S(2)}, u32[]{:S(2)}) collective-permute-start(bf16[1024,128]{1,0:T(8,128)(2,1)} %pool_quarter.5), channel_id=1, source_target_pairs={{0,1},{1,2},{2,3},{3,0},{4,5},{5,6},{6,7},{7,4},{8,9},{9,10},{10,1... | collective-permute-start | bytes 786440 | tf_op jit(solution)/shard_map/ppermute | solution.py:17
  38.8 11.8 %all-to-all-start = ((bf16[8,128,128]{2,1,0:T(8,128)(2,1)}), bf16[8,128,128]{2,1,0:T(8,128)(2,1)}, u32[]{:S(2)}, u32[]{:S(2)}) async-start(bf16[8,128,128]{2,1,0:T(8,128)(2,1)} %bitcast.2), calls=%async_computation | async-start | bytes 524288 | tf_op jit(solution)/shard_map/all_to_all | solution.py:407
  45.9 49.5 %collective-permute-start.6 = (bf16[256,1024]{1,0:T(8,128)(2,1)}, bf16[256,1024]{1,0:T(8,128)(2,1)S(1)}, u32[]{:S(2)}, u32[]{:S(2)}) collective-permute-start(bf16[256,1024]{1,0:T(8,128)(2,1)} %get-tuple-element.39), channel_id=1, source_target_pairs={{0,3},{1,0},{2,1},{3,2},{4,7},{5,4},{6,5},{7,6},{8,11},{9,8},{10,9... | collective-permute-start | bytes 1572872 | tf_op jit(solution)/shard_map/ppermute | solution.py:17
  49.4 34.4 %collective-permute-start.30 = (bf16[128,1024]{1,0:T(8,128)(2,1)}, bf16[128,1024]{1,0:T(8,128)(2,1)}, u32[]{:S(2)}, u32[]{:S(2)}) collective-permute-start(bf16[128,1024]{1,0:T(8,128)(2,1)} %get-tuple-element.25), channel_id=1, source_target_pairs={{0,2},{1,3},{2,0},{3,1},{4,6},{5,7},{6,4},{7,5},{8,10},{9,11},{10,... | collective-permute-start | bytes 786440 | tf_op jit(solution)/shard_map/ppermute | solution.py:17
  49.4 49.5 %collective-permute-start.14 = (bf16[256,1024]{1,0:T(8,128)(2,1)}, bf16[256,1024]{1,0:T(8,128)(2,1)S(1)}, u32[]{:S(2)}, u32[]{:S(2)}) collective-permute-start(bf16[256,1024]{1,0:T(8,128)(2,1)} %get-tuple-element.21), channel_id=1, source_target_pairs={{0,1},{1,2},{2,3},{3,0},{4,5},{5,6},{6,7},{7,4},{8,9},{9,10},{10,1... | collective-permute-start | bytes 1572872 | tf_op jit(solution)/shard_map/ppermute | solution.py:17
  83.8 17.6 %collective-permute-start.34 = (bf16[128,1024]{1,0:T(8,128)(2,1)}, bf16[128,1024]{1,0:T(8,128)(2,1)S(1)}, u32[]{:S(2)}, u32[]{:S(2)}) collective-permute-start(bf16[128,1024]{1,0:T(8,128)(2,1)} %collective-permute-done.30.refs_30_), channel_id=1, source_target_pairs={{0,4},{4,0},{8,12},{12,8},{16,20},{20,16},{24,28},{28,24},{1,5},{5... | collective-permute-start | bytes 786440 | tf_op jit(solution)/shard_map/ppermute | solution.py:21
  83.8 19.7 %collective-permute-start.32 = (bf16[128,1024]{1,0:T(8,128)(2,1)}, bf16[128,1024]{1,0:T(8,128)(2,1)S(1)}, u32[]{:S(2)}, u32[]{:S(2)}) collective-permute-start(bf16[128,1024]{1,0:T(8,128)(2,1)} %collective-permute-done.30.refs_30_), channel_id=1, source_target_pairs={{0,8},{4,12},{8,0},{12,4},{16,24},{20,28},{24,16},{28,20},{1,9},{5... | collective-permute-start | bytes 786440 | tf_op jit(solution)/shard_map/ppermute | solution.py:21
  85.4 5.4 %collective-permute-start.40 = (f32[1024]{0:T(1024)S(1)}, f32[1024]{0:T(1024)S(1)}, u32[]{:S(2)}, u32[]{:S(2)}) collective-permute-start(f32[1024]{0:T(1024)S(1)} %copy-done.44), channel_id=1, source_target_pairs={{0,1},{1,2},{2,3},{3,0},{4,5},{5,6},{6,7},{7,4},{8,9},{9,10},{10,1... | collective-permute-start | bytes 12296 | tf_op jit(solution)/shard_map/ppermute | solution.py:17
  90.9 4.5 %collective-permute-start.39 = (f32[1024]{0:T(1024)S(1)}, f32[1024]{0:T(1024)S(1)}, u32[]{:S(2)}, u32[]{:S(2)}) collective-permute-start(f32[1024]{0:T(1024)S(1)} %copy-done.44), channel_id=1, source_target_pairs={{0,2},{1,3},{2,0},{3,1},{4,6},{5,7},{6,4},{7,5},{8,10},{9,11},{10,... | collective-permute-start | bytes 12296 | tf_op jit(solution)/shard_map/ppermute | solution.py:17
  95.4 3.6 %collective-permute-start.38 = (f32[1024]{0:T(1024)S(1)}, f32[1024]{0:T(1024)S(1)}, u32[]{:S(2)}, u32[]{:S(2)}) collective-permute-start(f32[1024]{0:T(1024)S(1)} %copy-done.44), channel_id=1, source_target_pairs={{0,3},{1,0},{2,1},{3,2},{4,7},{5,4},{6,5},{7,6},{8,11},{9,8},{10,9... | collective-permute-start | bytes 12296 | tf_op jit(solution)/shard_map/ppermute | solution.py:17
  95.4 8.7 %collective-permute-start.31 = (bf16[128,1024]{1,0:T(8,128)(2,1)}, bf16[128,1024]{1,0:T(8,128)(2,1)S(1)}, u32[]{:S(2)}, u32[]{:S(2)}) collective-permute-start(bf16[128,1024]{1,0:T(8,128)(2,1)} %collective-permute-done.30.refs_30_), channel_id=1, source_target_pairs={{0,16},{4,20},{8,24},{12,28},{16,0},{20,4},{24,8},{28,12},{1,17},{... | collective-permute-start | bytes 786440 | tf_op jit(solution)/shard_map/ppermute | solution.py:21
  99.0 11.0 %collective-permute-start.5 = (bf16[128,1024]{1,0:T(8,128)(2,1)S(1)}, bf16[128,1024]{1,0:T(8,128)(2,1)S(1)}, u32[]{:S(2)}, u32[]{:S(2)}) collective-permute-start(bf16[128,1024]{1,0:T(8,128)(2,1)S(1)} %copy_bitcast_fusion.refs_0_), channel_id=1, source_target_pairs={{0,1},{1,2},{2,3},{3,0},{4,5},{5,6},{6,7},{7,4},{8,9},{9,10},{10,1... | collective-permute-start | bytes 786440 | tf_op jit(solution)/shard_map/ppermute | solution.py:17
  99.0 18.2 %collective-permute-start.4 = (bf16[128,1024]{1,0:T(8,128)(2,1)S(1)}, bf16[128,1024]{1,0:T(8,128)(2,1)S(1)}, u32[]{:S(2)}, u32[]{:S(2)}) collective-permute-start(bf16[128,1024]{1,0:T(8,128)(2,1)S(1)} %copy_bitcast_fusion.refs_0_), channel_id=1, source_target_pairs={{0,2},{1,3},{2,0},{3,1},{4,6},{5,7},{6,4},{7,5},{8,10},{9,11},{10,... | collective-permute-start | bytes 786440 | tf_op jit(solution)/shard_map/ppermute | solution.py:17
  102.1 16.3 %collective-permute-start.22 = (bf16[128,1024]{1,0:T(8,128)(2,1)S(1)}, bf16[128,1024]{1,0:T(8,128)(2,1)S(1)}, u32[]{:S(2)}, u32[]{:S(2)}) collective-permute-start(bf16[128,1024]{1,0:T(8,128)(2,1)S(1)} %slice.4), channel_id=1, source_target_pairs={{0,3},{1,0},{2,1},{3,2},{4,7},{5,4},{6,5},{7,6},{8,11},{9,8},{10,9... | collective-permute-start | bytes 786440 | tf_op jit(solution)/shard_map/ppermute | solution.py:17
  103.5 18.5 %collective-permute-start.3 = (bf16[128,1024]{1,0:T(8,128)(2,1)S(1)}, bf16[128,1024]{1,0:T(8,128)(2,1)S(1)}, u32[]{:S(2)}, u32[]{:S(2)}) collective-permute-start(bf16[128,1024]{1,0:T(8,128)(2,1)S(1)} %copy_bitcast_fusion.refs_0_), channel_id=1, source_target_pairs={{0,3},{1,0},{2,1},{3,2},{4,7},{5,4},{6,5},{7,6},{8,11},{9,8},{10,9... | collective-permute-start | bytes 786440 | tf_op jit(solution)/shard_map/ppermute | solution.py:17
  104.1 18.7 %collective-permute-start.36 = (bf16[128,1024]{1,0:T(8,128)(2,1)S(1)}, bf16[128,1024]{1,0:T(8,128)(2,1)S(1)}, u32[]{:S(2)}, u32[]{:S(2)}) collective-permute-start(bf16[128,1024]{1,0:T(8,128)(2,1)S(1)} %collective-permute-done.32.refs_32_), channel_id=1, source_target_pairs={{0,4},{4,0},{8,12},{12,8},{16,20},{20,16},{24,28},{28,24},{1,5},{5... | collective-permute-start | bytes 786440 | tf_op jit(solution)/shard_map/ppermute | solution.py:21
  110.7 13.9 %collective-permute-start.35 = (bf16[128,1024]{1,0:T(8,128)(2,1)S(1)}, bf16[128,1024]{1,0:T(8,128)(2,1)S(1)}, u32[]{:S(2)}, u32[]{:S(2)}) collective-permute-start(bf16[128,1024]{1,0:T(8,128)(2,1)S(1)} %collective-permute-done.31.refs_31_), channel_id=1, source_target_pairs={{0,4},{4,0},{8,12},{12,8},{16,20},{20,16},{24,28},{28,24},{1,5},{5... | collective-permute-start | bytes 786440 | tf_op jit(solution)/shard_map/ppermute | solution.py:21
  117.9 17.5 %collective-permute-start.10 = (bf16[256,1024]{1,0:T(8,128)(2,1)S(1)}, bf16[256,1024]{1,0:T(8,128)(2,1)S(1)}, u32[]{:S(2)}, u32[]{:S(2)}) collective-permute-start(bf16[256,1024]{1,0:T(8,128)(2,1)S(1)} %collective-permute-done.6.refs_6_), channel_id=1, source_target_pairs={{0,4},{4,0},{8,12},{12,8},{16,20},{20,16},{24,28},{28,24},{1,5},{5... | collective-permute-start | bytes 1572872 | tf_op jit(solution)/shard_map/ppermute | solution.py:21
  118.4 8.3 %collective-permute-start.33 = (bf16[128,1024]{1,0:T(8,128)(2,1)S(1)}, bf16[128,1024]{1,0:T(8,128)(2,1)S(1)}, u32[]{:S(2)}, u32[]{:S(2)}) collective-permute-start(bf16[128,1024]{1,0:T(8,128)(2,1)S(1)} %collective-permute-done.31.refs_31_), channel_id=1, source_target_pairs={{0,8},{4,12},{8,0},{12,4},{16,24},{20,28},{24,16},{28,20},{1,9},{5... | collective-permute-start | bytes 786440 | tf_op jit(solution)/shard_map/ppermute | solution.py:21
  122.8 5.4 %collective-permute-start.26 = (bf16[128,1024]{1,0:T(8,128)(2,1)S(1)}, bf16[128,1024]{1,0:T(8,128)(2,1)S(1)}, u32[]{:S(2)}, u32[]{:S(2)}) collective-permute-start(bf16[128,1024]{1,0:T(8,128)(2,1)S(1)} %collective-permute-done.22.refs_22_), channel_id=1, source_target_pairs={{0,4},{4,0},{8,12},{12,8},{16,20},{20,16},{24,28},{28,24},{1,5},{5... | collective-permute-start | bytes 786440 | tf_op jit(solution)/shard_map/ppermute | solution.py:21
  123.5 9.2 %collective-permute-start.24 = (bf16[128,1024]{1,0:T(8,128)(2,1)S(1)}, bf16[128,1024]{1,0:T(8,128)(2,1)S(1)}, u32[]{:S(2)}, u32[]{:S(2)}) collective-permute-start(bf16[128,1024]{1,0:T(8,128)(2,1)S(1)} %collective-permute-done.22.refs_22_), channel_id=1, source_target_pairs={{0,16},{4,20},{8,24},{12,28},{16,0},{20,4},{24,8},{28,12},{1,17},{... | collective-permute-start | bytes 786440 | tf_op jit(solution)/shard_map/ppermute | solution.py:21
  125.4 9.2 %collective-permute-start.23 = (bf16[128,1024]{1,0:T(8,128)(2,1)S(1)}, bf16[128,1024]{1,0:T(8,128)(2,1)S(1)}, u32[]{:S(2)}, u32[]{:S(2)}) collective-permute-start(bf16[128,1024]{1,0:T(8,128)(2,1)S(1)} %collective-permute-done.22.refs_22_), channel_id=1, source_target_pairs={{0,8},{4,12},{8,0},{12,4},{16,24},{20,28},{24,16},{28,20},{1,9},{5... | collective-permute-start | bytes 786440 | tf_op jit(solution)/shard_map/ppermute | solution.py:21
  126.6 19.2 %collective-permute-start.8 = (bf16[256,1024]{1,0:T(8,128)(2,1)S(1)}, bf16[256,1024]{1,0:T(8,128)(2,1)S(1)}, u32[]{:S(2)}, u32[]{:S(2)}) collective-permute-start(bf16[256,1024]{1,0:T(8,128)(2,1)S(1)} %collective-permute-done.6.refs_6_), channel_id=1, source_target_pairs={{0,8},{4,12},{8,0},{12,4},{16,24},{20,28},{24,16},{28,20},{1,9},{5... | collective-permute-start | bytes 1572872 | tf_op jit(solution)/shard_map/ppermute | solution.py:21
  128.8 17.7 %collective-permute-start.7 = (bf16[256,1024]{1,0:T(8,128)(2,1)S(1)}, bf16[256,1024]{1,0:T(8,128)(2,1)}, u32[]{:S(2)}, u32[]{:S(2)}) collective-permute-start(bf16[256,1024]{1,0:T(8,128)(2,1)S(1)} %collective-permute-done.6.refs_6_), channel_id=1, source_target_pairs={{0,16},{4,20},{8,24},{12,28},{16,0},{20,4},{24,8},{28,12},{1,17},{... | collective-permute-start | bytes 1572872 | tf_op jit(solution)/shard_map/ppermute | solution.py:21
  132.6 15.1 %collective-permute-start.18 = (bf16[256,1024]{1,0:T(8,128)(2,1)S(1)}, bf16[256,1024]{1,0:T(8,128)(2,1)S(1)}, u32[]{:S(2)}, u32[]{:S(2)}) collective-permute-start(bf16[256,1024]{1,0:T(8,128)(2,1)S(1)} %collective-permute-done.14.refs_14_), channel_id=1, source_target_pairs={{0,4},{4,0},{8,12},{12,8},{16,20},{20,16},{24,28},{28,24},{1,5},{5... | collective-permute-start | bytes 1572872 | tf_op jit(solution)/shard_map/ppermute | solution.py:21
  134.6 20.2 %collective-permute-start.16 = (bf16[256,1024]{1,0:T(8,128)(2,1)S(1)}, bf16[256,1024]{1,0:T(8,128)(2,1)}, u32[]{:S(2)}, u32[]{:S(2)}) collective-permute-start(bf16[256,1024]{1,0:T(8,128)(2,1)S(1)} %collective-permute-done.14.refs_14_), channel_id=1, source_target_pairs={{0,16},{4,20},{8,24},{12,28},{16,0},{20,4},{24,8},{28,12},{1,17},{... | collective-permute-start | bytes 1572872 | tf_op jit(solution)/shard_map/ppermute | solution.py:21
  136.2 20.2 %collective-permute-start.15 = (bf16[256,1024]{1,0:T(8,128)(2,1)S(1)}, bf16[256,1024]{1,0:T(8,128)(2,1)}, u32[]{:S(2)}, u32[]{:S(2)}) collective-permute-start(bf16[256,1024]{1,0:T(8,128)(2,1)S(1)} %collective-permute-done.14.refs_14_), channel_id=1, source_target_pairs={{0,8},{4,12},{8,0},{12,4},{16,24},{20,28},{24,16},{28,20},{1,9},{5... | collective-permute-start | bytes 1572872 | tf_op jit(solution)/shard_map/ppermute | solution.py:21
  145.8 11.2 %collective-permute-start.37 = (bf16[128,1024]{1,0:T(8,128)(2,1)S(1)}, bf16[128,1024]{1,0:T(8,128)(2,1)S(1)}, u32[]{:S(2)}, u32[]{:S(2)}) collective-permute-start(bf16[128,1024]{1,0:T(8,128)(2,1)S(1)} %collective-permute-done.33.refs_33_), channel_id=1, source_target_pairs={{0,4},{4,0},{8,12},{12,8},{16,20},{20,16},{24,28},{28,24},{1,5},{5... | collective-permute-start | bytes 786440 | tf_op jit(solution)/shard_map/ppermute | solution.py:21
  146.5 12.0 %collective-permute-start.28 = (bf16[128,1024]{1,0:T(8,128)(2,1)S(1)}, bf16[128,1024]{1,0:T(8,128)(2,1)S(1)}, u32[]{:S(2)}, u32[]{:S(2)}) collective-permute-start(bf16[128,1024]{1,0:T(8,128)(2,1)S(1)} %collective-permute-done.24.refs_24_), channel_id=1, source_target_pairs={{0,4},{4,0},{8,12},{12,8},{16,20},{20,16},{24,28},{28,24},{1,5},{5... | collective-permute-start | bytes 786440 | tf_op jit(solution)/shard_map/ppermute | solution.py:21
  148.5 10.7 %collective-permute-start.27 = (bf16[128,1024]{1,0:T(8,128)(2,1)S(1)}, bf16[128,1024]{1,0:T(8,128)(2,1)S(1)}, u32[]{:S(2)}, u32[]{:S(2)}) collective-permute-start(bf16[128,1024]{1,0:T(8,128)(2,1)S(1)} %collective-permute-done.23.refs_23_), channel_id=1, source_target_pairs={{0,4},{4,0},{8,12},{12,8},{16,20},{20,16},{24,28},{28,24},{1,5},{5... | collective-permute-start | bytes 786440 | tf_op jit(solution)/shard_map/ppermute | solution.py:21
  154.8 21.9 %collective-permute-start.12 = (bf16[256,1024]{1,0:T(8,128)(2,1)S(1)}, bf16[256,1024]{1,0:T(8,128)(2,1)S(1)}, u32[]{:S(2)}, u32[]{:S(2)}) collective-permute-start(bf16[256,1024]{1,0:T(8,128)(2,1)S(1)} %collective-permute-done.8.refs_8_), channel_id=1, source_target_pairs={{0,4},{4,0},{8,12},{12,8},{16,20},{20,16},{24,28},{28,24},{1,5},{5... | collective-permute-start | bytes 1572872 | tf_op jit(solution)/shard_map/ppermute | solution.py:21
  156.4 21.8 %collective-permute-start.9 = (bf16[256,1024]{1,0:T(8,128)(2,1)}, bf16[256,1024]{1,0:T(8,128)(2,1)}, u32[]{:S(2)}, u32[]{:S(2)}) collective-permute-start(bf16[256,1024]{1,0:T(8,128)(2,1)} %collective-permute-done.7.refs_7_), channel_id=1, source_target_pairs={{0,8},{4,12},{8,0},{12,4},{16,24},{20,28},{24,16},{28,20},{1,9},{5... | collective-permute-start | bytes 1572872 | tf_op jit(solution)/shard_map/ppermute | solution.py:21
  157.6 21.0 %collective-permute-start.17 = (bf16[256,1024]{1,0:T(8,128)(2,1)}, bf16[256,1024]{1,0:T(8,128)(2,1)}, u32[]{:S(2)}, u32[]{:S(2)}) collective-permute-start(bf16[256,1024]{1,0:T(8,128)(2,1)} %collective-permute-done.15.refs_15_), channel_id=1, source_target_pairs={{0,16},{4,20},{8,24},{12,28},{16,0},{20,4},{24,8},{28,12},{1,17},{... | collective-permute-start | bytes 1572872 | tf_op jit(solution)/shard_map/ppermute | solution.py:21
  159.2 23.7 %collective-permute-start.11 = (bf16[256,1024]{1,0:T(8,128)(2,1)}, bf16[256,1024]{1,0:T(8,128)(2,1)}, u32[]{:S(2)}, u32[]{:S(2)}) collective-permute-start(bf16[256,1024]{1,0:T(8,128)(2,1)} %collective-permute-done.7.refs_7_), channel_id=1, source_target_pairs={{0,4},{4,0},{8,12},{12,8},{16,20},{20,16},{24,28},{28,24},{1,5},{5... | collective-permute-start | bytes 1572872 | tf_op jit(solution)/shard_map/ppermute | solution.py:21
  159.9 16.8 %collective-permute-start.25 = (bf16[128,1024]{1,0:T(8,128)(2,1)S(1)}, bf16[128,1024]{1,0:T(8,128)(2,1)S(1)}, u32[]{:S(2)}, u32[]{:S(2)}) collective-permute-start(bf16[128,1024]{1,0:T(8,128)(2,1)S(1)} %collective-permute-done.23.refs_23_), channel_id=1, source_target_pairs={{0,16},{4,20},{8,24},{12,28},{16,0},{20,4},{24,8},{28,12},{1,17},{... | collective-permute-start | bytes 786440 | tf_op jit(solution)/shard_map/ppermute | solution.py:21
  176.7 8.8 %collective-permute-start.20 = (bf16[256,1024]{1,0:T(8,128)(2,1)}, bf16[256,1024]{1,0:T(8,128)(2,1)}, u32[]{:S(2)}, u32[]{:S(2)}) collective-permute-start(bf16[256,1024]{1,0:T(8,128)(2,1)} %collective-permute-done.16.refs_16_), channel_id=1, source_target_pairs={{0,4},{4,0},{8,12},{12,8},{16,20},{20,16},{24,28},{28,24},{1,5},{5... | collective-permute-start | bytes 1572872 | tf_op jit(solution)/shard_map/ppermute | solution.py:21
  178.2 16.9 %collective-permute-start.19 = (bf16[256,1024]{1,0:T(8,128)(2,1)}, bf16[256,1024]{1,0:T(8,128)(2,1)}, u32[]{:S(2)}, u32[]{:S(2)}) collective-permute-start(bf16[256,1024]{1,0:T(8,128)(2,1)} %collective-permute-done.15.refs_15_), channel_id=1, source_target_pairs={{0,4},{4,0},{8,12},{12,8},{16,20},{20,16},{24,28},{28,24},{1,5},{5... | collective-permute-start | bytes 1572872 | tf_op jit(solution)/shard_map/ppermute | solution.py:21
  178.2 17.6 %collective-permute-start.13 = (bf16[256,1024]{1,0:T(8,128)(2,1)}, bf16[256,1024]{1,0:T(8,128)(2,1)}, u32[]{:S(2)}, u32[]{:S(2)}) collective-permute-start(bf16[256,1024]{1,0:T(8,128)(2,1)} %collective-permute-done.9.refs_9_), channel_id=1, source_target_pairs={{0,4},{4,0},{8,12},{12,8},{16,20},{20,16},{24,28},{28,24},{1,5},{5... | collective-permute-start | bytes 1572872 | tf_op jit(solution)/shard_map/ppermute | solution.py:21
  178.7 17.1 %collective-permute-start.21 = (bf16[256,1024]{1,0:T(8,128)(2,1)}, bf16[256,1024]{1,0:T(8,128)(2,1)}, u32[]{:S(2)}, u32[]{:S(2)}) collective-permute-start(bf16[256,1024]{1,0:T(8,128)(2,1)} %collective-permute-done.17.refs_17_), channel_id=1, source_target_pairs={{0,4},{4,0},{8,12},{12,8},{16,20},{20,16},{24,28},{28,24},{1,5},{5... | collective-permute-start | bytes 1572872 | tf_op jit(solution)/shard_map/ppermute | solution.py:21
  182.9 12.2 %collective-permute-start.29 = (bf16[128,1024]{1,0:T(8,128)(2,1)}, bf16[128,1024]{1,0:T(8,128)(2,1)S(1)}, u32[]{:S(2)}, u32[]{:S(2)}) collective-permute-start(bf16[128,1024]{1,0:T(8,128)(2,1)} %copy-done.41), channel_id=1, source_target_pairs={{0,4},{4,0},{8,12},{12,8},{16,20},{20,16},{24,28},{28,24},{1,5},{5... | collective-permute-start | bytes 786440 | tf_op jit(solution)/shard_map/ppermute | solution.py:21
  185.5 34.4 %collective-permute-start.44 = (bf16[528,128]{1,0:T(8,128)(2,1)}, bf16[528,128]{1,0:T(8,128)(2,1)S(1)}, u32[]{:S(2)}, u32[]{:S(2)}) collective-permute-start(bf16[528,128]{1,0:T(8,128)(2,1)} %get-tuple-element.32), channel_id=1, source_target_pairs={{0,3},{1,0},{2,1},{3,2},{4,7},{5,4},{6,5},{7,6},{8,11},{9,8},{10,9... | collective-permute-start | bytes 405512 | tf_op jit(solution)/shard_map/ppermute | solution.py:17
  195.1 25.4 %collective-permute-start.45 = (bf16[528,128]{1,0:T(8,128)(2,1)}, bf16[528,128]{1,0:T(8,128)(2,1)}, u32[]{:S(2)}, u32[]{:S(2)}) collective-permute-start(bf16[528,128]{1,0:T(8,128)(2,1)} %get-tuple-element.33), channel_id=1, source_target_pairs={{0,2},{1,3},{2,0},{3,1},{4,6},{5,7},{6,4},{7,5},{8,10},{9,11},{10,... | collective-permute-start | bytes 405512 | tf_op jit(solution)/shard_map/ppermute | solution.py:17
  195.1 25.4 %collective-permute-start.46 = (bf16[528,128]{1,0:T(8,128)(2,1)}, bf16[528,128]{1,0:T(8,128)(2,1)}, u32[]{:S(2)}, u32[]{:S(2)}) collective-permute-start(bf16[528,128]{1,0:T(8,128)(2,1)} %get-tuple-element.34), channel_id=1, source_target_pairs={{0,1},{1,2},{2,3},{3,0},{4,5},{5,6},{6,7},{7,4},{8,9},{9,10},{10,1... | collective-permute-start | bytes 405512 | tf_op jit(solution)/shard_map/ppermute | solution.py:17
  216.0 9.7 %collective-permute-start.43 = (f32[1,512]{1,0:T(1,128)S(1)}, f32[1,512]{1,0:T(1,128)S(1)}, u32[]{:S(2)}, u32[]{:S(2)}) collective-permute-start(f32[1,512]{1,0:T(1,128)S(1)} %get-tuple-element.29), channel_id=1, source_target_pairs={{0,1},{1,2},{2,3},{3,0},{4,5},{5,6},{6,7},{7,4},{8,9},{9,10},{10,1... | collective-permute-start | bytes 6152 | tf_op jit(solution)/shard_map/ppermute | solution.py:17
  218.9 6.8 %collective-permute-start.42 = (f32[1,512]{1,0:T(1,128)S(1)}, f32[1,512]{1,0:T(1,128)S(1)}, u32[]{:S(2)}, u32[]{:S(2)}) collective-permute-start(f32[1,512]{1,0:T(1,128)S(1)} %get-tuple-element.29), channel_id=1, source_target_pairs={{0,3},{1,0},{2,1},{3,2},{4,7},{5,4},{6,5},{7,6},{8,11},{9,8},{10,9... | collective-permute-start | bytes 6152 | tf_op jit(solution)/shard_map/ppermute | solution.py:17
  219.9 5.8 %collective-permute-start.41 = (f32[1,512]{1,0:T(1,128)S(1)}, f32[1,512]{1,0:T(1,128)S(1)}, u32[]{:S(2)}, u32[]{:S(2)}) collective-permute-start(f32[1,512]{1,0:T(1,128)S(1)} %get-tuple-element.29), channel_id=1, source_target_pairs={{0,2},{1,3},{2,0},{3,1},{4,6},{5,7},{6,4},{7,5},{8,10},{9,11},{10,... | collective-permute-start | bytes 6152 | tf_op jit(solution)/shard_map/ppermute | solution.py:17
  (47 other events, 264.8 us)

commit v2 on v1

--- a/solution.py
+++ b/solution.py
@@ -406,9 +406,13 @@
     arrived_slices[last] = first_piece, second_piece
     arrived = lax.all_to_all(summed, "wide", split_axis=0, concat_axis=0, tiled=True)
     own_features = jnp.transpose(arrived, (1, 0, 2)).reshape(quarter_rows, wide_count * emb)
-    features = [own_features] + [
-        from_ahead(own_features, distance, count) for distance in range(1, count)
-    ]
+    features = {0: own_features}
+    for chain, hop in ((range(1, last + 1), 1), (range(count - 1, last, -1), count - 1)):
+        held = own_features
+        for distance in chain:
+            held = from_ahead(held, hop, count)
+            features[distance] = held
+    features = [features[distance] for distance in range(count)]
 
     sections = section_rows(
         holder_counts[0], after(miss_rows[0], own_part), miss_slots[0], slot_count
@@ -429,7 +433,7 @@
     }
     first_piece, second_piece = arrived_slices[last]
     parts[last] = spread(
-        first_piece, ((0, 0, first_height),), bits, wide_count, own_features
+        first_piece, ((0, 0, first_height),), bits[::-1], wide_count, own_features
     ) + spread(second_piece, ((1, 0, second_height),), bits[::-1], wide_count, own_features)
     own_second = lax.dynamic_slice(
         w_second,

time: 227 us -> 220 us (0.969)
  waiting for transfers between devices: 98.5 us -> 89.4 us
    ppermute x19, waiting for transfers between devices: 62.5 us -> 57.1 us  [from_ahead(): return lax.ppermute(value, 'narrow', pairs)]
    ppermute x28, starting transfers between devices: 13.4 us -> 17.6 us  [from_flipped(): lax.ppermute(value, 'wide', [(index, index ^ bit) for index in range(coun...]
    ppermute x28, waiting for transfers between devices: 36 us -> 32.4 us  [from_flipped(): lax.ppermute(value, 'wide', [(index, index ^ bit) for index in range(coun...]
    ppermute x19, starting transfers between devices: 29.8 us -> 27.2 us  [from_ahead(): return lax.ppermute(value, 'narrow', pairs)]
  transfers between devices with their start and end apart: 48 -> 48, of which waited for: 15 -> 13; matrix products, arithmetic and copies ran while one was open for 3% -> 3% of each run, Pallas kernels for 17% -> 17%
where the time goes in v2:
time: 220 us; the launch traced here: 219 us
  waiting for transfers between devices  89.4 us (41%)
  starting transfers between devices  48.8 us (22%)
  Pallas kernels  44 us (20%)
  local copies, waits for them, and re-layouts  32 us (15%)
  other arithmetic  3.57 us (2%)
    ppermute x19, waiting for transfers between devices, from_ahead(): return lax.ppermute(value, 'narrow', pairs)  57.1 us
    ppermute x28, waiting for transfers between devices, from_flipped(): lax.ppermute(value, 'wide', [(index, index ^ bit) for index in range(coun...  32.4 us
    ppermute x19, starting transfers between devices, from_ahead(): return lax.ppermute(value, 'narrow', pairs)  27.2 us
    unnamed x95, local copies, waits for them, and re-layouts  25.4 us
    pallas_call x4, Pallas kernels, pool_quarter(): pl.pallas_call(kernel, out_shape=jax.ShapeDtypeStruct((total, emb), jnp.b...  23.3 us
    ppermute x28, starting transfers between devices, from_flipped(): lax.ppermute(value, 'wide', [(index, index ^ bit) for index in range(coun...  17.6 us
    pallas_call x1, Pallas kernels, top_network(): pl.pallas_call(kernel, out_shape=(jax.ShapeDtypeStruct((rows, columns), j...  11.6 us
    pallas_call x1, Pallas kernels, place_rows(): pl.pallas_call(kernel, out_shape=jax.ShapeDtypeStruct((slot_count, emb),...  5.13 us
  transfers between devices with their start and end apart: 48, of which 13 were waited for; matrix products, arithmetic and copies ran while one was open for 3% of the time, Pallas kernels for 17%

profile of v2, /device:TPU:0, one launch (start us, length us, event | category | flops | bytes accessed | tf_op | source)
XLA Modules:
  0.0 218.8 jit_solution(12128218064869300745)
XLA Ops:
  0.6 1.5 copy.18
  2.2 1.5 reshape_squeeze.6.lookups_ref
  3.7 5.8 %pool_quarter.6 = bf16[1024,128]{1,0:T(8,128)(2,1)} custom-call(s32[8,4,8,256]{3,2,1,0:T(8,128)} %reshape_squeeze.6.lookups_ref, s32[32,128]{1,0:T(8,128)} %bitcast.30, bf16[2048,128]{1,0:T(8,128)(2,1)} %bitcast.24), custom_call_target="tpu_custom_call" | custom-call | flops 1073741824 | bytes 262144 | tf_op jit(solution)/shard_map/pool_quarter/pallas_call | solution.py:92
  9.5 4.1 %collective-permute-start.1 = (bf16[1024,128]{1,0:T(8,128)(2,1)}, bf16[1024,128]{1,0:T(8,128)(2,1)S(1)}, u32[]{:S(2)}, u32[]{:S(2)}) collective-permute-start(bf16[1024,128]{1,0:T(8,128)(2,1)} %pool_quarter.6), channel_id=1, source_target_pairs={{0,2},{1,3},{2,0},{3,1},{4,6},{5,7},{6,4},{7,5},{8,10},{9,11},{10,... | collective-permute-start | bytes 786440 | tf_op jit(solution)/shard_map/ppermute | solution.py:17
  13.6 5.8 %pool_quarter.7 = bf16[1024,128]{1,0:T(8,128)(2,1)} custom-call(s32[8,4,8,256]{3,2,1,0:T(8,128)} %reshape_squeeze.6.lookups_ref, s32[32,128]{1,0:T(8,128)} %bitcast.31, bf16[2048,128]{1,0:T(8,128)(2,1)} %bitcast.25), custom_call_target="tpu_custom_call" | custom-call | flops 1073741824 | bytes 262144 | tf_op jit(solution)/shard_map/pool_quarter/pallas_call | solution.py:92
  19.3 1.3 collective-permute-start.2
  20.7 5.8 %pool_quarter.5 = bf16[1024,128]{1,0:T(8,128)(2,1)} custom-call(s32[8,4,8,256]{3,2,1,0:T(8,128)} %reshape_squeeze.6.lookups_ref, s32[32,128]{1,0:T(8,128)} %bitcast.32, bf16[2048,128]{1,0:T(8,128)(2,1)} %bitcast.26), custom_call_target="tpu_custom_call" | custom-call | flops 1073741824 | bytes 262144 | tf_op jit(solution)/shard_map/pool_quarter/pallas_call | solution.py:92
  27.1 6.0 %pool_quarter.4 = f32[1024,128]{1,0:T(8,128)} custom-call(s32[8,4,8,256]{3,2,1,0:T(8,128)} %reshape_squeeze.6.lookups_ref, s32[32,128]{1,0:T(8,128)} %bitcast.33, bf16[2048,128]{1,0:T(8,128)(2,1)} %bitcast.27), custom_call_target="tpu_custom_call" | custom-call | flops 1073741824 | bytes 262144 | tf_op jit(solution)/shard_map/pool_quarter/pallas_call | solution.py:92
  33.1 3.8 %collective-permute-done.2 = bf16[1024,128]{1,0:T(8,128)(2,1)S(1)} collective-permute-done((bf16[1024,128]{1,0:T(8,128)(2,1)}, bf16[1024,128]{1,0:T(8,128)(2,1)S(1)}, u32[]{:S(2)}, u32[]{:S(2)}) %collective-permute-start.2) | collective-permute-done | bytes 262176 | tf_op jit(solution)/shard_map/ppermute | solution.py:17
  36.9 1.9 add_convert_fusion
  38.8 4.0 %all-to-all-start = ((bf16[8,128,128]{2,1,0:T(8,128)(2,1)}), bf16[8,128,128]{2,1,0:T(8,128)(2,1)}, u32[]{:S(2)}, u32[]{:S(2)}) async-start(bf16[8,128,128]{2,1,0:T(8,128)(2,1)} %bitcast.2), calls=%async_computation | async-start | bytes 524288 | tf_op jit(solution)/shard_map/all_to_all | solution.py:407
  42.9 1.9 fusion
  44.8 1.1 pad_maximum_fusion
  45.9 3.5 %collective-permute-start.6 = (bf16[256,1024]{1,0:T(8,128)(2,1)}, bf16[256,1024]{1,0:T(8,128)(2,1)S(1)}, u32[]{:S(2)}, u32[]{:S(2)}) collective-permute-start(bf16[256,1024]{1,0:T(8,128)(2,1)} %get-tuple-element.39), channel_id=1, source_target_pairs={{0,3},{1,0},{2,1},{3,2},{4,7},{5,4},{6,5},{7,6},{8,11},{9,8},{10,9... | collective-permute-start | bytes 1572872 | tf_op jit(solution)/shard_map/ppermute | solution.py:17
  49.4 1.2 collective-permute-start.14
  50.6 1.0 copy_bitcast_fusion.refs_0_
  51.6 32.2 %collective-permute-done.30.refs_30_ = bf16[128,1024]{1,0:T(8,128)(2,1)} collective-permute-done((bf16[128,1024]{1,0:T(8,128)(2,1)}, bf16[128,1024]{1,0:T(8,128)(2,1)}, u32[]{:S(2)}, u32[]{:S(2)}) %collective-permute-start.30) | collective-permute-done | bytes 262176 | tf_op jit(solution)/shard_map/ppermute | solution.py:17
  83.8 1.6 collective-permute-start.32
  85.5 5.4 %collective-permute-done.40 = f32[1024]{0:T(1024)S(1)} collective-permute-done((f32[1024]{0:T(1024)S(1)}, f32[1024]{0:T(1024)S(1)}, u32[]{:S(2)}, u32[]{:S(2)}) %collective-permute-start.40) | collective-permute-done | bytes 4128 | tf_op jit(solution)/shard_map/ppermute | solution.py:17
  90.9 4.5 %collective-permute-done.39 = f32[1024]{0:T(1024)S(1)} collective-permute-done((f32[1024]{0:T(1024)S(1)}, f32[1024]{0:T(1024)S(1)}, u32[]{:S(2)}, u32[]{:S(2)}) %collective-permute-start.39) | collective-permute-done | bytes 4128 | tf_op jit(solution)/shard_map/ppermute | solution.py:17
  95.4 1.5 collective-permute-start.31
  96.9 2.1 collective-permute-done.38
  99.0 3.8 %collective-permute-start.3 = (bf16[128,1024]{1,0:T(8,128)(2,1)S(1)}, bf16[128,1024]{1,0:T(8,128)(2,1)S(1)}, u32[]{:S(2)}, u32[]{:S(2)}) collective-permute-start(bf16[128,1024]{1,0:T(8,128)(2,1)S(1)} %copy_bitcast_fusion.refs_0_), channel_id=1, source_target_pairs={{0,3},{1,0},{2,1},{3,2},{4,7},{5,4},{6,5},{7,6},{8,11},{9,8},{10,9... | collective-permute-start | bytes 786440 | tf_op jit(solution)/shard_map/ppermute | solution.py:17
  104.8 5.2 %collective-permute-done.5.refs_3_ = bf16[128,1024]{1,0:T(8,128)(2,1)S(1)} collective-permute-done((bf16[128,1024]{1,0:T(8,128)(2,1)S(1)}, bf16[128,1024]{1,0:T(8,128)(2,1)S(1)}, u32[]{:S(2)}, u32[]{:S(2)}) %collective-permute-start.5) | collective-permute-done | bytes 262176 | tf_op jit(solution)/shard_map/ppermute | solution.py:17
  111.8 3.7 %collective-permute-done.22.refs_22_ = bf16[128,1024]{1,0:T(8,128)(2,1)S(1)} collective-permute-done((bf16[128,1024]{1,0:T(8,128)(2,1)S(1)}, bf16[128,1024]{1,0:T(8,128)(2,1)S(1)}, u32[]{:S(2)}, u32[]{:S(2)}) %collective-permute-start.22) | collective-permute-done | bytes 262176 | tf_op jit(solution)/shard_map/ppermute | solution.py:17
  115.5 4.2 %collective-permute-start.4 = (bf16[128,1024]{1,0:T(8,128)(2,1)S(1)}, bf16[128,1024]{1,0:T(8,128)(2,1)S(1)}, u32[]{:S(2)}, u32[]{:S(2)}) collective-permute-start(bf16[128,1024]{1,0:T(8,128)(2,1)S(1)} %collective-permute-done.3.refs_1_), channel_id=1, source_target_pairs={{0,3},{1,0},{2,1},{3,2},{4,7},{5,4},{6,5},{7,6},{8,11},{9,8},{10,9... | collective-permute-start | bytes 786440 | tf_op jit(solution)/shard_map/ppermute | solution.py:17
  122.0 1.6 collective-permute-start.24
  123.7 1.5 collective-permute-start.23
  126.6 1.6 collective-permute-start.8
  129.0 1.5 collective-permute-start.7
  131.2 1.6 collective-permute-done.23.refs_23_
  132.8 1.5 collective-permute-start.16
  135.7 6.8 %collective-permute-done.8.refs_8_ = bf16[256,1024]{1,0:T(8,128)(2,1)S(1)} collective-permute-done((bf16[256,1024]{1,0:T(8,128)(2,1)S(1)}, bf16[256,1024]{1,0:T(8,128)(2,1)S(1)}, u32[]{:S(2)}, u32[]{:S(2)}) %collective-permute-start.8) | collective-permute-done | bytes 524320 | tf_op jit(solution)/shard_map/ppermute | solution.py:21
  143.1 1.0 collective-permute-done.7.refs_7_
  146.2 8.3 %collective-permute-done.16.refs_16_ = bf16[256,1024]{1,0:T(8,128)(2,1)} collective-permute-done((bf16[256,1024]{1,0:T(8,128)(2,1)S(1)}, bf16[256,1024]{1,0:T(8,128)(2,1)}, u32[]{:S(2)}, u32[]{:S(2)}) %collective-permute-start.16) | collective-permute-done | bytes 524320 | tf_op jit(solution)/shard_map/ppermute | solution.py:21
  156.4 1.6 collective-permute-start.17
  159.5 1.5 collective-permute-start.25
  161.6 13.8 %collective-permute-done.25.refs_25_ = bf16[128,1024]{1,0:T(8,128)(2,1)S(1)} collective-permute-done((bf16[128,1024]{1,0:T(8,128)(2,1)S(1)}, bf16[128,1024]{1,0:T(8,128)(2,1)S(1)}, u32[]{:S(2)}, u32[]{:S(2)}) %collective-permute-start.25) | collective-permute-done | bytes 262176 | tf_op jit(solution)/shard_map/ppermute | solution.py:21
  177.5 4.0 %section_rows.1 = (bf16[528,128]{1,0:T(8,128)(2,1)}, bf16[528,128]{1,0:T(8,128)(2,1)}, bf16[528,128]{1,0:T(8,128)(2,1)}, bf16[528,128]{1,0:T(8,128)(2,1)}) custom-call(s32[4]{0:T(128)} %bitcast.34, bf16[1024,128]{1,0:T(8,128)(2,1)} %bitcast.29, s32[1,1024]{1,0:T(1,128)} %slots_ref.1), custom_call_target="tpu_custom_call" | custom-call | flops 536870912 | bytes 524288 | tf_op jit(solution)/shard_map/section_rows/pallas_call | solution.py:138
  182.2 2.1 constant_dynamic-slice_fusion.1.refs_5_
  184.3 3.3 %collective-permute-start.44 = (bf16[528,128]{1,0:T(8,128)(2,1)}, bf16[528,128]{1,0:T(8,128)(2,1)S(1)}, u32[]{:S(2)}, u32[]{:S(2)}) collective-permute-start(bf16[528,128]{1,0:T(8,128)(2,1)} %get-tuple-element.32), channel_id=1, source_target_pairs={{0,3},{1,0},{2,1},{3,2},{4,7},{5,4},{6,5},{7,6},{8,11},{9,8},{10,9... | collective-permute-start | bytes 405512 | tf_op jit(solution)/shard_map/ppermute | solution.py:17
  190.3 0.9 copy-done.30
  191.3 0.9 copy-done.32
  192.2 0.9 copy-done.34
  197.0 11.6 %top_network.1 = (bf16[512,1024]{1,0:T(8,128)(2,1)}, f32[1,512]{1,0:T(1,128)S(1)}) custom-call(bf16[128,1024]{1,0:T(8,128)(2,1)S(1)} %copy_bitcast_fusion.refs_0_, bf16[128,1024]{1,0:T(8,128)(2,1)S(1)} %copy-done.18, bf16[128,1024]{1,0:T(8,128)(2,1)S(1)} %copy-done.28, bf16[128,1024]{1,0:T(8,128)(2,1)S(1)} %copy-done.16, bf16[1024,1024]{1,0:T(8,128)(2,1)S(1)} %copy-done, ...), custom_call_target="tpu_custom_call" | custom-call | flops 8589934592 | bytes 16777216 | tf_op jit(solution)/shard_map/top_network/pallas_call | solution.py:280
  208.5 2.9 %collective-permute-start.43 = (f32[1,512]{1,0:T(1,128)S(1)}, f32[1,512]{1,0:T(1,128)S(1)}, u32[]{:S(2)}, u32[]{:S(2)}) collective-permute-start(f32[1,512]{1,0:T(1,128)S(1)} %get-tuple-element.29), channel_id=1, source_target_pairs={{0,1},{1,2},{2,3},{3,0},{4,5},{5,6},{6,7},{7,4},{8,9},{9,10},{10,1... | collective-permute-start | bytes 6152 | tf_op jit(solution)/shard_map/ppermute | solution.py:17
  211.4 1.0 collective-permute-start.42
  213.1 5.1 %place_rows.1 = bf16[2048,128]{1,0:T(8,128)(2,1)} custom-call(bf16[528,128]{1,0:T(8,128)(2,1)} %get-tuple-element.31.refs_0_, bf16[528,128]{1,0:T(8,128)(2,1)} %copy-done.46, bf16[528,128]{1,0:T(8,128)(2,1)} %collective-permute-done.45.refs_2_, bf16[528,128]{1,0:T(8,128)(2,1)} %collective-permute-done.46.refs_3_, bf16[2048,128]{1,0:T(8,128)(2,1)} %bitcast.28), custom_call_target="tpu_custom_call" | custom-call | flops 2147483648 | bytes 1048576 | tf_op jit(solution)/shard_map/place_rows/pallas_call | solution.py:187
  (160 shorter events, 28.1 us)
Async XLA Ops:
  9.5 23.6 %collective-permute-start.1 = (bf16[1024,128]{1,0:T(8,128)(2,1)}, bf16[1024,128]{1,0:T(8,128)(2,1)S(1)}, u32[]{:S(2)}, u32[]{:S(2)}) collective-permute-start(bf16[1024,128]{1,0:T(8,128)(2,1)} %pool_quarter.6), channel_id=1, source_target_pairs={{0,2},{1,3},{2,0},{3,1},{4,6},{5,7},{6,4},{7,5},{8,10},{9,11},{10,... | collective-permute-start | bytes 786440 | tf_op jit(solution)/shard_map/ppermute | solution.py:17
  19.3 17.6 %collective-permute-start.2 = (bf16[1024,128]{1,0:T(8,128)(2,1)}, bf16[1024,128]{1,0:T(8,128)(2,1)S(1)}, u32[]{:S(2)}, u32[]{:S(2)}) collective-permute-start(bf16[1024,128]{1,0:T(8,128)(2,1)} %pool_quarter.7), channel_id=1, source_target_pairs={{0,3},{1,0},{2,1},{3,2},{4,7},{5,4},{6,5},{7,6},{8,11},{9,8},{10,9... | collective-permute-start | bytes 786440 | tf_op jit(solution)/shard_map/ppermute | solution.py:17
  26.4 10.5 %collective-permute-start = (bf16[1024,128]{1,0:T(8,128)(2,1)}, bf16[1024,128]{1,0:T(8,128)(2,1)S(1)}, u32[]{:S(2)}, u32[]{:S(2)}) collective-permute-start(bf16[1024,128]{1,0:T(8,128)(2,1)} %pool_quarter.5), channel_id=1, source_target_pairs={{0,1},{1,2},{2,3},{3,0},{4,5},{5,6},{6,7},{7,4},{8,9},{9,10},{10,1... | collective-permute-start | bytes 786440 | tf_op jit(solution)/shard_map/ppermute | solution.py:17
  38.8 11.8 %all-to-all-start = ((bf16[8,128,128]{2,1,0:T(8,128)(2,1)}), bf16[8,128,128]{2,1,0:T(8,128)(2,1)}, u32[]{:S(2)}, u32[]{:S(2)}) async-start(bf16[8,128,128]{2,1,0:T(8,128)(2,1)} %bitcast.2), calls=%async_computation | async-start | bytes 524288 | tf_op jit(solution)/shard_map/all_to_all | solution.py:407
  45.9 49.5 %collective-permute-start.6 = (bf16[256,1024]{1,0:T(8,128)(2,1)}, bf16[256,1024]{1,0:T(8,128)(2,1)S(1)}, u32[]{:S(2)}, u32[]{:S(2)}) collective-permute-start(bf16[256,1024]{1,0:T(8,128)(2,1)} %get-tuple-element.39), channel_id=1, source_target_pairs={{0,3},{1,0},{2,1},{3,2},{4,7},{5,4},{6,5},{7,6},{8,11},{9,8},{10,9... | collective-permute-start | bytes 1572872 | tf_op jit(solution)/shard_map/ppermute | solution.py:17
  49.4 34.4 %collective-permute-start.30 = (bf16[128,1024]{1,0:T(8,128)(2,1)}, bf16[128,1024]{1,0:T(8,128)(2,1)}, u32[]{:S(2)}, u32[]{:S(2)}) collective-permute-start(bf16[128,1024]{1,0:T(8,128)(2,1)} %get-tuple-element.25), channel_id=1, source_target_pairs={{0,2},{1,3},{2,0},{3,1},{4,6},{5,7},{6,4},{7,5},{8,10},{9,11},{10,... | collective-permute-start | bytes 786440 | tf_op jit(solution)/shard_map/ppermute | solution.py:17
  49.4 49.6 %collective-permute-start.14 = (bf16[256,1024]{1,0:T(8,128)(2,1)}, bf16[256,1024]{1,0:T(8,128)(2,1)S(1)}, u32[]{:S(2)}, u32[]{:S(2)}) collective-permute-start(bf16[256,1024]{1,0:T(8,128)(2,1)} %get-tuple-element.21), channel_id=1, source_target_pairs={{0,1},{1,2},{2,3},{3,0},{4,5},{5,6},{6,7},{7,4},{8,9},{9,10},{10,1... | collective-permute-start | bytes 1572872 | tf_op jit(solution)/shard_map/ppermute | solution.py:17
  83.8 19.0 %collective-permute-start.34 = (bf16[128,1024]{1,0:T(8,128)(2,1)}, bf16[128,1024]{1,0:T(8,128)(2,1)S(1)}, u32[]{:S(2)}, u32[]{:S(2)}) collective-permute-start(bf16[128,1024]{1,0:T(8,128)(2,1)} %collective-permute-done.30.refs_30_), channel_id=1, source_target_pairs={{0,4},{4,0},{8,12},{12,8},{16,20},{20,16},{24,28},{28,24},{1,5},{5... | collective-permute-start | bytes 786440 | tf_op jit(solution)/shard_map/ppermute | solution.py:21
  83.8 19.8 %collective-permute-start.32 = (bf16[128,1024]{1,0:T(8,128)(2,1)}, bf16[128,1024]{1,0:T(8,128)(2,1)S(1)}, u32[]{:S(2)}, u32[]{:S(2)}) collective-permute-start(bf16[128,1024]{1,0:T(8,128)(2,1)} %collective-permute-done.30.refs_30_), channel_id=1, source_target_pairs={{0,8},{4,12},{8,0},{12,4},{16,24},{20,28},{24,16},{28,20},{1,9},{5... | collective-permute-start | bytes 786440 | tf_op jit(solution)/shard_map/ppermute | solution.py:21
  85.4 5.4 %collective-permute-start.40 = (f32[1024]{0:T(1024)S(1)}, f32[1024]{0:T(1024)S(1)}, u32[]{:S(2)}, u32[]{:S(2)}) collective-permute-start(f32[1024]{0:T(1024)S(1)} %copy-done.44), channel_id=1, source_target_pairs={{0,1},{1,2},{2,3},{3,0},{4,5},{5,6},{6,7},{7,4},{8,9},{9,10},{10,1... | collective-permute-start | bytes 12296 | tf_op jit(solution)/shard_map/ppermute | solution.py:17
  90.9 4.5 %collective-permute-start.39 = (f32[1024]{0:T(1024)S(1)}, f32[1024]{0:T(1024)S(1)}, u32[]{:S(2)}, u32[]{:S(2)}) collective-permute-start(f32[1024]{0:T(1024)S(1)} %copy-done.44), channel_id=1, source_target_pairs={{0,2},{1,3},{2,0},{3,1},{4,6},{5,7},{6,4},{7,5},{8,10},{9,11},{10,... | collective-permute-start | bytes 12296 | tf_op jit(solution)/shard_map/ppermute | solution.py:17
  95.4 3.6 %collective-permute-start.38 = (f32[1024]{0:T(1024)S(1)}, f32[1024]{0:T(1024)S(1)}, u32[]{:S(2)}, u32[]{:S(2)}) collective-permute-start(f32[1024]{0:T(1024)S(1)} %copy-done.44), channel_id=1, source_target_pairs={{0,3},{1,0},{2,1},{3,2},{4,7},{5,4},{6,5},{7,6},{8,11},{9,8},{10,9... | collective-permute-start | bytes 12296 | tf_op jit(solution)/shard_map/ppermute | solution.py:17
  95.4 8.9 %collective-permute-start.31 = (bf16[128,1024]{1,0:T(8,128)(2,1)}, bf16[128,1024]{1,0:T(8,128)(2,1)S(1)}, u32[]{:S(2)}, u32[]{:S(2)}) collective-permute-start(bf16[128,1024]{1,0:T(8,128)(2,1)} %collective-permute-done.30.refs_30_), channel_id=1, source_target_pairs={{0,16},{4,20},{8,24},{12,28},{16,0},{20,4},{24,8},{28,12},{1,17},{... | collective-permute-start | bytes 786440 | tf_op jit(solution)/shard_map/ppermute | solution.py:21
  99.0 11.0 %collective-permute-start.5 = (bf16[128,1024]{1,0:T(8,128)(2,1)S(1)}, bf16[128,1024]{1,0:T(8,128)(2,1)S(1)}, u32[]{:S(2)}, u32[]{:S(2)}) collective-permute-start(bf16[128,1024]{1,0:T(8,128)(2,1)S(1)} %copy_bitcast_fusion.refs_0_), channel_id=1, source_target_pairs={{0,1},{1,2},{2,3},{3,0},{4,5},{5,6},{6,7},{7,4},{8,9},{9,10},{10,1... | collective-permute-start | bytes 786440 | tf_op jit(solution)/shard_map/ppermute | solution.py:17
  99.0 12.8 %collective-permute-start.3 = (bf16[128,1024]{1,0:T(8,128)(2,1)S(1)}, bf16[128,1024]{1,0:T(8,128)(2,1)S(1)}, u32[]{:S(2)}, u32[]{:S(2)}) collective-permute-start(bf16[128,1024]{1,0:T(8,128)(2,1)S(1)} %copy_bitcast_fusion.refs_0_), channel_id=1, source_target_pairs={{0,3},{1,0},{2,1},{3,2},{4,7},{5,4},{6,5},{7,6},{8,11},{9,8},{10,9... | collective-permute-start | bytes 786440 | tf_op jit(solution)/shard_map/ppermute | solution.py:17
  103.5 12.0 %collective-permute-start.22 = (bf16[128,1024]{1,0:T(8,128)(2,1)S(1)}, bf16[128,1024]{1,0:T(8,128)(2,1)S(1)}, u32[]{:S(2)}, u32[]{:S(2)}) collective-permute-start(bf16[128,1024]{1,0:T(8,128)(2,1)S(1)} %slice.4), channel_id=1, source_target_pairs={{0,3},{1,0},{2,1},{3,2},{4,7},{5,4},{6,5},{7,6},{8,11},{9,8},{10,9... | collective-permute-start | bytes 786440 | tf_op jit(solution)/shard_map/ppermute | solution.py:17
  103.6 16.8 %collective-permute-start.36 = (bf16[128,1024]{1,0:T(8,128)(2,1)S(1)}, bf16[128,1024]{1,0:T(8,128)(2,1)S(1)}, u32[]{:S(2)}, u32[]{:S(2)}) collective-permute-start(bf16[128,1024]{1,0:T(8,128)(2,1)S(1)} %collective-permute-done.32.refs_32_), channel_id=1, source_target_pairs={{0,4},{4,0},{8,12},{12,8},{16,20},{20,16},{24,28},{28,24},{1,5},{5... | collective-permute-start | bytes 786440 | tf_op jit(solution)/shard_map/ppermute | solution.py:21
  104.3 17.0 %collective-permute-start.35 = (bf16[128,1024]{1,0:T(8,128)(2,1)S(1)}, bf16[128,1024]{1,0:T(8,128)(2,1)S(1)}, u32[]{:S(2)}, u32[]{:S(2)}) collective-permute-start(bf16[128,1024]{1,0:T(8,128)(2,1)S(1)} %collective-permute-done.31.refs_31_), channel_id=1, source_target_pairs={{0,4},{4,0},{8,12},{12,8},{16,20},{20,16},{24,28},{28,24},{1,5},{5... | collective-permute-start | bytes 786440 | tf_op jit(solution)/shard_map/ppermute | solution.py:21
  110.7 13.0 %collective-permute-start.33 = (bf16[128,1024]{1,0:T(8,128)(2,1)S(1)}, bf16[128,1024]{1,0:T(8,128)(2,1)S(1)}, u32[]{:S(2)}, u32[]{:S(2)}) collective-permute-start(bf16[128,1024]{1,0:T(8,128)(2,1)S(1)} %collective-permute-done.31.refs_31_), channel_id=1, source_target_pairs={{0,8},{4,12},{8,0},{12,4},{16,24},{20,28},{24,16},{28,20},{1,9},{5... | collective-permute-start | bytes 786440 | tf_op jit(solution)/shard_map/ppermute | solution.py:21
  111.8 22.5 %collective-permute-start.10 = (bf16[256,1024]{1,0:T(8,128)(2,1)S(1)}, bf16[256,1024]{1,0:T(8,128)(2,1)S(1)}, u32[]{:S(2)}, u32[]{:S(2)}) collective-permute-start(bf16[256,1024]{1,0:T(8,128)(2,1)S(1)} %collective-permute-done.6.refs_6_), channel_id=1, source_target_pairs={{0,4},{4,0},{8,12},{12,8},{16,20},{20,16},{24,28},{28,24},{1,5},{5... | collective-permute-start | bytes 1572872 | tf_op jit(solution)/shard_map/ppermute | solution.py:21
  115.5 10.4 %collective-permute-start.4 = (bf16[128,1024]{1,0:T(8,128)(2,1)S(1)}, bf16[128,1024]{1,0:T(8,128)(2,1)S(1)}, u32[]{:S(2)}, u32[]{:S(2)}) collective-permute-start(bf16[128,1024]{1,0:T(8,128)(2,1)S(1)} %collective-permute-done.3.refs_1_), channel_id=1, source_target_pairs={{0,3},{1,0},{2,1},{3,2},{4,7},{5,4},{6,5},{7,6},{8,11},{9,8},{10,9... | collective-permute-start | bytes 786440 | tf_op jit(solution)/shard_map/ppermute | solution.py:17
  121.1 7.1 %collective-permute-start.26 = (bf16[128,1024]{1,0:T(8,128)(2,1)S(1)}, bf16[128,1024]{1,0:T(8,128)(2,1)S(1)}, u32[]{:S(2)}, u32[]{:S(2)}) collective-permute-start(bf16[128,1024]{1,0:T(8,128)(2,1)S(1)} %collective-permute-done.22.refs_22_), channel_id=1, source_target_pairs={{0,4},{4,0},{8,12},{12,8},{16,20},{20,16},{24,28},{28,24},{1,5},{5... | collective-permute-start | bytes 786440 | tf_op jit(solution)/shard_map/ppermute | solution.py:21
  122.0 9.2 %collective-permute-start.24 = (bf16[128,1024]{1,0:T(8,128)(2,1)S(1)}, bf16[128,1024]{1,0:T(8,128)(2,1)S(1)}, u32[]{:S(2)}, u32[]{:S(2)}) collective-permute-start(bf16[128,1024]{1,0:T(8,128)(2,1)S(1)} %collective-permute-done.22.refs_22_), channel_id=1, source_target_pairs={{0,8},{4,12},{8,0},{12,4},{16,24},{20,28},{24,16},{28,20},{1,9},{5... | collective-permute-start | bytes 786440 | tf_op jit(solution)/shard_map/ppermute | solution.py:21
  123.7 9.2 %collective-permute-start.23 = (bf16[128,1024]{1,0:T(8,128)(2,1)S(1)}, bf16[128,1024]{1,0:T(8,128)(2,1)S(1)}, u32[]{:S(2)}, u32[]{:S(2)}) collective-permute-start(bf16[128,1024]{1,0:T(8,128)(2,1)S(1)} %collective-permute-done.22.refs_22_), channel_id=1, source_target_pairs={{0,16},{4,20},{8,24},{12,28},{16,0},{20,4},{24,8},{28,12},{1,17},{... | collective-permute-start | bytes 786440 | tf_op jit(solution)/shard_map/ppermute | solution.py:21
  126.6 15.8 %collective-permute-start.8 = (bf16[256,1024]{1,0:T(8,128)(2,1)S(1)}, bf16[256,1024]{1,0:T(8,128)(2,1)S(1)}, u32[]{:S(2)}, u32[]{:S(2)}) collective-permute-start(bf16[256,1024]{1,0:T(8,128)(2,1)S(1)} %collective-permute-done.6.refs_6_), channel_id=1, source_target_pairs={{0,8},{4,12},{8,0},{12,4},{16,24},{20,28},{24,16},{28,20},{1,9},{5... | collective-permute-start | bytes 1572872 | tf_op jit(solution)/shard_map/ppermute | solution.py:21
  129.0 15.2 %collective-permute-start.7 = (bf16[256,1024]{1,0:T(8,128)(2,1)S(1)}, bf16[256,1024]{1,0:T(8,128)(2,1)}, u32[]{:S(2)}, u32[]{:S(2)}) collective-permute-start(bf16[256,1024]{1,0:T(8,128)(2,1)S(1)} %collective-permute-done.6.refs_6_), channel_id=1, source_target_pairs={{0,16},{4,20},{8,24},{12,28},{16,0},{20,4},{24,8},{28,12},{1,17},{... | collective-permute-start | bytes 1572872 | tf_op jit(solution)/shard_map/ppermute | solution.py:21
  131.2 13.7 %collective-permute-start.18 = (bf16[256,1024]{1,0:T(8,128)(2,1)S(1)}, bf16[256,1024]{1,0:T(8,128)(2,1)S(1)}, u32[]{:S(2)}, u32[]{:S(2)}) collective-permute-start(bf16[256,1024]{1,0:T(8,128)(2,1)S(1)} %collective-permute-done.14.refs_14_), channel_id=1, source_target_pairs={{0,4},{4,0},{8,12},{12,8},{16,20},{20,16},{24,28},{28,24},{1,5},{5... | collective-permute-start | bytes 1572872 | tf_op jit(solution)/shard_map/ppermute | solution.py:21
  132.8 21.7 %collective-permute-start.16 = (bf16[256,1024]{1,0:T(8,128)(2,1)S(1)}, bf16[256,1024]{1,0:T(8,128)(2,1)}, u32[]{:S(2)}, u32[]{:S(2)}) collective-permute-start(bf16[256,1024]{1,0:T(8,128)(2,1)S(1)} %collective-permute-done.14.refs_14_), channel_id=1, source_target_pairs={{0,16},{4,20},{8,24},{12,28},{16,0},{20,4},{24,8},{28,12},{1,17},{... | collective-permute-start | bytes 1572872 | tf_op jit(solution)/shard_map/ppermute | solution.py:21
  135.1 20.2 %collective-permute-start.15 = (bf16[256,1024]{1,0:T(8,128)(2,1)S(1)}, bf16[256,1024]{1,0:T(8,128)(2,1)}, u32[]{:S(2)}, u32[]{:S(2)}) collective-permute-start(bf16[256,1024]{1,0:T(8,128)(2,1)S(1)} %collective-permute-done.14.refs_14_), channel_id=1, source_target_pairs={{0,8},{4,12},{8,0},{12,4},{16,24},{20,28},{24,16},{28,20},{1,9},{5... | collective-permute-start | bytes 1572872 | tf_op jit(solution)/shard_map/ppermute | solution.py:21
  142.4 13.3 %collective-permute-start.37 = (bf16[128,1024]{1,0:T(8,128)(2,1)S(1)}, bf16[128,1024]{1,0:T(8,128)(2,1)S(1)}, u32[]{:S(2)}, u32[]{:S(2)}) collective-permute-start(bf16[128,1024]{1,0:T(8,128)(2,1)S(1)} %collective-permute-done.33.refs_33_), channel_id=1, source_target_pairs={{0,4},{4,0},{8,12},{12,8},{16,20},{20,16},{24,28},{28,24},{1,5},{5... | collective-permute-start | bytes 786440 | tf_op jit(solution)/shard_map/ppermute | solution.py:21
  144.2 13.9 %collective-permute-start.28 = (bf16[128,1024]{1,0:T(8,128)(2,1)S(1)}, bf16[128,1024]{1,0:T(8,128)(2,1)S(1)}, u32[]{:S(2)}, u32[]{:S(2)}) collective-permute-start(bf16[128,1024]{1,0:T(8,128)(2,1)S(1)} %collective-permute-done.24.refs_24_), channel_id=1, source_target_pairs={{0,4},{4,0},{8,12},{12,8},{16,20},{20,16},{24,28},{28,24},{1,5},{5... | collective-permute-start | bytes 786440 | tf_op jit(solution)/shard_map/ppermute | solution.py:21
  145.7 13.1 %collective-permute-start.27 = (bf16[128,1024]{1,0:T(8,128)(2,1)S(1)}, bf16[128,1024]{1,0:T(8,128)(2,1)S(1)}, u32[]{:S(2)}, u32[]{:S(2)}) collective-permute-start(bf16[128,1024]{1,0:T(8,128)(2,1)S(1)} %collective-permute-done.23.refs_23_), channel_id=1, source_target_pairs={{0,4},{4,0},{8,12},{12,8},{16,20},{20,16},{24,28},{28,24},{1,5},{5... | collective-permute-start | bytes 786440 | tf_op jit(solution)/shard_map/ppermute | solution.py:21
  154.5 21.0 %collective-permute-start.12 = (bf16[256,1024]{1,0:T(8,128)(2,1)S(1)}, bf16[256,1024]{1,0:T(8,128)(2,1)S(1)}, u32[]{:S(2)}, u32[]{:S(2)}) collective-permute-start(bf16[256,1024]{1,0:T(8,128)(2,1)S(1)} %collective-permute-done.8.refs_8_), channel_id=1, source_target_pairs={{0,4},{4,0},{8,12},{12,8},{16,20},{20,16},{24,28},{28,24},{1,5},{5... | collective-permute-start | bytes 1572872 | tf_op jit(solution)/shard_map/ppermute | solution.py:21
  155.3 21.7 %collective-permute-start.9 = (bf16[256,1024]{1,0:T(8,128)(2,1)}, bf16[256,1024]{1,0:T(8,128)(2,1)}, u32[]{:S(2)}, u32[]{:S(2)}) collective-permute-start(bf16[256,1024]{1,0:T(8,128)(2,1)} %collective-permute-done.7.refs_7_), channel_id=1, source_target_pairs={{0,8},{4,12},{8,0},{12,4},{16,24},{20,28},{24,16},{28,20},{1,9},{5... | collective-permute-start | bytes 1572872 | tf_op jit(solution)/shard_map/ppermute | solution.py:21
  156.4 21.1 %collective-permute-start.17 = (bf16[256,1024]{1,0:T(8,128)(2,1)}, bf16[256,1024]{1,0:T(8,128)(2,1)}, u32[]{:S(2)}, u32[]{:S(2)}) collective-permute-start(bf16[256,1024]{1,0:T(8,128)(2,1)} %collective-permute-done.15.refs_15_), channel_id=1, source_target_pairs={{0,16},{4,20},{8,24},{12,28},{16,0},{20,4},{24,8},{28,12},{1,17},{... | collective-permute-start | bytes 1572872 | tf_op jit(solution)/shard_map/ppermute | solution.py:21
  158.8 22.9 %collective-permute-start.11 = (bf16[256,1024]{1,0:T(8,128)(2,1)}, bf16[256,1024]{1,0:T(8,128)(2,1)}, u32[]{:S(2)}, u32[]{:S(2)}) collective-permute-start(bf16[256,1024]{1,0:T(8,128)(2,1)} %collective-permute-done.7.refs_7_), channel_id=1, source_target_pairs={{0,4},{4,0},{8,12},{12,8},{16,20},{20,16},{24,28},{28,24},{1,5},{5... | collective-permute-start | bytes 1572872 | tf_op jit(solution)/shard_map/ppermute | solution.py:21
  159.5 16.0 %collective-permute-start.25 = (bf16[128,1024]{1,0:T(8,128)(2,1)S(1)}, bf16[128,1024]{1,0:T(8,128)(2,1)S(1)}, u32[]{:S(2)}, u32[]{:S(2)}) collective-permute-start(bf16[128,1024]{1,0:T(8,128)(2,1)S(1)} %collective-permute-done.23.refs_23_), channel_id=1, source_target_pairs={{0,8},{4,12},{8,0},{12,4},{16,24},{20,28},{24,16},{28,20},{1,9},{5... | collective-permute-start | bytes 786440 | tf_op jit(solution)/shard_map/ppermute | solution.py:21
  175.5 8.8 %collective-permute-start.20 = (bf16[256,1024]{1,0:T(8,128)(2,1)}, bf16[256,1024]{1,0:T(8,128)(2,1)}, u32[]{:S(2)}, u32[]{:S(2)}) collective-permute-start(bf16[256,1024]{1,0:T(8,128)(2,1)} %collective-permute-done.16.refs_16_), channel_id=1, source_target_pairs={{0,4},{4,0},{8,12},{12,8},{16,20},{20,16},{24,28},{28,24},{1,5},{5... | collective-permute-start | bytes 1572872 | tf_op jit(solution)/shard_map/ppermute | solution.py:21
  177.0 10.7 %collective-permute-start.19 = (bf16[256,1024]{1,0:T(8,128)(2,1)}, bf16[256,1024]{1,0:T(8,128)(2,1)}, u32[]{:S(2)}, u32[]{:S(2)}) collective-permute-start(bf16[256,1024]{1,0:T(8,128)(2,1)} %collective-permute-done.15.refs_15_), channel_id=1, source_target_pairs={{0,4},{4,0},{8,12},{12,8},{16,20},{20,16},{24,28},{28,24},{1,5},{5... | collective-permute-start | bytes 1572872 | tf_op jit(solution)/shard_map/ppermute | solution.py:21
  177.0 11.3 %collective-permute-start.13 = (bf16[256,1024]{1,0:T(8,128)(2,1)}, bf16[256,1024]{1,0:T(8,128)(2,1)}, u32[]{:S(2)}, u32[]{:S(2)}) collective-permute-start(bf16[256,1024]{1,0:T(8,128)(2,1)} %collective-permute-done.9.refs_9_), channel_id=1, source_target_pairs={{0,4},{4,0},{8,12},{12,8},{16,20},{20,16},{24,28},{28,24},{1,5},{5... | collective-permute-start | bytes 1572872 | tf_op jit(solution)/shard_map/ppermute | solution.py:21
  177.5 10.8 %collective-permute-start.21 = (bf16[256,1024]{1,0:T(8,128)(2,1)}, bf16[256,1024]{1,0:T(8,128)(2,1)}, u32[]{:S(2)}, u32[]{:S(2)}) collective-permute-start(bf16[256,1024]{1,0:T(8,128)(2,1)} %collective-permute-done.17.refs_17_), channel_id=1, source_target_pairs={{0,4},{4,0},{8,12},{12,8},{16,20},{20,16},{24,28},{28,24},{1,5},{5... | collective-permute-start | bytes 1572872 | tf_op jit(solution)/shard_map/ppermute | solution.py:21
  181.7 5.9 %collective-permute-start.29 = (bf16[128,1024]{1,0:T(8,128)(2,1)}, bf16[128,1024]{1,0:T(8,128)(2,1)S(1)}, u32[]{:S(2)}, u32[]{:S(2)}) collective-permute-start(bf16[128,1024]{1,0:T(8,128)(2,1)} %copy-done.41), channel_id=1, source_target_pairs={{0,4},{4,0},{8,12},{12,8},{16,20},{20,16},{24,28},{28,24},{1,5},{5... | collective-permute-start | bytes 786440 | tf_op jit(solution)/shard_map/ppermute | solution.py:21
  184.3 28.1 %collective-permute-start.44 = (bf16[528,128]{1,0:T(8,128)(2,1)}, bf16[528,128]{1,0:T(8,128)(2,1)S(1)}, u32[]{:S(2)}, u32[]{:S(2)}) collective-permute-start(bf16[528,128]{1,0:T(8,128)(2,1)} %get-tuple-element.32), channel_id=1, source_target_pairs={{0,3},{1,0},{2,1},{3,2},{4,7},{5,4},{6,5},{7,6},{8,11},{9,8},{10,9... | collective-permute-start | bytes 405512 | tf_op jit(solution)/shard_map/ppermute | solution.py:17
  187.6 25.4 %collective-permute-start.45 = (bf16[528,128]{1,0:T(8,128)(2,1)}, bf16[528,128]{1,0:T(8,128)(2,1)}, u32[]{:S(2)}, u32[]{:S(2)}) collective-permute-start(bf16[528,128]{1,0:T(8,128)(2,1)} %get-tuple-element.33), channel_id=1, source_target_pairs={{0,2},{1,3},{2,0},{3,1},{4,6},{5,7},{6,4},{7,5},{8,10},{9,11},{10,... | collective-permute-start | bytes 405512 | tf_op jit(solution)/shard_map/ppermute | solution.py:17
  187.6 25.4 %collective-permute-start.46 = (bf16[528,128]{1,0:T(8,128)(2,1)}, bf16[528,128]{1,0:T(8,128)(2,1)}, u32[]{:S(2)}, u32[]{:S(2)}) collective-permute-start(bf16[528,128]{1,0:T(8,128)(2,1)} %get-tuple-element.34), channel_id=1, source_target_pairs={{0,1},{1,2},{2,3},{3,0},{4,5},{5,6},{6,7},{7,4},{8,9},{9,10},{10,1... | collective-permute-start | bytes 405512 | tf_op jit(solution)/shard_map/ppermute | solution.py:17
  208.5 9.7 %collective-permute-start.43 = (f32[1,512]{1,0:T(1,128)S(1)}, f32[1,512]{1,0:T(1,128)S(1)}, u32[]{:S(2)}, u32[]{:S(2)}) collective-permute-start(f32[1,512]{1,0:T(1,128)S(1)} %get-tuple-element.29), channel_id=1, source_target_pairs={{0,1},{1,2},{2,3},{3,0},{4,5},{5,6},{6,7},{7,4},{8,9},{9,10},{10,1... | collective-permute-start | bytes 6152 | tf_op jit(solution)/shard_map/ppermute | solution.py:17
  211.4 6.8 %collective-permute-start.42 = (f32[1,512]{1,0:T(1,128)S(1)}, f32[1,512]{1,0:T(1,128)S(1)}, u32[]{:S(2)}, u32[]{:S(2)}) collective-permute-start(f32[1,512]{1,0:T(1,128)S(1)} %get-tuple-element.29), channel_id=1, source_target_pairs={{0,3},{1,0},{2,1},{3,2},{4,7},{5,4},{6,5},{7,6},{8,11},{9,8},{10,9... | collective-permute-start | bytes 6152 | tf_op jit(solution)/shard_map/ppermute | solution.py:17
  212.4 5.8 %collective-permute-start.41 = (f32[1,512]{1,0:T(1,128)S(1)}, f32[1,512]{1,0:T(1,128)S(1)}, u32[]{:S(2)}, u32[]{:S(2)}) collective-permute-start(f32[1,512]{1,0:T(1,128)S(1)} %get-tuple-element.29), channel_id=1, source_target_pairs={{0,2},{1,3},{2,0},{3,1},{4,6},{5,7},{6,4},{7,5},{8,10},{9,11},{10,... | collective-permute-start | bytes 6152 | tf_op jit(solution)/shard_map/ppermute | solution.py:17
  (47 other events, 177.1 us)

commit v3 on v2

--- a/solution.py
+++ b/solution.py
@@ -324,9 +324,10 @@
         for mask, array in pieces:
             flipped.append((mask ^ bit, from_flipped(array, bit, wide_count)))
         pieces = pieces + flipped
-    pieces = pieces + [
-        (mask ^ 1, from_flipped(array, 1, wide_count)) for mask, array in pieces
-    ]
+    others = []
+    for mask, array in pieces:
+        others.append((mask ^ 1, from_flipped(array, 1, wide_count)))
+    pieces = pieces + others
     return [(mask, array, spans) for mask, array in pieces]
 
 

time: 220 us -> 220 us (level)
  no operation moved by 1% of the time
where the time goes in v3:
time: 220 us; the launch traced here: 219 us
  waiting for transfers between devices  89.4 us (41%)
  starting transfers between devices  48.8 us (22%)
  Pallas kernels  44 us (20%)
  local copies, waits for them, and re-layouts  32 us (15%)
  other arithmetic  3.57 us (2%)
    ppermute x19, waiting for transfers between devices, from_ahead(): return lax.ppermute(value, 'narrow', pairs)  57.1 us
    ppermute x28, waiting for transfers between devices, from_flipped(): lax.ppermute(value, 'wide', [(index, index ^ bit) for index in range(coun...  32.4 us
    ppermute x19, starting transfers between devices, from_ahead(): return lax.ppermute(value, 'narrow', pairs)  27.2 us
    unnamed x95, local copies, waits for them, and re-layouts  25.4 us
    pallas_call x4, Pallas kernels, pool_quarter(): pl.pallas_call(kernel, out_shape=jax.ShapeDtypeStruct((total, emb), jnp.b...  23.3 us
    ppermute x28, starting transfers between devices, from_flipped(): lax.ppermute(value, 'wide', [(index, index ^ bit) for index in range(coun...  17.6 us
    pallas_call x1, Pallas kernels, top_network(): pl.pallas_call(kernel, out_shape=(jax.ShapeDtypeStruct((rows, columns), j...  11.6 us
    pallas_call x1, Pallas kernels, place_rows(): pl.pallas_call(kernel, out_shape=jax.ShapeDtypeStruct((slot_count, emb),...  5.13 us
  transfers between devices with their start and end apart: 48, of which 13 were waited for; matrix products, arithmetic and copies ran while one was open for 3% of the time, Pallas kernels for 17%

profile of v3, /device:TPU:0, one launch (start us, length us, event | category | flops | bytes accessed | tf_op | source)
XLA Modules:
  0.0 218.8 jit_solution(12128218064869300745)
XLA Ops:
  0.6 1.5 copy.18
  2.2 1.5 reshape_squeeze.6.lookups_ref
  3.7 5.8 %pool_quarter.6 = bf16[1024,128]{1,0:T(8,128)(2,1)} custom-call(s32[8,4,8,256]{3,2,1,0:T(8,128)} %reshape_squeeze.6.lookups_ref, s32[32,128]{1,0:T(8,128)} %bitcast.30, bf16[2048,128]{1,0:T(8,128)(2,1)} %bitcast.24), custom_call_target="tpu_custom_call" | custom-call | flops 1073741824 | bytes 262144 | tf_op jit(solution)/shard_map/pool_quarter/pallas_call | solution.py:92
  9.5 4.1 %collective-permute-start.1 = (bf16[1024,128]{1,0:T(8,128)(2,1)}, bf16[1024,128]{1,0:T(8,128)(2,1)S(1)}, u32[]{:S(2)}, u32[]{:S(2)}) collective-permute-start(bf16[1024,128]{1,0:T(8,128)(2,1)} %pool_quarter.6), channel_id=1, source_target_pairs={{0,2},{1,3},{2,0},{3,1},{4,6},{5,7},{6,4},{7,5},{8,10},{9,11},{10,... | collective-permute-start | bytes 786440 | tf_op jit(solution)/shard_map/ppermute | solution.py:17
  13.6 5.8 %pool_quarter.7 = bf16[1024,128]{1,0:T(8,128)(2,1)} custom-call(s32[8,4,8,256]{3,2,1,0:T(8,128)} %reshape_squeeze.6.lookups_ref, s32[32,128]{1,0:T(8,128)} %bitcast.31, bf16[2048,128]{1,0:T(8,128)(2,1)} %bitcast.25), custom_call_target="tpu_custom_call" | custom-call | flops 1073741824 | bytes 262144 | tf_op jit(solution)/shard_map/pool_quarter/pallas_call | solution.py:92
  19.3 1.3 collective-permute-start.2
  20.7 5.8 %pool_quarter.5 = bf16[1024,128]{1,0:T(8,128)(2,1)} custom-call(s32[8,4,8,256]{3,2,1,0:T(8,128)} %reshape_squeeze.6.lookups_ref, s32[32,128]{1,0:T(8,128)} %bitcast.32, bf16[2048,128]{1,0:T(8,128)(2,1)} %bitcast.26), custom_call_target="tpu_custom_call" | custom-call | flops 1073741824 | bytes 262144 | tf_op jit(solution)/shard_map/pool_quarter/pallas_call | solution.py:92
  27.1 6.0 %pool_quarter.4 = f32[1024,128]{1,0:T(8,128)} custom-call(s32[8,4,8,256]{3,2,1,0:T(8,128)} %reshape_squeeze.6.lookups_ref, s32[32,128]{1,0:T(8,128)} %bitcast.33, bf16[2048,128]{1,0:T(8,128)(2,1)} %bitcast.27), custom_call_target="tpu_custom_call" | custom-call | flops 1073741824 | bytes 262144 | tf_op jit(solution)/shard_map/pool_quarter/pallas_call | solution.py:92
  33.1 3.8 %collective-permute-done.2 = bf16[1024,128]{1,0:T(8,128)(2,1)S(1)} collective-permute-done((bf16[1024,128]{1,0:T(8,128)(2,1)}, bf16[1024,128]{1,0:T(8,128)(2,1)S(1)}, u32[]{:S(2)}, u32[]{:S(2)}) %collective-permute-start.2) | collective-permute-done | bytes 262176 | tf_op jit(solution)/shard_map/ppermute | solution.py:17
  36.9 1.9 add_convert_fusion
  38.8 4.0 %all-to-all-start = ((bf16[8,128,128]{2,1,0:T(8,128)(2,1)}), bf16[8,128,128]{2,1,0:T(8,128)(2,1)}, u32[]{:S(2)}, u32[]{:S(2)}) async-start(bf16[8,128,128]{2,1,0:T(8,128)(2,1)} %bitcast.2), calls=%async_computation | async-start | bytes 524288 | tf_op jit(solution)/shard_map/all_to_all | solution.py:408
  42.9 1.9 fusion
  44.8 1.1 pad_maximum_fusion
  45.9 3.5 %collective-permute-start.6 = (bf16[256,1024]{1,0:T(8,128)(2,1)}, bf16[256,1024]{1,0:T(8,128)(2,1)S(1)}, u32[]{:S(2)}, u32[]{:S(2)}) collective-permute-start(bf16[256,1024]{1,0:T(8,128)(2,1)} %get-tuple-element.39), channel_id=1, source_target_pairs={{0,3},{1,0},{2,1},{3,2},{4,7},{5,4},{6,5},{7,6},{8,11},{9,8},{10,9... | collective-permute-start | bytes 1572872 | tf_op jit(solution)/shard_map/ppermute | solution.py:17
  49.4 1.2 collective-permute-start.14
  50.6 1.0 copy_bitcast_fusion.refs_0_
  51.6 32.2 %collective-permute-done.30.refs_30_ = bf16[128,1024]{1,0:T(8,128)(2,1)} collective-permute-done((bf16[128,1024]{1,0:T(8,128)(2,1)}, bf16[128,1024]{1,0:T(8,128)(2,1)}, u32[]{:S(2)}, u32[]{:S(2)}) %collective-permute-start.30) | collective-permute-done | bytes 262176 | tf_op jit(solution)/shard_map/ppermute | solution.py:17
  83.8 1.6 collective-permute-start.32
  85.5 5.4 %collective-permute-done.40 = f32[1024]{0:T(1024)S(1)} collective-permute-done((f32[1024]{0:T(1024)S(1)}, f32[1024]{0:T(1024)S(1)}, u32[]{:S(2)}, u32[]{:S(2)}) %collective-permute-start.40) | collective-permute-done | bytes 4128 | tf_op jit(solution)/shard_map/ppermute | solution.py:17
  90.9 4.5 %collective-permute-done.39 = f32[1024]{0:T(1024)S(1)} collective-permute-done((f32[1024]{0:T(1024)S(1)}, f32[1024]{0:T(1024)S(1)}, u32[]{:S(2)}, u32[]{:S(2)}) %collective-permute-start.39) | collective-permute-done | bytes 4128 | tf_op jit(solution)/shard_map/ppermute | solution.py:17
  95.4 1.5 collective-permute-start.31
  96.9 2.1 collective-permute-done.38
  99.0 3.8 %collective-permute-start.3 = (bf16[128,1024]{1,0:T(8,128)(2,1)S(1)}, bf16[128,1024]{1,0:T(8,128)(2,1)S(1)}, u32[]{:S(2)}, u32[]{:S(2)}) collective-permute-start(bf16[128,1024]{1,0:T(8,128)(2,1)S(1)} %copy_bitcast_fusion.refs_0_), channel_id=1, source_target_pairs={{0,3},{1,0},{2,1},{3,2},{4,7},{5,4},{6,5},{7,6},{8,11},{9,8},{10,9... | collective-permute-start | bytes 786440 | tf_op jit(solution)/shard_map/ppermute | solution.py:17
  104.8 5.2 %collective-permute-done.5.refs_3_ = bf16[128,1024]{1,0:T(8,128)(2,1)S(1)} collective-permute-done((bf16[128,1024]{1,0:T(8,128)(2,1)S(1)}, bf16[128,1024]{1,0:T(8,128)(2,1)S(1)}, u32[]{:S(2)}, u32[]{:S(2)}) %collective-permute-start.5) | collective-permute-done | bytes 262176 | tf_op jit(solution)/shard_map/ppermute | solution.py:17
  111.8 3.7 %collective-permute-done.22.refs_22_ = bf16[128,1024]{1,0:T(8,128)(2,1)S(1)} collective-permute-done((bf16[128,1024]{1,0:T(8,128)(2,1)S(1)}, bf16[128,1024]{1,0:T(8,128)(2,1)S(1)}, u32[]{:S(2)}, u32[]{:S(2)}) %collective-permute-start.22) | collective-permute-done | bytes 262176 | tf_op jit(solution)/shard_map/ppermute | solution.py:17
  115.5 4.2 %collective-permute-start.4 = (bf16[128,1024]{1,0:T(8,128)(2,1)S(1)}, bf16[128,1024]{1,0:T(8,128)(2,1)S(1)}, u32[]{:S(2)}, u32[]{:S(2)}) collective-permute-start(bf16[128,1024]{1,0:T(8,128)(2,1)S(1)} %collective-permute-done.3.refs_1_), channel_id=1, source_target_pairs={{0,3},{1,0},{2,1},{3,2},{4,7},{5,4},{6,5},{7,6},{8,11},{9,8},{10,9... | collective-permute-start | bytes 786440 | tf_op jit(solution)/shard_map/ppermute | solution.py:17
  122.0 1.6 collective-permute-start.24
  123.7 1.5 collective-permute-start.23
  126.6 1.6 collective-permute-start.8
  129.0 1.5 collective-permute-start.7
  131.2 1.6 collective-permute-done.23.refs_23_
  132.8 1.5 collective-permute-start.16
  135.7 6.8 %collective-permute-done.8.refs_8_ = bf16[256,1024]{1,0:T(8,128)(2,1)S(1)} collective-permute-done((bf16[256,1024]{1,0:T(8,128)(2,1)S(1)}, bf16[256,1024]{1,0:T(8,128)(2,1)S(1)}, u32[]{:S(2)}, u32[]{:S(2)}) %collective-permute-start.8) | collective-permute-done | bytes 524320 | tf_op jit(solution)/shard_map/ppermute | solution.py:21
  143.1 1.0 collective-permute-done.7.refs_7_
  146.2 8.3 %collective-permute-done.16.refs_16_ = bf16[256,1024]{1,0:T(8,128)(2,1)} collective-permute-done((bf16[256,1024]{1,0:T(8,128)(2,1)S(1)}, bf16[256,1024]{1,0:T(8,128)(2,1)}, u32[]{:S(2)}, u32[]{:S(2)}) %collective-permute-start.16) | collective-permute-done | bytes 524320 | tf_op jit(solution)/shard_map/ppermute | solution.py:21
  156.4 1.6 collective-permute-start.17
  159.5 1.5 collective-permute-start.25
  161.6 13.8 %collective-permute-done.25.refs_25_ = bf16[128,1024]{1,0:T(8,128)(2,1)S(1)} collective-permute-done((bf16[128,1024]{1,0:T(8,128)(2,1)S(1)}, bf16[128,1024]{1,0:T(8,128)(2,1)S(1)}, u32[]{:S(2)}, u32[]{:S(2)}) %collective-permute-start.25) | collective-permute-done | bytes 262176 | tf_op jit(solution)/shard_map/ppermute | solution.py:21
  177.5 4.0 %section_rows.1 = (bf16[528,128]{1,0:T(8,128)(2,1)}, bf16[528,128]{1,0:T(8,128)(2,1)}, bf16[528,128]{1,0:T(8,128)(2,1)}, bf16[528,128]{1,0:T(8,128)(2,1)}) custom-call(s32[4]{0:T(128)} %bitcast.34, bf16[1024,128]{1,0:T(8,128)(2,1)} %bitcast.29, s32[1,1024]{1,0:T(1,128)} %slots_ref.1), custom_call_target="tpu_custom_call" | custom-call | flops 536870912 | bytes 524288 | tf_op jit(solution)/shard_map/section_rows/pallas_call | solution.py:138
  182.2 2.1 constant_dynamic-slice_fusion.1.refs_5_
  184.3 3.3 %collective-permute-start.44 = (bf16[528,128]{1,0:T(8,128)(2,1)}, bf16[528,128]{1,0:T(8,128)(2,1)S(1)}, u32[]{:S(2)}, u32[]{:S(2)}) collective-permute-start(bf16[528,128]{1,0:T(8,128)(2,1)} %get-tuple-element.32), channel_id=1, source_target_pairs={{0,3},{1,0},{2,1},{3,2},{4,7},{5,4},{6,5},{7,6},{8,11},{9,8},{10,9... | collective-permute-start | bytes 405512 | tf_op jit(solution)/shard_map/ppermute | solution.py:17
  190.3 0.9 copy-done.30
  191.3 0.9 copy-done.32
  192.2 0.9 copy-done.34
  197.0 11.6 %top_network.1 = (bf16[512,1024]{1,0:T(8,128)(2,1)}, f32[1,512]{1,0:T(1,128)S(1)}) custom-call(bf16[128,1024]{1,0:T(8,128)(2,1)S(1)} %copy_bitcast_fusion.refs_0_, bf16[128,1024]{1,0:T(8,128)(2,1)S(1)} %copy-done.18, bf16[128,1024]{1,0:T(8,128)(2,1)S(1)} %copy-done.28, bf16[128,1024]{1,0:T(8,128)(2,1)S(1)} %copy-done.16, bf16[1024,1024]{1,0:T(8,128)(2,1)S(1)} %copy-done, ...), custom_call_target="tpu_custom_call" | custom-call | flops 8589934592 | bytes 16777216 | tf_op jit(solution)/shard_map/top_network/pallas_call | solution.py:280
  208.5 2.9 %collective-permute-start.43 = (f32[1,512]{1,0:T(1,128)S(1)}, f32[1,512]{1,0:T(1,128)S(1)}, u32[]{:S(2)}, u32[]{:S(2)}) collective-permute-start(f32[1,512]{1,0:T(1,128)S(1)} %get-tuple-element.29), channel_id=1, source_target_pairs={{0,1},{1,2},{2,3},{3,0},{4,5},{5,6},{6,7},{7,4},{8,9},{9,10},{10,1... | collective-permute-start | bytes 6152 | tf_op jit(solution)/shard_map/ppermute | solution.py:17
  211.4 1.0 collective-permute-start.42
  213.1 5.1 %place_rows.1 = bf16[2048,128]{1,0:T(8,128)(2,1)} custom-call(bf16[528,128]{1,0:T(8,128)(2,1)} %get-tuple-element.31.refs_0_, bf16[528,128]{1,0:T(8,128)(2,1)} %copy-done.46, bf16[528,128]{1,0:T(8,128)(2,1)} %collective-permute-done.45.refs_2_, bf16[528,128]{1,0:T(8,128)(2,1)} %collective-permute-done.46.refs_3_, bf16[2048,128]{1,0:T(8,128)(2,1)} %bitcast.28), custom_call_target="tpu_custom_call" | custom-call | flops 2147483648 | bytes 1048576 | tf_op jit(solution)/shard_map/place_rows/pallas_call | solution.py:187
  (160 shorter events, 28.1 us)
Async XLA Ops:
  9.5 23.6 %collective-permute-start.1 = (bf16[1024,128]{1,0:T(8,128)(2,1)}, bf16[1024,128]{1,0:T(8,128)(2,1)S(1)}, u32[]{:S(2)}, u32[]{:S(2)}) collective-permute-start(bf16[1024,128]{1,0:T(8,128)(2,1)} %pool_quarter.6), channel_id=1, source_target_pairs={{0,2},{1,3},{2,0},{3,1},{4,6},{5,7},{6,4},{7,5},{8,10},{9,11},{10,... | collective-permute-start | bytes 786440 | tf_op jit(solution)/shard_map/ppermute | solution.py:17
  19.3 17.6 %collective-permute-start.2 = (bf16[1024,128]{1,0:T(8,128)(2,1)}, bf16[1024,128]{1,0:T(8,128)(2,1)S(1)}, u32[]{:S(2)}, u32[]{:S(2)}) collective-permute-start(bf16[1024,128]{1,0:T(8,128)(2,1)} %pool_quarter.7), channel_id=1, source_target_pairs={{0,3},{1,0},{2,1},{3,2},{4,7},{5,4},{6,5},{7,6},{8,11},{9,8},{10,9... | collective-permute-start | bytes 786440 | tf_op jit(solution)/shard_map/ppermute | solution.py:17
  26.4 10.5 %collective-permute-start = (bf16[1024,128]{1,0:T(8,128)(2,1)}, bf16[1024,128]{1,0:T(8,128)(2,1)S(1)}, u32[]{:S(2)}, u32[]{:S(2)}) collective-permute-start(bf16[1024,128]{1,0:T(8,128)(2,1)} %pool_quarter.5), channel_id=1, source_target_pairs={{0,1},{1,2},{2,3},{3,0},{4,5},{5,6},{6,7},{7,4},{8,9},{9,10},{10,1... | collective-permute-start | bytes 786440 | tf_op jit(solution)/shard_map/ppermute | solution.py:17
  38.8 11.8 %all-to-all-start = ((bf16[8,128,128]{2,1,0:T(8,128)(2,1)}), bf16[8,128,128]{2,1,0:T(8,128)(2,1)}, u32[]{:S(2)}, u32[]{:S(2)}) async-start(bf16[8,128,128]{2,1,0:T(8,128)(2,1)} %bitcast.2), calls=%async_computation | async-start | bytes 524288 | tf_op jit(solution)/shard_map/all_to_all | solution.py:408
  45.9 49.5 %collective-permute-start.6 = (bf16[256,1024]{1,0:T(8,128)(2,1)}, bf16[256,1024]{1,0:T(8,128)(2,1)S(1)}, u32[]{:S(2)}, u32[]{:S(2)}) collective-permute-start(bf16[256,1024]{1,0:T(8,128)(2,1)} %get-tuple-element.39), channel_id=1, source_target_pairs={{0,3},{1,0},{2,1},{3,2},{4,7},{5,4},{6,5},{7,6},{8,11},{9,8},{10,9... | collective-permute-start | bytes 1572872 | tf_op jit(solution)/shard_map/ppermute | solution.py:17
  49.4 34.4 %collective-permute-start.30 = (bf16[128,1024]{1,0:T(8,128)(2,1)}, bf16[128,1024]{1,0:T(8,128)(2,1)}, u32[]{:S(2)}, u32[]{:S(2)}) collective-permute-start(bf16[128,1024]{1,0:T(8,128)(2,1)} %get-tuple-element.25), channel_id=1, source_target_pairs={{0,2},{1,3},{2,0},{3,1},{4,6},{5,7},{6,4},{7,5},{8,10},{9,11},{10,... | collective-permute-start | bytes 786440 | tf_op jit(solution)/shard_map/ppermute | solution.py:17
  49.4 49.6 %collective-permute-start.14 = (bf16[256,1024]{1,0:T(8,128)(2,1)}, bf16[256,1024]{1,0:T(8,128)(2,1)S(1)}, u32[]{:S(2)}, u32[]{:S(2)}) collective-permute-start(bf16[256,1024]{1,0:T(8,128)(2,1)} %get-tuple-element.21), channel_id=1, source_target_pairs={{0,1},{1,2},{2,3},{3,0},{4,5},{5,6},{6,7},{7,4},{8,9},{9,10},{10,1... | collective-permute-start | bytes 1572872 | tf_op jit(solution)/shard_map/ppermute | solution.py:17
  83.8 19.0 %collective-permute-start.34 = (bf16[128,1024]{1,0:T(8,128)(2,1)}, bf16[128,1024]{1,0:T(8,128)(2,1)S(1)}, u32[]{:S(2)}, u32[]{:S(2)}) collective-permute-start(bf16[128,1024]{1,0:T(8,128)(2,1)} %collective-permute-done.30.refs_30_), channel_id=1, source_target_pairs={{0,4},{4,0},{8,12},{12,8},{16,20},{20,16},{24,28},{28,24},{1,5},{5... | collective-permute-start | bytes 786440 | tf_op jit(solution)/shard_map/ppermute | solution.py:21
  83.8 19.8 %collective-permute-start.32 = (bf16[128,1024]{1,0:T(8,128)(2,1)}, bf16[128,1024]{1,0:T(8,128)(2,1)S(1)}, u32[]{:S(2)}, u32[]{:S(2)}) collective-permute-start(bf16[128,1024]{1,0:T(8,128)(2,1)} %collective-permute-done.30.refs_30_), channel_id=1, source_target_pairs={{0,8},{4,12},{8,0},{12,4},{16,24},{20,28},{24,16},{28,20},{1,9},{5... | collective-permute-start | bytes 786440 | tf_op jit(solution)/shard_map/ppermute | solution.py:21
  85.4 5.4 %collective-permute-start.40 = (f32[1024]{0:T(1024)S(1)}, f32[1024]{0:T(1024)S(1)}, u32[]{:S(2)}, u32[]{:S(2)}) collective-permute-start(f32[1024]{0:T(1024)S(1)} %copy-done.44), channel_id=1, source_target_pairs={{0,1},{1,2},{2,3},{3,0},{4,5},{5,6},{6,7},{7,4},{8,9},{9,10},{10,1... | collective-permute-start | bytes 12296 | tf_op jit(solution)/shard_map/ppermute | solution.py:17
  90.9 4.5 %collective-permute-start.39 = (f32[1024]{0:T(1024)S(1)}, f32[1024]{0:T(1024)S(1)}, u32[]{:S(2)}, u32[]{:S(2)}) collective-permute-start(f32[1024]{0:T(1024)S(1)} %copy-done.44), channel_id=1, source_target_pairs={{0,2},{1,3},{2,0},{3,1},{4,6},{5,7},{6,4},{7,5},{8,10},{9,11},{10,... | collective-permute-start | bytes 12296 | tf_op jit(solution)/shard_map/ppermute | solution.py:17
  95.4 3.6 %collective-permute-start.38 = (f32[1024]{0:T(1024)S(1)}, f32[1024]{0:T(1024)S(1)}, u32[]{:S(2)}, u32[]{:S(2)}) collective-permute-start(f32[1024]{0:T(1024)S(1)} %copy-done.44), channel_id=1, source_target_pairs={{0,3},{1,0},{2,1},{3,2},{4,7},{5,4},{6,5},{7,6},{8,11},{9,8},{10,9... | collective-permute-start | bytes 12296 | tf_op jit(solution)/shard_map/ppermute | solution.py:17
  95.4 8.9 %collective-permute-start.31 = (bf16[128,1024]{1,0:T(8,128)(2,1)}, bf16[128,1024]{1,0:T(8,128)(2,1)S(1)}, u32[]{:S(2)}, u32[]{:S(2)}) collective-permute-start(bf16[128,1024]{1,0:T(8,128)(2,1)} %collective-permute-done.30.refs_30_), channel_id=1, source_target_pairs={{0,16},{4,20},{8,24},{12,28},{16,0},{20,4},{24,8},{28,12},{1,17},{... | collective-permute-start | bytes 786440 | tf_op jit(solution)/shard_map/ppermute | solution.py:21
  99.0 11.0 %collective-permute-start.5 = (bf16[128,1024]{1,0:T(8,128)(2,1)S(1)}, bf16[128,1024]{1,0:T(8,128)(2,1)S(1)}, u32[]{:S(2)}, u32[]{:S(2)}) collective-permute-start(bf16[128,1024]{1,0:T(8,128)(2,1)S(1)} %copy_bitcast_fusion.refs_0_), channel_id=1, source_target_pairs={{0,1},{1,2},{2,3},{3,0},{4,5},{5,6},{6,7},{7,4},{8,9},{9,10},{10,1... | collective-permute-start | bytes 786440 | tf_op jit(solution)/shard_map/ppermute | solution.py:17
  99.0 12.8 %collective-permute-start.3 = (bf16[128,1024]{1,0:T(8,128)(2,1)S(1)}, bf16[128,1024]{1,0:T(8,128)(2,1)S(1)}, u32[]{:S(2)}, u32[]{:S(2)}) collective-permute-start(bf16[128,1024]{1,0:T(8,128)(2,1)S(1)} %copy_bitcast_fusion.refs_0_), channel_id=1, source_target_pairs={{0,3},{1,0},{2,1},{3,2},{4,7},{5,4},{6,5},{7,6},{8,11},{9,8},{10,9... | collective-permute-start | bytes 786440 | tf_op jit(solution)/shard_map/ppermute | solution.py:17
  103.5 12.0 %collective-permute-start.22 = (bf16[128,1024]{1,0:T(8,128)(2,1)S(1)}, bf16[128,1024]{1,0:T(8,128)(2,1)S(1)}, u32[]{:S(2)}, u32[]{:S(2)}) collective-permute-start(bf16[128,1024]{1,0:T(8,128)(2,1)S(1)} %slice.4), channel_id=1, source_target_pairs={{0,3},{1,0},{2,1},{3,2},{4,7},{5,4},{6,5},{7,6},{8,11},{9,8},{10,9... | collective-permute-start | bytes 786440 | tf_op jit(solution)/shard_map/ppermute | solution.py:17
  103.6 16.8 %collective-permute-start.36 = (bf16[128,1024]{1,0:T(8,128)(2,1)S(1)}, bf16[128,1024]{1,0:T(8,128)(2,1)S(1)}, u32[]{:S(2)}, u32[]{:S(2)}) collective-permute-start(bf16[128,1024]{1,0:T(8,128)(2,1)S(1)} %collective-permute-done.32.refs_32_), channel_id=1, source_target_pairs={{0,4},{4,0},{8,12},{12,8},{16,20},{20,16},{24,28},{28,24},{1,5},{5... | collective-permute-start | bytes 786440 | tf_op jit(solution)/shard_map/ppermute | solution.py:21
  104.3 17.0 %collective-permute-start.35 = (bf16[128,1024]{1,0:T(8,128)(2,1)S(1)}, bf16[128,1024]{1,0:T(8,128)(2,1)S(1)}, u32[]{:S(2)}, u32[]{:S(2)}) collective-permute-start(bf16[128,1024]{1,0:T(8,128)(2,1)S(1)} %collective-permute-done.31.refs_31_), channel_id=1, source_target_pairs={{0,4},{4,0},{8,12},{12,8},{16,20},{20,16},{24,28},{28,24},{1,5},{5... | collective-permute-start | bytes 786440 | tf_op jit(solution)/shard_map/ppermute | solution.py:21
  110.7 13.0 %collective-permute-start.33 = (bf16[128,1024]{1,0:T(8,128)(2,1)S(1)}, bf16[128,1024]{1,0:T(8,128)(2,1)S(1)}, u32[]{:S(2)}, u32[]{:S(2)}) collective-permute-start(bf16[128,1024]{1,0:T(8,128)(2,1)S(1)} %collective-permute-done.31.refs_31_), channel_id=1, source_target_pairs={{0,8},{4,12},{8,0},{12,4},{16,24},{20,28},{24,16},{28,20},{1,9},{5... | collective-permute-start | bytes 786440 | tf_op jit(solution)/shard_map/ppermute | solution.py:21
  111.8 22.5 %collective-permute-start.10 = (bf16[256,1024]{1,0:T(8,128)(2,1)S(1)}, bf16[256,1024]{1,0:T(8,128)(2,1)S(1)}, u32[]{:S(2)}, u32[]{:S(2)}) collective-permute-start(bf16[256,1024]{1,0:T(8,128)(2,1)S(1)} %collective-permute-done.6.refs_6_), channel_id=1, source_target_pairs={{0,4},{4,0},{8,12},{12,8},{16,20},{20,16},{24,28},{28,24},{1,5},{5... | collective-permute-start | bytes 1572872 | tf_op jit(solution)/shard_map/ppermute | solution.py:21
  115.5 10.4 %collective-permute-start.4 = (bf16[128,1024]{1,0:T(8,128)(2,1)S(1)}, bf16[128,1024]{1,0:T(8,128)(2,1)S(1)}, u32[]{:S(2)}, u32[]{:S(2)}) collective-permute-start(bf16[128,1024]{1,0:T(8,128)(2,1)S(1)} %collective-permute-done.3.refs_1_), channel_id=1, source_target_pairs={{0,3},{1,0},{2,1},{3,2},{4,7},{5,4},{6,5},{7,6},{8,11},{9,8},{10,9... | collective-permute-start | bytes 786440 | tf_op jit(solution)/shard_map/ppermute | solution.py:17
  121.1 7.1 %collective-permute-start.26 = (bf16[128,1024]{1,0:T(8,128)(2,1)S(1)}, bf16[128,1024]{1,0:T(8,128)(2,1)S(1)}, u32[]{:S(2)}, u32[]{:S(2)}) collective-permute-start(bf16[128,1024]{1,0:T(8,128)(2,1)S(1)} %collective-permute-done.22.refs_22_), channel_id=1, source_target_pairs={{0,4},{4,0},{8,12},{12,8},{16,20},{20,16},{24,28},{28,24},{1,5},{5... | collective-permute-start | bytes 786440 | tf_op jit(solution)/shard_map/ppermute | solution.py:21
  122.0 9.2 %collective-permute-start.24 = (bf16[128,1024]{1,0:T(8,128)(2,1)S(1)}, bf16[128,1024]{1,0:T(8,128)(2,1)S(1)}, u32[]{:S(2)}, u32[]{:S(2)}) collective-permute-start(bf16[128,1024]{1,0:T(8,128)(2,1)S(1)} %collective-permute-done.22.refs_22_), channel_id=1, source_target_pairs={{0,8},{4,12},{8,0},{12,4},{16,24},{20,28},{24,16},{28,20},{1,9},{5... | collective-permute-start | bytes 786440 | tf_op jit(solution)/shard_map/ppermute | solution.py:21
  123.7 9.2 %collective-permute-start.23 = (bf16[128,1024]{1,0:T(8,128)(2,1)S(1)}, bf16[128,1024]{1,0:T(8,128)(2,1)S(1)}, u32[]{:S(2)}, u32[]{:S(2)}) collective-permute-start(bf16[128,1024]{1,0:T(8,128)(2,1)S(1)} %collective-permute-done.22.refs_22_), channel_id=1, source_target_pairs={{0,16},{4,20},{8,24},{12,28},{16,0},{20,4},{24,8},{28,12},{1,17},{... | collective-permute-start | bytes 786440 | tf_op jit(solution)/shard_map/ppermute | solution.py:21
  126.6 15.8 %collective-permute-start.8 = (bf16[256,1024]{1,0:T(8,128)(2,1)S(1)}, bf16[256,1024]{1,0:T(8,128)(2,1)S(1)}, u32[]{:S(2)}, u32[]{:S(2)}) collective-permute-start(bf16[256,1024]{1,0:T(8,128)(2,1)S(1)} %collective-permute-done.6.refs_6_), channel_id=1, source_target_pairs={{0,8},{4,12},{8,0},{12,4},{16,24},{20,28},{24,16},{28,20},{1,9},{5... | collective-permute-start | bytes 1572872 | tf_op jit(solution)/shard_map/ppermute | solution.py:21
  129.0 15.2 %collective-permute-start.7 = (bf16[256,1024]{1,0:T(8,128)(2,1)S(1)}, bf16[256,1024]{1,0:T(8,128)(2,1)}, u32[]{:S(2)}, u32[]{:S(2)}) collective-permute-start(bf16[256,1024]{1,0:T(8,128)(2,1)S(1)} %collective-permute-done.6.refs_6_), channel_id=1, source_target_pairs={{0,16},{4,20},{8,24},{12,28},{16,0},{20,4},{24,8},{28,12},{1,17},{... | collective-permute-start | bytes 1572872 | tf_op jit(solution)/shard_map/ppermute | solution.py:21
  131.2 13.7 %collective-permute-start.18 = (bf16[256,1024]{1,0:T(8,128)(2,1)S(1)}, bf16[256,1024]{1,0:T(8,128)(2,1)S(1)}, u32[]{:S(2)}, u32[]{:S(2)}) collective-permute-start(bf16[256,1024]{1,0:T(8,128)(2,1)S(1)} %collective-permute-done.14.refs_14_), channel_id=1, source_target_pairs={{0,4},{4,0},{8,12},{12,8},{16,20},{20,16},{24,28},{28,24},{1,5},{5... | collective-permute-start | bytes 1572872 | tf_op jit(solution)/shard_map/ppermute | solution.py:21
  132.8 21.7 %collective-permute-start.16 = (bf16[256,1024]{1,0:T(8,128)(2,1)S(1)}, bf16[256,1024]{1,0:T(8,128)(2,1)}, u32[]{:S(2)}, u32[]{:S(2)}) collective-permute-start(bf16[256,1024]{1,0:T(8,128)(2,1)S(1)} %collective-permute-done.14.refs_14_), channel_id=1, source_target_pairs={{0,16},{4,20},{8,24},{12,28},{16,0},{20,4},{24,8},{28,12},{1,17},{... | collective-permute-start | bytes 1572872 | tf_op jit(solution)/shard_map/ppermute | solution.py:21
  135.1 20.2 %collective-permute-start.15 = (bf16[256,1024]{1,0:T(8,128)(2,1)S(1)}, bf16[256,1024]{1,0:T(8,128)(2,1)}, u32[]{:S(2)}, u32[]{:S(2)}) collective-permute-start(bf16[256,1024]{1,0:T(8,128)(2,1)S(1)} %collective-permute-done.14.refs_14_), channel_id=1, source_target_pairs={{0,8},{4,12},{8,0},{12,4},{16,24},{20,28},{24,16},{28,20},{1,9},{5... | collective-permute-start | bytes 1572872 | tf_op jit(solution)/shard_map/ppermute | solution.py:21
  142.4 13.3 %collective-permute-start.37 = (bf16[128,1024]{1,0:T(8,128)(2,1)S(1)}, bf16[128,1024]{1,0:T(8,128)(2,1)S(1)}, u32[]{:S(2)}, u32[]{:S(2)}) collective-permute-start(bf16[128,1024]{1,0:T(8,128)(2,1)S(1)} %collective-permute-done.33.refs_33_), channel_id=1, source_target_pairs={{0,4},{4,0},{8,12},{12,8},{16,20},{20,16},{24,28},{28,24},{1,5},{5... | collective-permute-start | bytes 786440 | tf_op jit(solution)/shard_map/ppermute | solution.py:21
  144.2 13.9 %collective-permute-start.28 = (bf16[128,1024]{1,0:T(8,128)(2,1)S(1)}, bf16[128,1024]{1,0:T(8,128)(2,1)S(1)}, u32[]{:S(2)}, u32[]{:S(2)}) collective-permute-start(bf16[128,1024]{1,0:T(8,128)(2,1)S(1)} %collective-permute-done.24.refs_24_), channel_id=1, source_target_pairs={{0,4},{4,0},{8,12},{12,8},{16,20},{20,16},{24,28},{28,24},{1,5},{5... | collective-permute-start | bytes 786440 | tf_op jit(solution)/shard_map/ppermute | solution.py:21
  145.7 13.1 %collective-permute-start.27 = (bf16[128,1024]{1,0:T(8,128)(2,1)S(1)}, bf16[128,1024]{1,0:T(8,128)(2,1)S(1)}, u32[]{:S(2)}, u32[]{:S(2)}) collective-permute-start(bf16[128,1024]{1,0:T(8,128)(2,1)S(1)} %collective-permute-done.23.refs_23_), channel_id=1, source_target_pairs={{0,4},{4,0},{8,12},{12,8},{16,20},{20,16},{24,28},{28,24},{1,5},{5... | collective-permute-start | bytes 786440 | tf_op jit(solution)/shard_map/ppermute | solution.py:21
  154.5 21.0 %collective-permute-start.12 = (bf16[256,1024]{1,0:T(8,128)(2,1)S(1)}, bf16[256,1024]{1,0:T(8,128)(2,1)S(1)}, u32[]{:S(2)}, u32[]{:S(2)}) collective-permute-start(bf16[256,1024]{1,0:T(8,128)(2,1)S(1)} %collective-permute-done.8.refs_8_), channel_id=1, source_target_pairs={{0,4},{4,0},{8,12},{12,8},{16,20},{20,16},{24,28},{28,24},{1,5},{5... | collective-permute-start | bytes 1572872 | tf_op jit(solution)/shard_map/ppermute | solution.py:21
  155.3 21.7 %collective-permute-start.9 = (bf16[256,1024]{1,0:T(8,128)(2,1)}, bf16[256,1024]{1,0:T(8,128)(2,1)}, u32[]{:S(2)}, u32[]{:S(2)}) collective-permute-start(bf16[256,1024]{1,0:T(8,128)(2,1)} %collective-permute-done.7.refs_7_), channel_id=1, source_target_pairs={{0,8},{4,12},{8,0},{12,4},{16,24},{20,28},{24,16},{28,20},{1,9},{5... | collective-permute-start | bytes 1572872 | tf_op jit(solution)/shard_map/ppermute | solution.py:21
  156.4 21.1 %collective-permute-start.17 = (bf16[256,1024]{1,0:T(8,128)(2,1)}, bf16[256,1024]{1,0:T(8,128)(2,1)}, u32[]{:S(2)}, u32[]{:S(2)}) collective-permute-start(bf16[256,1024]{1,0:T(8,128)(2,1)} %collective-permute-done.15.refs_15_), channel_id=1, source_target_pairs={{0,16},{4,20},{8,24},{12,28},{16,0},{20,4},{24,8},{28,12},{1,17},{... | collective-permute-start | bytes 1572872 | tf_op jit(solution)/shard_map/ppermute | solution.py:21
  158.8 22.9 %collective-permute-start.11 = (bf16[256,1024]{1,0:T(8,128)(2,1)}, bf16[256,1024]{1,0:T(8,128)(2,1)}, u32[]{:S(2)}, u32[]{:S(2)}) collective-permute-start(bf16[256,1024]{1,0:T(8,128)(2,1)} %collective-permute-done.7.refs_7_), channel_id=1, source_target_pairs={{0,4},{4,0},{8,12},{12,8},{16,20},{20,16},{24,28},{28,24},{1,5},{5... | collective-permute-start | bytes 1572872 | tf_op jit(solution)/shard_map/ppermute | solution.py:21
  159.5 16.0 %collective-permute-start.25 = (bf16[128,1024]{1,0:T(8,128)(2,1)S(1)}, bf16[128,1024]{1,0:T(8,128)(2,1)S(1)}, u32[]{:S(2)}, u32[]{:S(2)}) collective-permute-start(bf16[128,1024]{1,0:T(8,128)(2,1)S(1)} %collective-permute-done.23.refs_23_), channel_id=1, source_target_pairs={{0,8},{4,12},{8,0},{12,4},{16,24},{20,28},{24,16},{28,20},{1,9},{5... | collective-permute-start | bytes 786440 | tf_op jit(solution)/shard_map/ppermute | solution.py:21
  175.5 8.8 %collective-permute-start.20 = (bf16[256,1024]{1,0:T(8,128)(2,1)}, bf16[256,1024]{1,0:T(8,128)(2,1)}, u32[]{:S(2)}, u32[]{:S(2)}) collective-permute-start(bf16[256,1024]{1,0:T(8,128)(2,1)} %collective-permute-done.16.refs_16_), channel_id=1, source_target_pairs={{0,4},{4,0},{8,12},{12,8},{16,20},{20,16},{24,28},{28,24},{1,5},{5... | collective-permute-start | bytes 1572872 | tf_op jit(solution)/shard_map/ppermute | solution.py:21
  177.0 10.7 %collective-permute-start.19 = (bf16[256,1024]{1,0:T(8,128)(2,1)}, bf16[256,1024]{1,0:T(8,128)(2,1)}, u32[]{:S(2)}, u32[]{:S(2)}) collective-permute-start(bf16[256,1024]{1,0:T(8,128)(2,1)} %collective-permute-done.15.refs_15_), channel_id=1, source_target_pairs={{0,4},{4,0},{8,12},{12,8},{16,20},{20,16},{24,28},{28,24},{1,5},{5... | collective-permute-start | bytes 1572872 | tf_op jit(solution)/shard_map/ppermute | solution.py:21
  177.0 11.3 %collective-permute-start.13 = (bf16[256,1024]{1,0:T(8,128)(2,1)}, bf16[256,1024]{1,0:T(8,128)(2,1)}, u32[]{:S(2)}, u32[]{:S(2)}) collective-permute-start(bf16[256,1024]{1,0:T(8,128)(2,1)} %collective-permute-done.9.refs_9_), channel_id=1, source_target_pairs={{0,4},{4,0},{8,12},{12,8},{16,20},{20,16},{24,28},{28,24},{1,5},{5... | collective-permute-start | bytes 1572872 | tf_op jit(solution)/shard_map/ppermute | solution.py:21
  177.5 10.8 %collective-permute-start.21 = (bf16[256,1024]{1,0:T(8,128)(2,1)}, bf16[256,1024]{1,0:T(8,128)(2,1)}, u32[]{:S(2)}, u32[]{:S(2)}) collective-permute-start(bf16[256,1024]{1,0:T(8,128)(2,1)} %collective-permute-done.17.refs_17_), channel_id=1, source_target_pairs={{0,4},{4,0},{8,12},{12,8},{16,20},{20,16},{24,28},{28,24},{1,5},{5... | collective-permute-start | bytes 1572872 | tf_op jit(solution)/shard_map/ppermute | solution.py:21
  181.7 5.9 %collective-permute-start.29 = (bf16[128,1024]{1,0:T(8,128)(2,1)}, bf16[128,1024]{1,0:T(8,128)(2,1)S(1)}, u32[]{:S(2)}, u32[]{:S(2)}) collective-permute-start(bf16[128,1024]{1,0:T(8,128)(2,1)} %copy-done.41), channel_id=1, source_target_pairs={{0,4},{4,0},{8,12},{12,8},{16,20},{20,16},{24,28},{28,24},{1,5},{5... | collective-permute-start | bytes 786440 | tf_op jit(solution)/shard_map/ppermute | solution.py:21
  184.3 28.1 %collective-permute-start.44 = (bf16[528,128]{1,0:T(8,128)(2,1)}, bf16[528,128]{1,0:T(8,128)(2,1)S(1)}, u32[]{:S(2)}, u32[]{:S(2)}) collective-permute-start(bf16[528,128]{1,0:T(8,128)(2,1)} %get-tuple-element.32), channel_id=1, source_target_pairs={{0,3},{1,0},{2,1},{3,2},{4,7},{5,4},{6,5},{7,6},{8,11},{9,8},{10,9... | collective-permute-start | bytes 405512 | tf_op jit(solution)/shard_map/ppermute | solution.py:17
  187.6 25.4 %collective-permute-start.45 = (bf16[528,128]{1,0:T(8,128)(2,1)}, bf16[528,128]{1,0:T(8,128)(2,1)}, u32[]{:S(2)}, u32[]{:S(2)}) collective-permute-start(bf16[528,128]{1,0:T(8,128)(2,1)} %get-tuple-element.33), channel_id=1, source_target_pairs={{0,2},{1,3},{2,0},{3,1},{4,6},{5,7},{6,4},{7,5},{8,10},{9,11},{10,... | collective-permute-start | bytes 405512 | tf_op jit(solution)/shard_map/ppermute | solution.py:17
  187.6 25.4 %collective-permute-start.46 = (bf16[528,128]{1,0:T(8,128)(2,1)}, bf16[528,128]{1,0:T(8,128)(2,1)}, u32[]{:S(2)}, u32[]{:S(2)}) collective-permute-start(bf16[528,128]{1,0:T(8,128)(2,1)} %get-tuple-element.34), channel_id=1, source_target_pairs={{0,1},{1,2},{2,3},{3,0},{4,5},{5,6},{6,7},{7,4},{8,9},{9,10},{10,1... | collective-permute-start | bytes 405512 | tf_op jit(solution)/shard_map/ppermute | solution.py:17
  208.5 9.7 %collective-permute-start.43 = (f32[1,512]{1,0:T(1,128)S(1)}, f32[1,512]{1,0:T(1,128)S(1)}, u32[]{:S(2)}, u32[]{:S(2)}) collective-permute-start(f32[1,512]{1,0:T(1,128)S(1)} %get-tuple-element.29), channel_id=1, source_target_pairs={{0,1},{1,2},{2,3},{3,0},{4,5},{5,6},{6,7},{7,4},{8,9},{9,10},{10,1... | collective-permute-start | bytes 6152 | tf_op jit(solution)/shard_map/ppermute | solution.py:17
  211.4 6.8 %collective-permute-start.42 = (f32[1,512]{1,0:T(1,128)S(1)}, f32[1,512]{1,0:T(1,128)S(1)}, u32[]{:S(2)}, u32[]{:S(2)}) collective-permute-start(f32[1,512]{1,0:T(1,128)S(1)} %get-tuple-element.29), channel_id=1, source_target_pairs={{0,3},{1,0},{2,1},{3,2},{4,7},{5,4},{6,5},{7,6},{8,11},{9,8},{10,9... | collective-permute-start | bytes 6152 | tf_op jit(solution)/shard_map/ppermute | solution.py:17
  212.4 5.8 %collective-permute-start.41 = (f32[1,512]{1,0:T(1,128)S(1)}, f32[1,512]{1,0:T(1,128)S(1)}, u32[]{:S(2)}, u32[]{:S(2)}) collective-permute-start(f32[1,512]{1,0:T(1,128)S(1)} %get-tuple-element.29), channel_id=1, source_target_pairs={{0,2},{1,3},{2,0},{3,1},{4,6},{5,7},{6,4},{7,5},{8,10},{9,11},{10,... | collective-permute-start | bytes 6152 | tf_op jit(solution)/shard_map/ppermute | solution.py:17
  (47 other events, 177.1 us)
